TPU v7x, 512 devices: a whole 4x8x8 slice. The times are simulated.
512 devices in a mesh: dp: 16 (over y, core), ctx: 32 (over x, z).
Axes of the slice: x: 4, y: 8, z: 8, core: 2. Of those that a mesh axis runs over, the one named last changes fastest.
Arguments:
- mixer_input: bfloat16 [65536, 2560], P(('dp', 'ctx')), parts along dimension 0, may hold values from -6 to 6
- input_map: bfloat16 [65536, 128], P(('dp', 'ctx')), parts along dimension 0, may hold values from -6 to 6
- output_map: bfloat16 [65536, 128], P(('dp', 'ctx')), parts along dimension 0, may hold values from -0.015625 to 0.015625
- log_decay: float32 [65536, 40], P(('dp', 'ctx')), parts along dimension 0, may hold values from -1 to 0
- query_rows: bfloat16 [65536, 2560], P(('dp', 'ctx')), parts along dimension 0, may hold values from -7 to 7
- key_rows: bfloat16 [65536, 320], P(('dp', 'ctx')), parts along dimension 0, may hold values from -7 to 7
- value_rows: bfloat16 [65536, 320], P(('dp', 'ctx')), parts along dimension 0, may hold values from -6 to 6
Outputs:
- mixer_output: bfloat16 [65536, 2560], P(('dp', 'ctx')), parts along dimension 0
- attention_output: bfloat16 [65536, 2560], P(('dp', 'ctx')), parts along dimension 0
There are 16 independent parts, one for each index of `dp`. A program takes and returns all parts, laid end to end along the dimension named above; each array names one. Nothing has to cross between parts.
All inputs are finite; a program needn't handle non-finite values.
Results may differ from a plain program's by a relative error of at most 0.0049.
Values may be sent and summed in bfloat16 or wider, within the bound.
No kernel may reach another device: no remote copies, remote signals or barrier semaphores. Data moves between devices by JAX's collectives and lax.ppermute only.
A program may use at most 128 MiB of HBM per device.

v0:
```python
import math

import jax
import jax.numpy as jnp
from jax import lax
from jax.sharding import PartitionSpec as P

MIXER_HEADS = 40
P_SIZE = 64
N = 128
QH = 32
KVH = 4
DH = 80
STRETCH = 128


masked_score = -1e30


def entering_2(part, axis, combine, identity):
    place = lax.axis_index(axis)
    gathered = jax.tree.map(lambda a: lax.all_gather(a, axis), part)
    state = jax.tree.map(lambda a, e: jnp.zeros_like(a) + jnp.asarray(e, a.dtype), part, identity)

    def one(step, state):
        return combine(
            state, jax.tree.map(lambda a: lax.dynamic_index_in_dim(a, step, 0, False), gathered)
        )

    return lax.fori_loop(0, place, one, state)


def mixer_part(mixer_input, input_map, output_map, log_decay):
    row_count = mixer_input.shape[0]
    count = row_count // STRETCH
    x_blocks = mixer_input.reshape(count, STRETCH, MIXER_HEADS, P_SIZE)
    in_blocks = input_map.reshape(count, STRETCH, N)
    out_blocks = output_map.reshape(count, STRETCH, N)
    cumulative = jnp.cumsum(log_decay.reshape(count, STRETCH, MIXER_HEADS), axis=1).transpose(
        0, 2, 1
    )
    lower_mask = jnp.tril(jnp.ones((STRETCH, STRETCH), dtype=bool))
    match = jnp.einsum("ktn,ksn->kts", out_blocks, in_blocks, preferred_element_type=jnp.float32)
    decay_gap = jnp.where(lower_mask, cumulative[..., :, None] - cumulative[..., None, :], 0.0)
    weights = jnp.where(lower_mask, match[:, None] * jnp.exp(decay_gap), 0.0).astype(jnp.bfloat16)
    inner = jnp.einsum("khts,kshp->kthp", weights, x_blocks, preferred_element_type=jnp.float32)
    tail_decay = jnp.exp(cumulative[..., -1:] - cumulative)
    weighted = (tail_decay[..., None] * in_blocks[:, None].astype(jnp.float32)).astype(jnp.bfloat16)
    updates = jnp.einsum("khsn,kshp->khnp", weighted, x_blocks, preferred_element_type=jnp.float32)
    factors = jnp.exp(cumulative[..., -1])
    zero_state = jnp.zeros((MIXER_HEADS, N, P_SIZE), jnp.float32)

    def fold_block(state, items):
        factor, update = items
        return (factor[:, None, None] * state + update, None)

    local_end, unused = lax.scan(fold_block, zero_state, (factors, updates))
    span_decay = jnp.prod(factors, axis=0)

    def combine(earlier, later):
        return (earlier[0] * later[0], later[0][:, None, None] * earlier[1] + later[1])

    prefix = entering_2(
        (span_decay, local_end),
        "ctx",
        combine,
        (jnp.ones_like(span_decay), jnp.zeros_like(local_end)),
    )
    incoming = prefix[1]

    def enter_block(state, items):
        factor, update = items
        return (factor[:, None, None] * state + update, state)

    unused_end, entering = lax.scan(enter_block, incoming, (factors, updates))
    carried = jnp.einsum(
        "ktn,khnp->kthp", out_blocks.astype(jnp.float32), entering, precision=lax.Precision.HIGHEST
    )
    carried = carried * jnp.exp(cumulative).transpose(0, 2, 1)[..., None]
    return (inner + carried).astype(jnp.bfloat16).reshape(row_count, MIXER_HEADS * P_SIZE)


def attend(query_local, key_local, value_local):
    length = query_local.shape[0]
    heads_here = query_local.shape[1] // DH
    block = min(512, length)
    block_count = length // block
    query_heads = query_local.reshape(length, heads_here, DH)
    key_heads = key_local.reshape(length, heads_here, DH)
    value_heads = value_local.reshape(length, heads_here, DH)
    scale = 1.0 / math.sqrt(DH)
    offsets = jnp.arange(block, dtype=jnp.int32)

    def one_block(query_index, result):
        query_block = lax.dynamic_slice_in_dim(query_heads, query_index * block, block, 0)

        def visit(key_index, running):
            running_max, running_sum, total = running
            key_block = lax.dynamic_slice_in_dim(key_heads, key_index * block, block, 0)
            scores = (
                jnp.einsum(
                    "thd,shd->hts", query_block, key_block, preferred_element_type=jnp.float32
                )
                * scale
            )
            visible = (key_index * block + offsets)[None, :] <= (query_index * block + offsets)[
                :, None
            ]
            scores = jnp.where(visible[None], scores, masked_score)
            new_max = jnp.maximum(running_max, jnp.max(scores, axis=-1))
            rescale = jnp.exp(running_max - new_max)
            expo = jnp.exp(scores - new_max[..., None])
            running_sum = running_sum * rescale + jnp.sum(expo, axis=-1)
            value_block = lax.dynamic_slice_in_dim(value_heads, key_index * block, block, 0)
            total = total * rescale.T[..., None] + jnp.einsum(
                "hts,shd->thd",
                expo.astype(jnp.bfloat16),
                value_block,
                preferred_element_type=jnp.float32,
            )
            return (new_max, running_sum, total)

        start = (
            jnp.full((heads_here, block), masked_score, jnp.float32),
            jnp.zeros((heads_here, block), jnp.float32),
            jnp.zeros((block, heads_here, DH), jnp.float32),
        )
        row_max, row_sum, total = lax.fori_loop(0, query_index + 1, visit, start)
        finished = (
            (total / row_sum.T[..., None]).astype(jnp.bfloat16).reshape(block, heads_here * DH)
        )
        return lax.dynamic_update_slice_in_dim(result, finished, query_index * block, 0)

    return lax.fori_loop(
        0, block_count, one_block, jnp.zeros((length, heads_here * DH), jnp.bfloat16)
    )


def attention_part(query_rows, key_rows, value_rows):
    group = QH // KVH
    heads_here = QH // lax.axis_size("ctx")
    query_local = lax.all_to_all(query_rows, "ctx", split_axis=1, concat_axis=0, tiled=True)
    key_whole, value_whole = (
        lax.all_gather(key_rows, "ctx", axis=0, tiled=True),
        lax.all_gather(value_rows, "ctx", axis=0, tiled=True),
    )
    kv_head = lax.axis_index("ctx") * heads_here // group
    key_local = jnp.tile(lax.dynamic_slice_in_dim(key_whole, kv_head * DH, DH, 1), (1, heads_here))
    value_local = jnp.tile(
        lax.dynamic_slice_in_dim(value_whole, kv_head * DH, DH, 1), (1, heads_here)
    )
    attended = attend(query_local, key_local, value_local)
    return lax.all_to_all(attended, "ctx", split_axis=0, concat_axis=1, tiled=True)


def per_device(mixer_input, input_map, output_map, log_decay, query_rows, key_rows, value_rows):
    mixer_output = mixer_part(mixer_input, input_map, output_map, log_decay)
    attention_output = attention_part(query_rows, key_rows, value_rows)
    return (mixer_output, attention_output)


def solution(mesh):
    return jax.shard_map(
        per_device,
        mesh=mesh,
        in_specs=(
            P(("dp", "ctx"), None),
            P(("dp", "ctx"), None),
            P(("dp", "ctx"), None),
            P(("dp", "ctx"), None),
            P(("dp", "ctx"), None),
            P(("dp", "ctx"), None),
            P(("dp", "ctx"), None),
        ),
        out_specs=(P(("dp", "ctx"), None), P(("dp", "ctx"), None)),
        check_vma=False,
    )
```

profile of v0, /device:TPU:454, one launch (start us, length us, event | category | flops | bytes accessed | tf_op | source)
XLA Modules:
  0.0 734.0 jit_solution(539815930219791122)
XLA Ops:
  15.3 7.1 all-to-all-start
  22.5 19.2 %all-to-all-done = bf16[128,32,80]{0,2,1:T(8,128)(2,1)S(1)} async-done(((bf16[128,32,80]{0,2,1:T(8,128)(2,1)}), bf16[128,32,80]{0,2,1:T(8,128)(2,1)S(1)}, u32[]{:S(2)}, u32[]{:S(2)}) %all-to-all-start) | async-done | bytes 655392 | tf_op jit(solution)/shard_map/all_to_all | solution.py:142
  42.2 53.1 %all-gather.6.cloned.1.call-done = bf16[4096,320]{0,1:T(8,128)(2,1)} async-done(((bf16[128,320]{0,1:T(8,128)(2,1)}), bf16[4096,320]{0,1:T(8,128)(2,1)}) %all-gather.6.cloned.1.call-update) | async-done | bytes 2621456 | tf_op jit(solution)/shard_map/all_gather | solution.py:144
  97.2 83.6 %all-gather.8.cloned.1.call-done = bf16[4096,320]{0,1:T(8,128)(2,1)} async-done(((bf16[128,320]{0,1:T(8,128)(2,1)}), bf16[4096,320]{0,1:T(8,128)(2,1)}) %all-gather.8.cloned.1.call-update) | async-done | bytes 2621456 | tf_op jit(solution)/shard_map/all_gather | solution.py:145
  181.9 67.5 %while.73 = (s32[]{:T(128)}, bf16[4096,80]{0,1:T(8,128)(2,1)S(1)}, bf16[4096,1,80]{0,2,1:T(8,128)(2,1)S(1)}, bf16[4096,1,80]{0,2,1:T(8,128)(2,1)}, bf16[4096,1,8...) while((s32[]{:T(128)}, bf16[4096,80]{0,1:T(8,128)(2,1)S(1)}, ...), condition=%wide.region_8.9_spmd.clone.clone, body=%wide.region_3.8_spmd.clone.clone.sunk | while | flops 86149128 | bytes 4344346 | solution.py:134
  184.0 3.7 while.74
  187.8 5.5 while.74
  193.5 7.4 %while.74 = (s32[]{:T(128)}, f32[1,512]{1,0:T(1,128)S(1)}, f32[1,512]{1,0:T(1,128)S(1)}, f32[512,1,80]{0,2,1:T(8,128)S(1)}, s32[]{:T(128)}, /*index=5*/s32[512]{...) while((s32[]{:T(128)}, f32[1,512]{1,0:T(1,128)S(1)}, ...), condition=%wide.region_7.7_spmd.clone, body=%wide.region_4.6_spmd.clone.sunk | while | flops 86067200 | bytes 3762379 | solution.py:128
  201.0 9.2 %while.74 = (s32[]{:T(128)}, f32[1,512]{1,0:T(1,128)S(1)}, f32[1,512]{1,0:T(1,128)S(1)}, f32[512,1,80]{0,2,1:T(8,128)S(1)}, s32[]{:T(128)}, /*index=5*/s32[512]{...) while((s32[]{:T(128)}, f32[1,512]{1,0:T(1,128)S(1)}, ...), condition=%wide.region_7.7_spmd.clone, body=%wide.region_4.6_spmd.clone.sunk | while | flops 86067200 | bytes 3762379 | solution.py:128
  210.4 11.1 %while.74 = (s32[]{:T(128)}, f32[1,512]{1,0:T(1,128)S(1)}, f32[1,512]{1,0:T(1,128)S(1)}, f32[512,1,80]{0,2,1:T(8,128)S(1)}, s32[]{:T(128)}, /*index=5*/s32[512]{...) while((s32[]{:T(128)}, f32[1,512]{1,0:T(1,128)S(1)}, ...), condition=%wide.region_7.7_spmd.clone, body=%wide.region_4.6_spmd.clone.sunk | while | flops 86067200 | bytes 3762379 | solution.py:128
  221.6 12.9 %while.74 = (s32[]{:T(128)}, f32[1,512]{1,0:T(1,128)S(1)}, f32[1,512]{1,0:T(1,128)S(1)}, f32[512,1,80]{0,2,1:T(8,128)S(1)}, s32[]{:T(128)}, /*index=5*/s32[512]{...) while((s32[]{:T(128)}, f32[1,512]{1,0:T(1,128)S(1)}, ...), condition=%wide.region_7.7_spmd.clone, body=%wide.region_4.6_spmd.clone.sunk | while | flops 86067200 | bytes 3762379 | solution.py:128
  234.6 14.7 %while.74 = (s32[]{:T(128)}, f32[1,512]{1,0:T(1,128)S(1)}, f32[1,512]{1,0:T(1,128)S(1)}, f32[512,1,80]{0,2,1:T(8,128)S(1)}, s32[]{:T(128)}, /*index=5*/s32[512]{...) while((s32[]{:T(128)}, f32[1,512]{1,0:T(1,128)S(1)}, ...), condition=%wide.region_7.7_spmd.clone, body=%wide.region_4.6_spmd.clone.sunk | while | flops 86067200 | bytes 3762379 | solution.py:128
  250.4 8.3 %all-to-all-start.1 = ((bf16[32,128,80]{1,2,0:T(8,128)(2,1)}), bf16[32,128,80]{1,2,0:T(8,128)(2,1)S(1)}, u32[]{:S(2)}, u32[]{:S(2)}) async-start(bf16[32,128,80]{1,2,0:T(8,128)(2,1)} %copy_bitcast_fusion), calls=%async_computation.1 | async-start | bytes 1310720 | tf_op jit(solution)/shard_map/all_to_all | solution.py:153
  258.9 40.9 %all-gather = f32[32,40,1]{1,2,0:T(1,128)S(1)} all-gather(f32[1,40,1]{1,2,0:T(1,128)S(1)} %get-tuple-element.442), channel_id=2, replica_groups=mesh['dp'=16,'ctx'=32] {'ctx'}, dimensions={0}, use_global_device_ids=true | all-gather | bytes 5280 | tf_op jit(solution)/shard_map/all_gather | solution.py:22
  301.1 168.8 %all-gather.10.cloned.1.call-done = f32[1280,128,64]{1,2,0:T(8,128)} async-done(((f32[40,128,64]{1,2,0:T(8,128)}), f32[1280,128,64]{1,2,0:T(8,128)}) %all-gather.10.cloned.1.call-update) | async-done | bytes 41943056 | tf_op jit(solution)/shard_map/all_gather | solution.py:22
  471.7 249.4 %while.71 = (s32[]{:T(128)}, f32[40,128,64]{2,1,0:T(8,128)}, s32[]{:T(128)}, f32[32,40]{1,0:T(8,128)S(1)}, f32[32,40,128,64]{2,3,1,0:T(8,128)}, /*index=5*/s32[]{:T(128)}, s32[]{:T(128)}, s32[]{:T(128)}) while((s32[]{:T(128)}, f32[40,128,64]{2,1,0:T(8,128)}, s32[]{:T(128)}, f32[32,40]{1,0:T(8,128)S(1)}, f32[32,40,128,64]{2,3,1,0:T(8,128)}, ...), condition=%wide.region_2.3_spmd, body=%wide.region_1.2_spmd.sunk | while | flops 655365 | bytes 9175655 | solution.py:30
  471.7 2.5 constant_dynamic-slice_fusion.4
  476.2 3.6 bitcast_add_fusion.2
  479.8 2.5 constant_dynamic-slice_fusion.4
  484.2 3.6 bitcast_add_fusion.2
  492.3 3.6 bitcast_add_fusion.2
  495.8 2.5 constant_dynamic-slice_fusion.4
  500.3 3.6 bitcast_add_fusion.2
  503.9 2.5 constant_dynamic-slice_fusion.4
  508.4 3.6 bitcast_add_fusion.2
  511.9 2.5 constant_dynamic-slice_fusion.4
  516.4 3.6 bitcast_add_fusion.2
  520.0 2.5 constant_dynamic-slice_fusion.4
  524.5 3.6 bitcast_add_fusion.2
  528.0 2.5 constant_dynamic-slice_fusion.4
  532.5 3.6 bitcast_add_fusion.2
  536.1 2.5 constant_dynamic-slice_fusion.4
  540.5 3.6 bitcast_add_fusion.2
  544.1 2.5 constant_dynamic-slice_fusion.4
  548.6 3.6 bitcast_add_fusion.2
  552.2 2.5 constant_dynamic-slice_fusion.4
  556.6 3.6 bitcast_add_fusion.2
  560.2 2.5 constant_dynamic-slice_fusion.4
  564.7 3.6 bitcast_add_fusion.2
  568.3 2.5 constant_dynamic-slice_fusion.4
  572.7 3.6 bitcast_add_fusion.2
  576.3 2.5 constant_dynamic-slice_fusion.4
  580.8 3.6 bitcast_add_fusion.2
  584.3 2.5 constant_dynamic-slice_fusion.4
  588.8 3.6 bitcast_add_fusion.2
  592.4 2.5 constant_dynamic-slice_fusion.4
  596.9 3.6 bitcast_add_fusion.2
  600.4 2.5 constant_dynamic-slice_fusion.4
  604.9 3.6 bitcast_add_fusion.2
  613.0 3.6 bitcast_add_fusion.2
  621.0 3.6 bitcast_add_fusion.2
  629.1 3.6 bitcast_add_fusion.2
  637.1 3.6 bitcast_add_fusion.2
  645.1 3.6 bitcast_add_fusion.2
  653.2 3.6 bitcast_add_fusion.2
  661.2 3.6 bitcast_add_fusion.2
  669.3 3.6 bitcast_add_fusion.2
  677.3 3.6 bitcast_add_fusion.2
  685.4 3.6 bitcast_add_fusion.2
  693.4 3.6 bitcast_add_fusion.2
  701.5 3.6 bitcast_add_fusion.2
  709.5 3.6 bitcast_add_fusion.2
  717.6 3.6 bitcast_add_fusion.2
  721.1 4.0 fusion.17
  (416 shorter events, 182.9 us)
Async XLA Ops:
  7.2 292.7 %copy-start = (bf16[128,128]{1,0:T(8,128)(2,1)S(1)}, bf16[128,128]{1,0:T(8,128)(2,1)}, u32[]{:S(2)}) copy-start(bf16[128,128]{1,0:T(8,128)(2,1)} %param.15) | copy-start | bytes 98308
  7.2 88.0 %all-gather.6.cloned.1.call-start = ((), (), s32[]{:S(2)}) async-start(), calls=%async_computation.2 | async-start | bytes 2703360 | tf_op jit(solution)/shard_map/all_gather | solution.py:144
  7.9 172.8 %all-gather.8.cloned.1.call-start = ((), (), s32[]{:S(2)}) async-start(), calls=%async_computation.3 | async-start | bytes 2703360 | tf_op jit(solution)/shard_map/all_gather | solution.py:145
  8.7 5.5 copy-start.1
  8.7 461.2 %all-gather.10.cloned.1.call-start = ((), (), s32[]{:S(2)}) async-start(), calls=%async_computation.4 | async-start | bytes 43253760 | tf_op jit(solution)/shard_map/all_gather | solution.py:22
  15.3 26.4 %all-to-all-start = ((bf16[128,32,80]{0,2,1:T(8,128)(2,1)}), bf16[128,32,80]{0,2,1:T(8,128)(2,1)S(1)}, u32[]{:S(2)}, u32[]{:S(2)}) async-start(bf16[128,32,80]{0,2,1:T(8,128)(2,1)} %bitcast.19), calls=%async_computation | async-start | bytes 1310720 | tf_op jit(solution)/shard_map/all_to_all | solution.py:142
  249.4 50.4 %copy-start.2 = (bf16[128,128]{1,0:T(8,128)(2,1)S(1)}, bf16[128,128]{1,0:T(8,128)(2,1)}, u32[]{:S(2)}) copy-start(bf16[128,128]{1,0:T(8,128)(2,1)} %param.14) | copy-start | bytes 98308
  250.4 49.6 %all-to-all-start.1 = ((bf16[32,128,80]{1,2,0:T(8,128)(2,1)}), bf16[32,128,80]{1,2,0:T(8,128)(2,1)S(1)}, u32[]{:S(2)}, u32[]{:S(2)}) async-start(bf16[32,128,80]{1,2,0:T(8,128)(2,1)} %copy_bitcast_fusion), calls=%async_computation.1 | async-start | bytes 1310720 | tf_op jit(solution)/shard_map/all_to_all | solution.py:153
Sparse Core Ops, SparseCore 0:
  11.1 84.1 all-gather.5
  98.3 82.4 all-gather.7
  183.9 285.9 all-gather.9
where the time goes:
time: 739 us; the launch traced here: 734 us
  waiting for transfers between devices  326 us (44%)
  local copies, waits for them, and re-layouts  151 us (20%)
  other arithmetic  120 us (16%)
  matrix products  63.8 us (9%)
  blocking collectives  40.9 us (6%)
  starting transfers between devices  15.6 us (2%)
  between operations  13.9 us (2%)
    all_gather x1, waiting for transfers between devices, entering_2(): gathered = jax.tree.map(lambda a: lax.all_gather(a, axis), part)  169 us
    dynamic_slice x62, local copies, waits for them, and re-layouts, one(): lax.dynamic_index_in_dim(a, step, 0, False)  138 us
    add x31, other arithmetic, combine(): later[0][:, None, None] * earlier[1] + later[1]  111 us
    all_gather x1, waiting for transfers between devices, attention_part(): lax.all_gather(value_rows, 'ctx', axis=0, tiled=True)  83.6 us
    all_gather x1, waiting for transfers between devices, attention_part(): lax.all_gather(key_rows, 'ctx', axis=0, tiled=True)  53.1 us
    dot_general x36, matrix products, visit(): jnp.einsum('thd,shd->hts', query_block, key_block, preferred_element_type...  44.4 us
    all_gather x1, blocking collectives, entering_2(): gathered = jax.tree.map(lambda a: lax.all_gather(a, axis), part)  40.9 us
    all_to_all x1, waiting for transfers between devices, attention_part(): lax.all_to_all(query_rows, 'ctx', split_axis=1, concat_axis=0, tiled=True)  19.2 us
  transfers between devices with their start and end apart: 5, of which 4 were waited for; matrix products, arithmetic and copies ran while one was open for 11% of the time, Pallas kernels for 0%

commit v1 on v0

v1 whole, which is shorter than its diff:
```python
import math

import jax
import jax.numpy as jnp
from jax import lax
from jax.experimental import pallas as pl
from jax.experimental.pallas import tpu as pltpu
from jax.sharding import Mesh
from jax.sharding import PartitionSpec as P

MIXER_HEADS = 40
P_SIZE = 64
N = 128
QH = 32
KVH = 4
DH = 80
T = 128
WIDTH = MIXER_HEADS * P_SIZE
GROUP = QH // KVH
GDH = GROUP * DH
NX = 4
NZ = 8
NCTX = NX * NZ
PIECE_ROWS = 16
PIECE_COLS = 640
masked_score = -1e30
F32 = jnp.float32
BF16 = jnp.bfloat16


def split2(a):
    hi = a.astype(BF16)
    return hi, (a - hi.astype(F32)).astype(BF16)


def dot(a, b):
    return jnp.dot(a, b, preferred_element_type=F32)


def dot_nt(a, b):
    return lax.dot_general(a, b, (((1,), (1,)), ((), ())), preferred_element_type=F32)


def head_spread():
    rows = lax.broadcasted_iota(jnp.int32, (MIXER_HEADS, WIDTH), 0)
    cols = lax.broadcasted_iota(jnp.int32, (MIXER_HEADS, WIDTH), 1)
    return jnp.where(cols // P_SIZE == rows, 1.0, 0.0).astype(BF16)


def spread(a, onehot):
    hi, lo = split2(a)
    return dot(hi, onehot) + dot(lo, onehot)


def cumulative_of(decay):
    rows = lax.broadcasted_iota(jnp.int32, (T, T), 0)
    cols = lax.broadcasted_iota(jnp.int32, (T, T), 1)
    lower = jnp.where(cols <= rows, 1.0, 0.0).astype(F32)
    return jnp.dot(lower, decay, precision=lax.Precision.HIGHEST, preferred_element_type=F32)


def update_kernel(x_ref, in_ref, decay_ref, out_ref):
    cumulative = cumulative_of(decay_ref[...])
    last = cumulative[T - 1 : T, :]
    onehot = head_spread()
    tail = spread(jnp.exp(last - cumulative), onehot)
    hi, lo = split2(x_ref[...].astype(F32) * tail)
    in_t = in_ref[...].astype(F32).T.astype(BF16)
    update = (dot(in_t, hi) + dot(in_t, lo)).astype(BF16)
    total = jnp.broadcast_to(jnp.exp(last), (PIECE_ROWS, MIXER_HEADS))
    total_hi, total_lo = split2(total)
    head = lax.broadcasted_iota(jnp.int32, (MIXER_HEADS, 128), 0)
    lane = lax.broadcasted_iota(jnp.int32, (MIXER_HEADS, 128), 1)
    place_hi = jnp.where(lane == head, 1.0, 0.0).astype(BF16)
    place_lo = jnp.where(lane == head + 64, 1.0, 0.0).astype(BF16)
    factor = (dot(total_hi, place_hi) + dot(total_lo, place_lo)).astype(BF16)
    for i in range(N // PIECE_ROWS):
        for j in range(WIDTH // PIECE_COLS):
            d = i * (WIDTH // PIECE_COLS) + j
            out_ref[d, :, :PIECE_COLS] = update[
                i * PIECE_ROWS : (i + 1) * PIECE_ROWS, j * PIECE_COLS : (j + 1) * PIECE_COLS
            ]
            out_ref[d, :, PIECE_COLS:] = factor


def prefix_kernel(place_ref, in_ref, out_ref):
    first_head = (place_ref[0] % (WIDTH // PIECE_COLS)) * (PIECE_COLS // P_SIZE)
    lane = lax.broadcasted_iota(jnp.int32, (128, PIECE_COLS), 0)
    cols = lax.broadcasted_iota(jnp.int32, (128, PIECE_COLS), 1)
    head = first_head + cols // P_SIZE
    onehot = jnp.where((lane == head) | (lane == head + 64), 1.0, 0.0).astype(BF16)
    state = jnp.zeros((PIECE_ROWS, PIECE_COLS), F32)
    for k in range(NCTX):
        out_ref[k] = state.astype(BF16)
        factor = dot(in_ref[k, :, PIECE_COLS:], onehot)
        state = factor * state + in_ref[k, :, :PIECE_COLS].astype(F32)


def mix_kernel(x_ref, in_ref, map_ref, decay_ref, enter_ref, out_ref):
    cumulative = cumulative_of(decay_ref[...])
    middle = 0.5 * cumulative[T - 1 : T, :]
    onehot = head_spread()
    ahead = spread(jnp.exp(cumulative - middle), onehot)
    behind = spread(jnp.exp(middle - cumulative), onehot)
    start = spread(jnp.exp(jnp.broadcast_to(middle, (8, MIXER_HEADS))), onehot)[0:1, :]
    hi, lo = split2(x_ref[...].astype(F32) * behind)
    out_map = map_ref[...]
    match = dot_nt(out_map, in_ref[...])
    rows = lax.broadcasted_iota(jnp.int32, (T, T), 0)
    cols = lax.broadcasted_iota(jnp.int32, (T, T), 1)
    match_hi, match_lo = split2(jnp.where(cols <= rows, match, 0.0))
    inner = dot(match_hi, hi) + dot(match_hi, lo) + dot(match_lo, hi)
    for j in range(WIDTH // PIECE_COLS):
        cut = slice(j * PIECE_COLS, (j + 1) * PIECE_COLS)
        entering = jnp.concatenate(
            [enter_ref[i * (WIDTH // PIECE_COLS) + j] for i in range(N // PIECE_ROWS)], axis=0
        )
        carried = dot(out_map, entering)
        out_ref[:, cut] = (ahead[:, cut] * (inner[:, cut] + start[:, cut] * carried)).astype(BF16)


QT = 256
CHUNK = NZ * T


def attend_kernel(place_ref, q_ref, kv_ref, out_ref, k_buf, v_buf, q_buf, o_buf):
    z = place_ref[0]
    pad = jnp.zeros((128 - DH, CHUNK), BF16)
    ones = jnp.where(lax.broadcasted_iota(jnp.int32, (16, CHUNK), 0) == 0, 1.0, 0.0).astype(BF16)
    for c in range(NX):
        cut = slice(c * CHUNK, (c + 1) * CHUNK)
        k_buf[DH:128, cut] = pad
        k_buf[128 + DH : 256, cut] = pad
        v_buf[DH : DH + 16, cut] = ones
        for b in range(NZ):
            at = slice(c * CHUNK + b * T, c * CHUNK + (b + 1) * T)
            k = kv_ref[b, c, :DH, :]
            k_buf[:DH, at] = k
            k_buf[128 : 128 + DH, at] = k
            v_buf[:DH, at] = kv_ref[b, c, DH:, :]
    scale = math.log2(math.e) / math.sqrt(DH)
    zero = jnp.zeros((T, 128 - DH), F32)
    for c in range(NX):
        for h in range(GROUP):
            q = q_ref[c, :, h * DH : (h + 1) * DH].astype(F32) * scale
            hi, lo = split2(jnp.concatenate([q, zero], axis=1))
            q_buf[c, h * T : (h + 1) * T, :128] = hi
            q_buf[c, h * T : (h + 1) * T, 128:] = lo
    row = lax.broadcasted_iota(jnp.int32, (QT, CHUNK), 0) % T
    col = lax.broadcasted_iota(jnp.int32, (QT, CHUNK), 1)
    visible = col <= row + z * T
    for c in range(NX):
        seen = c * CHUNK

        def one_tile(i, carry, c=c, seen=seen):
            at = pl.ds(pl.multiple_of(i * QT, QT), QT)
            q = q_buf[c, at, :]
            near = dot(q, k_buf[:, seen : seen + CHUNK])
            near = jnp.where(visible, near, masked_score)
            top = jnp.max(near, axis=1, keepdims=True)
            if c:
                far = dot(q, k_buf[:, :seen])
                top = jnp.maximum(top, jnp.max(far, axis=1, keepdims=True))
            total = dot_nt(jnp.exp2(near - top).astype(BF16), v_buf[:, seen : seen + CHUNK])
            if c:
                total += dot_nt(jnp.exp2(far - top).astype(BF16), v_buf[:, :seen])
            o_buf[at, :] = total[:, :DH] / total[:, DH : DH + 1]
            return carry

        lax.fori_loop(0, GROUP * T // QT, one_tile, 0)
        out_ref[c] = jnp.concatenate(
            [o_buf[h * T : (h + 1) * T, :] for h in range(GROUP)], axis=1
        ).astype(BF16)


VMEM_SPEC = pl.BlockSpec(memory_space=pltpu.VMEM)
SMEM_SPEC = pl.BlockSpec(memory_space=pltpu.SMEM)


def call(kernel, shape, specs, scratch=(), limit=48):
    return pl.pallas_call(
        kernel,
        out_shape=jax.ShapeDtypeStruct(shape, BF16),
        in_specs=specs,
        out_specs=VMEM_SPEC,
        scratch_shapes=list(scratch),
        compiler_params=pltpu.CompilerParams(vmem_limit_bytes=limit << 20),
    )


def per_device(mixer_input, input_map, output_map, log_decay, query_rows, key_rows, value_rows):
    place_z = lax.axis_index("cz").astype(jnp.int32).reshape(1)
    place = (lax.axis_index("cx") * NZ + lax.axis_index("cz")).astype(jnp.int32).reshape(1)
    kv = jnp.concatenate(
        [key_rows.T.reshape(KVH, DH, T), value_rows.T.reshape(KVH, DH, T)], axis=1
    )
    kv = lax.all_to_all(kv, "cx", 0, 0)
    kv = lax.all_gather(kv, "cz")
    q = query_rows.reshape(T, KVH, GDH).transpose(1, 0, 2)
    q = lax.all_to_all(q, "cx", 0, 0)
    update = call(
        update_kernel, (NCTX, PIECE_ROWS, PIECE_COLS + 128), [VMEM_SPEC] * 3
    )(mixer_input, input_map, log_decay)
    update = lax.all_to_all(update, ("cx", "cz"), 0, 0)
    entering = call(prefix_kernel, (NCTX, PIECE_ROWS, PIECE_COLS), [SMEM_SPEC, VMEM_SPEC])(
        place, update
    )
    entering = lax.all_to_all(entering, ("cx", "cz"), 0, 0)
    attended = call(
        attend_kernel,
        (NX, T, GDH),
        [SMEM_SPEC, VMEM_SPEC, VMEM_SPEC],
        [
            pltpu.VMEM((256, NX * CHUNK), BF16),
            pltpu.VMEM((DH + 16, NX * CHUNK), BF16),
            pltpu.VMEM((NX, GROUP * T, 256), BF16),
            pltpu.VMEM((GROUP * T, DH), F32),
        ],
    )(place_z, q, kv)
    attended = lax.all_to_all(attended, "cx", 0, 0)
    attention_output = attended.transpose(1, 0, 2).reshape(T, QH * DH)
    mixer_output = call(mix_kernel, (T, WIDTH), [VMEM_SPEC] * 5)(
        mixer_input, input_map, output_map, log_decay, entering
    )
    return mixer_output, attention_output


def solution(mesh):
    grid = Mesh(mesh.devices.reshape(-1, NX, NZ), ("dp", "cx", "cz"))
    spec = P(("dp", "cx", "cz"), None)
    return jax.shard_map(
        per_device,
        mesh=grid,
        in_specs=(spec,) * 7,
        out_specs=(spec, spec),
        check_vma=False,
    )
```

time: 739 us -> 138 us (0.19)
  the two profiles are of different devices: /device:TPU:454 before, /device:TPU:56 now
where the time goes in v1:
time: 138 us; the launch traced here: 137 us
  waiting for transfers between devices  44.4 us (32%)
  Pallas kernels  39.9 us (29%)
  starting transfers between devices  30 us (22%)
  between operations  14.1 us (10%)
  local copies, waits for them, and re-layouts  6.82 us (5%)
  other arithmetic  1.61 us (1%)
    pallas_call x1, Pallas kernels, per_device(): call(attend_kernel, (NX, T, GDH), [SMEM_SPEC, VMEM_SPEC, VMEM_SPEC], [plt...  33.1 us
    all_to_all x1, waiting for transfers between devices, per_device(): update = lax.all_to_all(update, ('cx', 'cz'), 0, 0)  20.6 us
    all_to_all x1, starting transfers between devices, per_device(): update = lax.all_to_all(update, ('cx', 'cz'), 0, 0)  12.4 us
    all_gather x1, waiting for transfers between devices, per_device(): kv = lax.all_gather(kv, 'cz')  8.96 us
    all_to_all x1, waiting for transfers between devices, per_device(): q = lax.all_to_all(q, 'cx', 0, 0)  6.92 us
    all_to_all x1, waiting for transfers between devices, per_device(): attended = lax.all_to_all(attended, 'cx', 0, 0)  6 us
    unnamed x19, local copies, waits for them, and re-layouts  5.41 us
    all_to_all x1, starting transfers between devices, per_device(): entering = lax.all_to_all(entering, ('cx', 'cz'), 0, 0)  5.03 us
  transfers between devices with their start and end apart: 6, of which 5 were waited for; matrix products, arithmetic and copies ran while one was open for 2% of the time, Pallas kernels for 29%

profile of v1, /device:TPU:56, one launch (start us, length us, event | category | flops | bytes accessed | tf_op | source)
XLA Modules:
  0.0 136.8 jit_solution(14941348422191110992)
XLA Ops:
  7.2 1.6 %pad_maximum_fusion = bf16[4,160,128]{2,1,0:T(8,128)(2,1)} fusion(bf16[4,80,128]{2,1,0:T(8,128)(2,1)} %bitcast.17, bf16[4,80,128]{2,1,0:T(8,128)(2,1)} %bitcast.18), kind=kLoop, calls=%fused_computation | loop fusion | flops 327680 | bytes 327680 | tf_op jit(solution)/shard_map/concatenate | solution.py:194
  8.8 4.3 %all-to-all-start.3 = ((bf16[4,160,128]{2,1,0:T(8,128)(2,1)}), bf16[4,160,128]{2,1,0:T(8,128)(2,1)S(1)}, u32[]{:S(2)}, u32[]{:S(2)}) async-start(bf16[4,160,128]{2,1,0:T(8,128)(2,1)} %pad_maximum_fusion), calls=%async_computation.3 | async-start | bytes 327680 | tf_op jit(solution)/shard_map/all_to_all | solution.py:197
  13.1 0.8 copy.18.decay_ref
  13.9 0.0 copy-start
  13.9 1.1 copy-done
  15.0 0.0 copy-start.3
  15.0 0.8 copy-done.3
  15.7 0.0 copy-start.6
  15.7 2.2 %shard_map.86 = bf16[32,16,768]{2,1,0:T(8,128)(2,1)} custom-call(bf16[128,2560]{1,0:T(8,128)(2,1)S(1)} %copy-done, bf16[128,128]{1,0:T(8,128)(2,1)S(1)} %copy-done.3, f32[128,40]{1,0:T(8,128)S(1)} %copy.18.decay_ref), custom_call_target="tpu_custom_call" | custom-call | tf_op jit(solution)/shard_map/pallas_call | solution.py:201
  18.0 1.3 all-to-all-done.3
  19.2 0.0 copy-start.7
  19.2 12.4 %all-to-all-start = ((bf16[32,16,768]{2,1,0:T(8,128)(2,1)}), bf16[32,16,768]{2,1,0:T(8,128)(2,1)S(1)}, u32[]{:S(2)}, u32[]{:S(2)}) async-start(bf16[32,16,768]{2,1,0:T(8,128)(2,1)} %shard_map.86), calls=%async_computation | async-start | bytes 1572864 | tf_op jit(solution)/shard_map/all_to_all | solution.py:204
  31.6 0.0 all-gather.3.cloned.1.call-start
  31.7 0.0 copy-done.7
  31.7 0.7 all-gather.3.cloned.1.call-update
  32.4 0.0 copy-done.6
  32.4 0.3 copy.19
  32.7 1.1 copy.20
  33.8 20.6 %all-to-all-done.in_ref = bf16[32,16,768]{2,1,0:T(8,128)(2,1)S(1)} async-done(((bf16[32,16,768]{2,1,0:T(8,128)(2,1)}), bf16[32,16,768]{2,1,0:T(8,128)(2,1)S(1)}, u32[]{:S(2)}, u32[]{:S(2)}) %all-to-all-start) | async-done | bytes 786464 | tf_op jit(solution)/shard_map/all_to_all | solution.py:204
  54.4 3.5 %all-to-all-start.2 = ((bf16[4,128,640]{2,1,0:T(8,128)(2,1)}), bf16[4,128,640]{2,1,0:T(8,128)(2,1)S(1)}, u32[]{:S(2)}, u32[]{:S(2)}) async-start(bf16[4,128,640]{2,1,0:T(8,128)(2,1)} %bitcast.3), calls=%async_computation.2 | async-start | bytes 1310720 | tf_op jit(solution)/shard_map/all_to_all | solution.py:200
  57.9 1.8 %shard_map.87 = bf16[32,16,640]{2,1,0:T(8,128)(2,1)} custom-call(s32[1]{0:T(128)} %bitcast.place_ref, bf16[32,16,768]{2,1,0:T(8,128)(2,1)S(1)} %all-to-all-done.in_ref), custom_call_target="tpu_custom_call" | custom-call | tf_op jit(solution)/shard_map/pallas_call | solution.py:205
  59.7 6.9 %all-to-all-done.2.q_ref = bf16[4,128,640]{2,1,0:T(8,128)(2,1)S(1)} async-done(((bf16[4,128,640]{2,1,0:T(8,128)(2,1)}), bf16[4,128,640]{2,1,0:T(8,128)(2,1)S(1)}, u32[]{:S(2)}, u32[]{:S(2)}) %all-to-all-start.2) | async-done | bytes 655392 | tf_op jit(solution)/shard_map/all_to_all | solution.py:200
  66.7 5.0 %all-to-all-start.1 = ((bf16[32,16,640]{2,1,0:T(8,128)(2,1)}), bf16[32,16,640]{2,1,0:T(8,128)(2,1)S(1)}, u32[]{:S(2)}, u32[]{:S(2)}) async-start(bf16[32,16,640]{2,1,0:T(8,128)(2,1)} %shard_map.87), calls=%async_computation.1 | async-start | bytes 1310720 | tf_op jit(solution)/shard_map/all_to_all | solution.py:208
  71.7 9.0 %all-gather.3.cloned.1.call-done = bf16[32,160,128]{2,1,0:T(8,128)(2,1)} async-done(((bf16[4,160,128]{2,1,0:T(8,128)(2,1)}), bf16[32,160,128]{2,1,0:T(8,128)(2,1)}) %all-gather.3.cloned.1.call-update) | async-done | bytes 1310736 | tf_op jit(solution)/shard_map/all_gather | solution.py:198
  80.6 0.0 copy-start.2
  80.7 1.3 copy-done.2
  82.0 33.1 %shard_map.89 = bf16[4,128,640]{2,1,0:T(8,128)(2,1)} custom-call(s32[1]{0:T(128)} %bitcast.1.place_ref, bf16[4,128,640]{2,1,0:T(8,128)(2,1)S(1)} %all-to-all-done.2.q_ref, bf16[8,4,160,128]{3,2,1,0:T(8,128)(2,1)S(1)} %bitcast.13), custom_call_target="tpu_custom_call" | custom-call | tf_op jit(solution)/shard_map/pallas_call | solution.py:209
  115.0 0.0 copy-start.1
  115.0 0.0 copy-start.4
  115.0 0.0 copy-start.5
  115.0 0.0 all-to-all-done.1.enter_ref
  115.1 4.7 %all-to-all-start.4 = ((bf16[4,128,640]{2,1,0:T(8,128)(2,1)}), bf16[4,128,640]{2,1,0:T(8,128)(2,1)S(1)}, u32[]{:S(2)}, u32[]{:S(2)}) async-start(bf16[4,128,640]{2,1,0:T(8,128)(2,1)} %shard_map.89), calls=%async_computation.4 | async-start | bytes 1310720 | tf_op jit(solution)/shard_map/all_to_all | solution.py:220
  119.7 0.0 copy-done.1
  119.8 0.0 copy-done.4
  119.8 0.0 copy-done.5
  119.8 2.8 %shard_map.88 = bf16[128,2560]{1,0:T(8,128)(2,1)} custom-call(bf16[128,2560]{1,0:T(8,128)(2,1)S(1)} %copy-done.1, bf16[128,128]{1,0:T(8,128)(2,1)S(1)} %copy-done.4, bf16[128,128]{1,0:T(8,128)(2,1)S(1)} %copy-done.5, f32[128,40]{1,0:T(8,128)S(1)} %copy.18.decay_ref, bf16[32,16,640]{2,1,0:T(8,128)(2,1)S(1)} %all-to-all-done.1.enter_ref), custom_call_target="tpu_custom_call" | custom-call | tf_op jit(solution)/shard_map/pallas_call | solution.py:222
  122.5 6.0 %all-to-all-done.4 = bf16[4,128,640]{2,1,0:T(8,128)(2,1)S(1)} async-done(((bf16[4,128,640]{2,1,0:T(8,128)(2,1)}), bf16[4,128,640]{2,1,0:T(8,128)(2,1)S(1)}, u32[]{:S(2)}, u32[]{:S(2)}) %all-to-all-start.4) | async-done | bytes 655392 | tf_op jit(solution)/shard_map/all_to_all | solution.py:220
  128.5 0.3 copy.21
  128.9 1.1 copy.22
Async XLA Ops:
  8.8 10.4 %all-to-all-start.3 = ((bf16[4,160,128]{2,1,0:T(8,128)(2,1)}), bf16[4,160,128]{2,1,0:T(8,128)(2,1)S(1)}, u32[]{:S(2)}, u32[]{:S(2)}) async-start(bf16[4,160,128]{2,1,0:T(8,128)(2,1)} %pad_maximum_fusion), calls=%async_computation.3 | async-start | bytes 327680 | tf_op jit(solution)/shard_map/all_to_all | solution.py:197
  13.9 1.1 copy-start
  15.0 0.8 copy-start.3
  15.7 16.6 %copy-start.6 = (bf16[128,2560]{1,0:T(8,128)(2,1)S(1)}, bf16[128,2560]{1,0:T(8,128)(2,1)}, u32[]{:S(2)}) copy-start(bf16[128,2560]{1,0:T(8,128)(2,1)} %param.11) | copy-start | bytes 1966084
  19.2 12.5 %copy-start.7 = (bf16[4,160,128]{2,1,0:T(8,128)(2,1)}, bf16[4,160,128]{2,1,0:T(8,128)(2,1)S(1)}, u32[]{:S(2)}) copy-start(bf16[4,160,128]{2,1,0:T(8,128)(2,1)S(1)} %all-to-all-done.3) | copy-start | bytes 491524
  19.2 35.2 %all-to-all-start = ((bf16[32,16,768]{2,1,0:T(8,128)(2,1)}), bf16[32,16,768]{2,1,0:T(8,128)(2,1)S(1)}, u32[]{:S(2)}, u32[]{:S(2)}) async-start(bf16[32,16,768]{2,1,0:T(8,128)(2,1)} %shard_map.86), calls=%async_computation | async-start | bytes 1572864 | tf_op jit(solution)/shard_map/all_to_all | solution.py:204
  31.6 49.0 %all-gather.3.cloned.1.call-start = ((), (), s32[]{:S(2)}) async-start(), calls=%async_computation.5 | async-start | bytes 1474560 | tf_op jit(solution)/shard_map/all_gather | solution.py:198
  54.4 12.2 %all-to-all-start.2 = ((bf16[4,128,640]{2,1,0:T(8,128)(2,1)}), bf16[4,128,640]{2,1,0:T(8,128)(2,1)S(1)}, u32[]{:S(2)}, u32[]{:S(2)}) async-start(bf16[4,128,640]{2,1,0:T(8,128)(2,1)} %bitcast.3), calls=%async_computation.2 | async-start | bytes 1310720 | tf_op jit(solution)/shard_map/all_to_all | solution.py:200
  66.7 48.4 %all-to-all-start.1 = ((bf16[32,16,640]{2,1,0:T(8,128)(2,1)}), bf16[32,16,640]{2,1,0:T(8,128)(2,1)S(1)}, u32[]{:S(2)}, u32[]{:S(2)}) async-start(bf16[32,16,640]{2,1,0:T(8,128)(2,1)} %shard_map.87), calls=%async_computation.1 | async-start | bytes 1310720 | tf_op jit(solution)/shard_map/all_to_all | solution.py:208
  80.6 1.3 copy-start.2
  115.0 4.7 %copy-start.1 = (bf16[128,2560]{1,0:T(8,128)(2,1)S(1)}, bf16[128,2560]{1,0:T(8,128)(2,1)}, u32[]{:S(2)}) copy-start(bf16[128,2560]{1,0:T(8,128)(2,1)} %x_ref.3) | copy-start | bytes 1966084
  115.0 4.7 %copy-start.4 = (bf16[128,128]{1,0:T(8,128)(2,1)S(1)}, bf16[128,128]{1,0:T(8,128)(2,1)}, u32[]{:S(2)}) copy-start(bf16[128,128]{1,0:T(8,128)(2,1)} %in_ref.3) | copy-start | bytes 98308
  115.0 4.7 %copy-start.5 = (bf16[128,128]{1,0:T(8,128)(2,1)S(1)}, bf16[128,128]{1,0:T(8,128)(2,1)}, u32[]{:S(2)}) copy-start(bf16[128,128]{1,0:T(8,128)(2,1)} %map_ref.1) | copy-start | bytes 98308
  115.1 13.5 %all-to-all-start.4 = ((bf16[4,128,640]{2,1,0:T(8,128)(2,1)}), bf16[4,128,640]{2,1,0:T(8,128)(2,1)S(1)}, u32[]{:S(2)}, u32[]{:S(2)}) async-start(bf16[4,128,640]{2,1,0:T(8,128)(2,1)} %shard_map.89), calls=%async_computation.4 | async-start | bytes 1310720 | tf_op jit(solution)/shard_map/all_to_all | solution.py:220
Sparse Core Ops, SparseCore 0:
  34.6 46.0 all-gather.2

commit v2 on v1

--- a/solution.py
+++ b/solution.py
@@ -59,7 +59,7 @@
     return jnp.dot(lower, decay, precision=lax.Precision.HIGHEST, preferred_element_type=F32)
 
 
-def update_kernel(x_ref, in_ref, decay_ref, out_ref):
+def update_kernel(x_ref, in_ref, decay_ref, after_ref, out_ref):
     cumulative = cumulative_of(decay_ref[...])
     last = cumulative[T - 1 : T, :]
     onehot = head_spread()
@@ -119,62 +119,86 @@
         out_ref[:, cut] = (ahead[:, cut] * (inner[:, cut] + start[:, cut] * carried)).astype(BF16)
 
 
-QT = 256
 CHUNK = NZ * T
-
-
-def attend_kernel(place_ref, q_ref, kv_ref, out_ref, k_buf, v_buf, q_buf, o_buf):
+QUERIES = GROUP * T
+KEYS = 512
+
+
+def pack_kernel(q_ref, k_ref, v_ref, out_ref):
+    pad = jnp.zeros((T, 384 - KVH * DH), F32)
+    k = jnp.concatenate([k_ref[...].astype(F32), pad], axis=1).T.astype(BF16)
+    v = jnp.concatenate([v_ref[...].astype(F32), pad], axis=1).T.astype(BF16)
+    for g in range(KVH):
+        q = q_ref[:, g * GDH : (g + 1) * GDH].astype(F32)
+        out_ref[g, :GDH, :] = q.T.astype(BF16)
+        out_ref[g, GDH : GDH + DH, :] = k[g * DH : (g + 1) * DH, :]
+        out_ref[g, GDH + DH :, :] = v[g * DH : (g + 1) * DH, :]
+
+
+def attend_kernel(place_ref, q_ref, kv_ref, after_ref, out_ref, kv_buf, k_buf, v_buf, q_buf, sems):
+    copies = [
+        pltpu.make_async_copy(kv_ref.at[:, c], kv_buf.at[c], sems.at[c]) for c in range(NX)
+    ]
+    for copy in copies:
+        copy.start()
     z = place_ref[0]
-    pad = jnp.zeros((128 - DH, CHUNK), BF16)
+    scale = math.log2(math.e) / math.sqrt(DH)
+    row = lax.broadcasted_iota(jnp.int32, (KEYS, QUERIES), 0)
+    col = lax.broadcasted_iota(jnp.int32, (KEYS, QUERIES), 1) % T
     ones = jnp.where(lax.broadcasted_iota(jnp.int32, (16, CHUNK), 0) == 0, 1.0, 0.0).astype(BF16)
+    blank = jnp.zeros((128 - DH, T), F32)
+    blank_q = jnp.zeros((128 - DH, QUERIES), BF16)
     for c in range(NX):
-        cut = slice(c * CHUNK, (c + 1) * CHUNK)
-        k_buf[DH:128, cut] = pad
-        k_buf[128 + DH : 256, cut] = pad
-        v_buf[DH : DH + 16, cut] = ones
+        q_buf[DH:128, :] = blank_q
+        q_buf[128 + DH :, :] = blank_q
+        for h in range(GROUP):
+            hi, lo = split2(q_ref[c, h * DH : (h + 1) * DH, :].astype(F32) * scale)
+            q_buf[:DH, h * T : (h + 1) * T] = hi
+            q_buf[128 : 128 + DH, h * T : (h + 1) * T] = lo
+        copies[c].wait()
+        v_buf[DH:, c * CHUNK : (c + 1) * CHUNK] = ones
         for b in range(NZ):
             at = slice(c * CHUNK + b * T, c * CHUNK + (b + 1) * T)
-            k = kv_ref[b, c, :DH, :]
-            k_buf[:DH, at] = k
-            k_buf[128 : 128 + DH, at] = k
-            v_buf[:DH, at] = kv_ref[b, c, DH:, :]
-    scale = math.log2(math.e) / math.sqrt(DH)
-    zero = jnp.zeros((T, 128 - DH), F32)
-    for c in range(NX):
+            v_buf[:DH, at] = kv_buf[c, b, DH:, :]
+            k = jnp.concatenate([kv_buf[c, b, :DH, :].astype(F32), blank], axis=0).T.astype(BF16)
+            k_buf[at, :128] = k
+            k_buf[at, 128:] = k
+        q = q_buf[...]
+
+        def scores(j, c=c, q=q):
+            found = dot(k_buf[j * KEYS : (j + 1) * KEYS, :], q)
+            if j * KEYS >= c * CHUNK:
+                seen = row + (j * KEYS - c * CHUNK) <= col + z * T
+                found = jnp.where(seen, found, masked_score)
+            return found
+
+        count = (c + 1) * CHUNK // KEYS
+        found = scores(0)
+        top = jnp.max(found, axis=0, keepdims=True)
+        total = None
+        for j in range(count):
+            later = scores(j + 1) if j + 1 < count else None
+            expos = jnp.exp2(found - top).astype(BF16)
+            summed = dot(v_buf[:, j * KEYS : (j + 1) * KEYS], expos)
+            total = summed if total is None else total + summed
+            if later is not None:
+                raised = jnp.maximum(top, jnp.max(later, axis=0, keepdims=True))
+                total = total * jnp.exp2(top - raised)
+                top = raised
+                found = later
+        done = (total[:DH, :] / total[DH : DH + 1, :]).astype(BF16)
         for h in range(GROUP):
-            q = q_ref[c, :, h * DH : (h + 1) * DH].astype(F32) * scale
-            hi, lo = split2(jnp.concatenate([q, zero], axis=1))
-            q_buf[c, h * T : (h + 1) * T, :128] = hi
-            q_buf[c, h * T : (h + 1) * T, 128:] = lo
-    row = lax.broadcasted_iota(jnp.int32, (QT, CHUNK), 0) % T
-    col = lax.broadcasted_iota(jnp.int32, (QT, CHUNK), 1)
-    visible = col <= row + z * T
-    for c in range(NX):
-        seen = c * CHUNK
-
-        def one_tile(i, carry, c=c, seen=seen):
-            at = pl.ds(pl.multiple_of(i * QT, QT), QT)
-            q = q_buf[c, at, :]
-            near = dot(q, k_buf[:, seen : seen + CHUNK])
-            near = jnp.where(visible, near, masked_score)
-            top = jnp.max(near, axis=1, keepdims=True)
-            if c:
-                far = dot(q, k_buf[:, :seen])
-                top = jnp.maximum(top, jnp.max(far, axis=1, keepdims=True))
-            total = dot_nt(jnp.exp2(near - top).astype(BF16), v_buf[:, seen : seen + CHUNK])
-            if c:
-                total += dot_nt(jnp.exp2(far - top).astype(BF16), v_buf[:, :seen])
-            o_buf[at, :] = total[:, :DH] / total[:, DH : DH + 1]
-            return carry
-
-        lax.fori_loop(0, GROUP * T // QT, one_tile, 0)
-        out_ref[c] = jnp.concatenate(
-            [o_buf[h * T : (h + 1) * T, :] for h in range(GROUP)], axis=1
-        ).astype(BF16)
+            out_ref[c, h * DH : (h + 1) * DH, :] = done[:, h * T : (h + 1) * T]
+
+
+def place_kernel(in_ref, after_ref, out_ref):
+    for g in range(KVH):
+        out_ref[:, g * GDH : (g + 1) * GDH] = in_ref[g].astype(F32).T.astype(BF16)
 
 
 VMEM_SPEC = pl.BlockSpec(memory_space=pltpu.VMEM)
 SMEM_SPEC = pl.BlockSpec(memory_space=pltpu.SMEM)
+ANY_SPEC = pl.BlockSpec(memory_space=pl.ANY)
 
 
 def call(kernel, shape, specs, scratch=(), limit=48):
@@ -191,36 +215,38 @@
 def per_device(mixer_input, input_map, output_map, log_decay, query_rows, key_rows, value_rows):
     place_z = lax.axis_index("cz").astype(jnp.int32).reshape(1)
     place = (lax.axis_index("cx") * NZ + lax.axis_index("cz")).astype(jnp.int32).reshape(1)
-    kv = jnp.concatenate(
-        [key_rows.T.reshape(KVH, DH, T), value_rows.T.reshape(KVH, DH, T)], axis=1
-    )
-    kv = lax.all_to_all(kv, "cx", 0, 0)
-    kv = lax.all_gather(kv, "cz")
-    q = query_rows.reshape(T, KVH, GDH).transpose(1, 0, 2)
-    q = lax.all_to_all(q, "cx", 0, 0)
+    packed = call(pack_kernel, (KVH, GDH + 2 * DH, T), [VMEM_SPEC] * 3)(
+        query_rows, key_rows, value_rows
+    )
+    packed = lax.all_to_all(packed, "cx", 0, 0)
+    kv_part = packed[:, GDH:, :]
+    kv = lax.all_gather(kv_part, "cz")
     update = call(
-        update_kernel, (NCTX, PIECE_ROWS, PIECE_COLS + 128), [VMEM_SPEC] * 3
-    )(mixer_input, input_map, log_decay)
+        update_kernel, (NCTX, PIECE_ROWS, PIECE_COLS + 128), [VMEM_SPEC] * 3 + [ANY_SPEC]
+    )(mixer_input, input_map, log_decay, packed)
     update = lax.all_to_all(update, ("cx", "cz"), 0, 0)
-    entering = call(prefix_kernel, (NCTX, PIECE_ROWS, PIECE_COLS), [SMEM_SPEC, VMEM_SPEC])(
+    prefix = call(prefix_kernel, (NCTX, PIECE_ROWS, PIECE_COLS), [SMEM_SPEC, VMEM_SPEC])(
         place, update
     )
-    entering = lax.all_to_all(entering, ("cx", "cz"), 0, 0)
+    entering = lax.all_to_all(prefix, ("cx", "cz"), 0, 0)
     attended = call(
         attend_kernel,
-        (NX, T, GDH),
-        [SMEM_SPEC, VMEM_SPEC, VMEM_SPEC],
+        (NX, GDH, T),
+        [SMEM_SPEC, VMEM_SPEC, ANY_SPEC, ANY_SPEC],
         [
-            pltpu.VMEM((256, NX * CHUNK), BF16),
+            pltpu.VMEM((NX, NZ, 2 * DH, T), BF16),
+            pltpu.VMEM((NX * CHUNK, 256), BF16),
             pltpu.VMEM((DH + 16, NX * CHUNK), BF16),
-            pltpu.VMEM((NX, GROUP * T, 256), BF16),
-            pltpu.VMEM((GROUP * T, DH), F32),
+            pltpu.VMEM((256, QUERIES), BF16),
+            pltpu.SemaphoreType.DMA((NX,)),
         ],
-    )(place_z, q, kv)
+    )(place_z, packed, kv, prefix)
     attended = lax.all_to_all(attended, "cx", 0, 0)
-    attention_output = attended.transpose(1, 0, 2).reshape(T, QH * DH)
     mixer_output = call(mix_kernel, (T, WIDTH), [VMEM_SPEC] * 5)(
         mixer_input, input_map, output_map, log_decay, entering
+    )
+    attention_output = call(place_kernel, (T, QH * DH), [VMEM_SPEC, VMEM_SPEC])(
+        attended, mixer_output[:16, :128]
     )
     return mixer_output, attention_output
 

time: 138 us -> 134 us (0.971)
  waiting for transfers between devices: 44.4 us -> 64.2 us
  Pallas kernels: 39.9 us -> 24.1 us
  starting transfers between devices: 30 us -> 25 us
  other arithmetic: 1.61 us -> 0 us
    all_gather x1, waiting for transfers between devices: 8.96 us -> 25.3 us  [per_device(): kv = lax.all_gather(kv_part, 'cz')]
    pallas_call x2 -> x4, Pallas kernels: 35.3 us -> 19.5 us  [the longest x1 15 us: per_device(): call(attend_kernel, (NX, GDH, T), [SMEM_SPEC, VMEM_SPEC, ANY_SPEC, ANY_SP...]
    all_to_all x3 -> x2, waiting for transfers between devices: 8.19 us -> 12.5 us  [the longest x1 12.5 us: per_device(): packed = lax.all_to_all(packed, 'cx', 0, 0)]
    all_to_all x3 -> x2, starting transfers between devices: 12.8 us -> 9.35 us  [the longest x1 5.06 us: per_device(): entering = lax.all_to_all(prefix, ('cx', 'cz'), 0, 0)]
    concatenate x1 -> x0, other arithmetic: 1.61 us -> none  [per_device(): jnp.concatenate([key_rows.T.reshape(KVH, DH, T), value_rows.T.reshape(KVH...]
    unnamed x19 -> x15, local copies, waits for them, and re-layouts: 5.41 us -> 4.52 us
  transfers between devices with their start and end apart: 6 -> 5, of which waited for: 5 -> 4; matrix products, arithmetic and copies ran while one was open for 2% -> 1% of each run, Pallas kernels for 29% -> 15%
where the time goes in v2:
time: 134 us; the launch traced here: 133 us
  waiting for transfers between devices  64.2 us (48%)
  starting transfers between devices  25 us (19%)
  Pallas kernels  24.1 us (18%)
  between operations  14.1 us (11%)
  local copies, waits for them, and re-layouts  5.88 us (4%)
    all_gather x1, waiting for transfers between devices, per_device(): kv = lax.all_gather(kv_part, 'cz')  25.3 us
    all_to_all x1, waiting for transfers between devices, per_device(): update = lax.all_to_all(update, ('cx', 'cz'), 0, 0)  21.1 us
    pallas_call x1, Pallas kernels, per_device(): call(attend_kernel, (NX, GDH, T), [SMEM_SPEC, VMEM_SPEC, ANY_SPEC, ANY_SP...  15 us
    all_to_all x1, waiting for transfers between devices, per_device(): packed = lax.all_to_all(packed, 'cx', 0, 0)  12.5 us
    all_to_all x1, starting transfers between devices, per_device(): update = lax.all_to_all(update, ('cx', 'cz'), 0, 0)  11.3 us
    all_to_all x1, waiting for transfers between devices, per_device(): attended = lax.all_to_all(attended, 'cx', 0, 0)  5.32 us
    all_to_all x1, starting transfers between devices, per_device(): entering = lax.all_to_all(prefix, ('cx', 'cz'), 0, 0)  5.06 us
    unnamed x15, local copies, waits for them, and re-layouts  4.52 us
  transfers between devices with their start and end apart: 5, of which 4 were waited for; matrix products, arithmetic and copies ran while one was open for 1% of the time, Pallas kernels for 15%

profile of v2, /device:TPU:56, one launch (start us, length us, event | category | flops | bytes accessed | tf_op | source)
XLA Modules:
  0.0 133.3 jit_solution(17967574565821697001)
XLA Ops:
  7.2 1.0 copy.13.k_ref
  8.2 1.0 copy.14.v_ref
  9.2 0.0 copy-start.2
  9.2 1.1 copy-done.2
  10.3 0.0 copy-start.5
  10.3 0.0 copy-start
  10.3 0.0 copy-start.3
  10.3 1.2 shard_map.86
  11.5 4.3 %all-to-all-start = ((bf16[4,800,128]{2,1,0:T(8,128)(2,1)}), bf16[4,800,128]{2,1,0:T(8,128)(2,1)S(1)}, u32[]{:S(2)}, u32[]{:S(2)}) async-start(bf16[4,800,128]{2,1,0:T(8,128)(2,1)} %shard_map.86), calls=%async_computation | async-start | bytes 1638400 | tf_op jit(solution)/shard_map/all_to_all | solution.py:221
  15.8 0.0 copy-done.5
  15.8 0.1 copy.16.decay_ref
  15.9 12.5 %all-to-all-done.after_ref.q_ref = bf16[4,800,128]{2,1,0:T(8,128)(2,1)S(1)} async-done(((bf16[4,800,128]{2,1,0:T(8,128)(2,1)}), bf16[4,800,128]{2,1,0:T(8,128)(2,1)S(1)}, u32[]{:S(2)}, u32[]{:S(2)}) %all-to-all-start) | async-done | bytes 819232 | tf_op jit(solution)/shard_map/all_to_all | solution.py:221
  28.4 0.0 copy-done
  28.4 0.0 copy-done.3
  28.4 2.2 %shard_map.87 = bf16[32,16,768]{2,1,0:T(8,128)(2,1)} custom-call(bf16[128,2560]{1,0:T(8,128)(2,1)S(1)} %copy-done, bf16[128,128]{1,0:T(8,128)(2,1)S(1)} %copy-done.3, f32[128,40]{1,0:T(8,128)S(1)} %copy.16.decay_ref, bf16[4,800,128]{2,1,0:T(8,128)(2,1)S(1)} %all-to-all-done.after_ref.q_ref), custom_call_target="tpu_custom_call" | custom-call | tf_op jit(solution)/shard_map/pallas_call | solution.py:224
  30.6 11.3 %all-to-all-start.1 = ((bf16[32,16,768]{2,1,0:T(8,128)(2,1)}), bf16[32,16,768]{2,1,0:T(8,128)(2,1)S(1)}, u32[]{:S(2)}, u32[]{:S(2)}) async-start(bf16[32,16,768]{2,1,0:T(8,128)(2,1)} %shard_map.87), calls=%async_computation.1 | async-start | bytes 1572864 | tf_op jit(solution)/shard_map/all_to_all | solution.py:227
  42.0 0.0 all-gather.3.cloned.1.call-start
  42.0 0.7 slice.8
  42.7 0.0 all-gather.3.cloned.1.call-update
  42.7 21.1 %all-to-all-done.1.in_ref = bf16[32,16,768]{2,1,0:T(8,128)(2,1)S(1)} async-done(((bf16[32,16,768]{2,1,0:T(8,128)(2,1)}), bf16[32,16,768]{2,1,0:T(8,128)(2,1)S(1)}, u32[]{:S(2)}, u32[]{:S(2)}) %all-to-all-start.1) | async-done | bytes 786464 | tf_op jit(solution)/shard_map/all_to_all | solution.py:227
  63.8 1.8 %shard_map.88.after_ref = bf16[32,16,640]{2,1,0:T(8,128)(2,1)} custom-call(s32[1]{0:T(128)} %bitcast.place_ref, bf16[32,16,768]{2,1,0:T(8,128)(2,1)S(1)} %all-to-all-done.1.in_ref), custom_call_target="tpu_custom_call" | custom-call | tf_op jit(solution)/shard_map/pallas_call | solution.py:228
  65.6 5.1 %all-to-all-start.2 = ((bf16[32,16,640]{2,1,0:T(8,128)(2,1)}), bf16[32,16,640]{2,1,0:T(8,128)(2,1)S(1)}, u32[]{:S(2)}, u32[]{:S(2)}) async-start(bf16[32,16,640]{2,1,0:T(8,128)(2,1)} %shard_map.88.after_ref), calls=%async_computation.2 | async-start | bytes 1310720 | tf_op jit(solution)/shard_map/all_to_all | solution.py:231
  70.7 25.3 %all-gather.3.cloned.1.call-done = bf16[32,160,128]{2,1,0:T(8,128)(2,1)} async-done(((bf16[4,160,128]{2,1,0:T(8,128)(2,1)}), bf16[32,160,128]{2,1,0:T(8,128)(2,1)}) %all-gather.3.cloned.1.call-update) | async-done | bytes 1310736 | tf_op jit(solution)/shard_map/all_gather | solution.py:223
  95.9 0.0 copy-start.1
  95.9 1.3 copy-done.1
  97.3 15.0 %shard_map.90 = bf16[4,640,128]{2,1,0:T(8,128)(2,1)} custom-call(s32[1]{0:T(128)} %bitcast.1.place_ref, bf16[4,800,128]{2,1,0:T(8,128)(2,1)S(1)} %all-to-all-done.after_ref.q_ref, bf16[8,4,160,128]{3,2,1,0:T(8,128)(2,1)S(1)} %bitcast.3, bf16[32,16,640]{2,1,0:T(8,128)(2,1)} %shard_map.88.after_ref), custom_call_target="tpu_custom_call" | custom-call | tf_op jit(solution)/shard_map/pallas_call | solution.py:232
  112.3 0.0 copy-start.4
  112.3 0.0 all-to-all-done.2.enter_ref
  112.3 4.3 %all-to-all-start.3 = ((bf16[4,640,128]{2,1,0:T(8,128)(2,1)}), bf16[4,640,128]{2,1,0:T(8,128)(2,1)S(1)}, u32[]{:S(2)}, u32[]{:S(2)}) async-start(bf16[4,640,128]{2,1,0:T(8,128)(2,1)} %shard_map.90), calls=%async_computation.3 | async-start | bytes 1310720 | tf_op jit(solution)/shard_map/all_to_all | solution.py:244
  116.6 0.0 copy-done.4
  116.6 2.8 %shard_map.89 = bf16[128,2560]{1,0:T(8,128)(2,1)} custom-call(bf16[128,2560]{1,0:T(8,128)(2,1)S(1)} %copy-done, bf16[128,128]{1,0:T(8,128)(2,1)S(1)} %copy-done.3, bf16[128,128]{1,0:T(8,128)(2,1)S(1)} %copy-done.4, f32[128,40]{1,0:T(8,128)S(1)} %copy.16.decay_ref, bf16[32,16,640]{2,1,0:T(8,128)(2,1)S(1)} %all-to-all-done.2.enter_ref), custom_call_target="tpu_custom_call" | custom-call | tf_op jit(solution)/shard_map/pallas_call | solution.py:245
  119.4 0.7 slice.9.after_ref
  120.1 5.3 %all-to-all-done.3.in_ref = bf16[4,640,128]{2,1,0:T(8,128)(2,1)S(1)} async-done(((bf16[4,640,128]{2,1,0:T(8,128)(2,1)}), bf16[4,640,128]{2,1,0:T(8,128)(2,1)S(1)}, u32[]{:S(2)}, u32[]{:S(2)}) %all-to-all-start.3) | async-done | bytes 655392 | tf_op jit(solution)/shard_map/all_to_all | solution.py:244
  125.4 1.1 shard_map.91
Async XLA Ops:
  9.2 1.1 copy-start.2
  10.3 5.5 %copy-start.5 = (f32[128,40]{0,1:T(8,128)S(1)}, f32[128,40]{0,1:T(8,128)}, u32[]{:S(2)}) copy-start(f32[128,40]{0,1:T(8,128)} %param.10) | copy-start | bytes 61444
  10.3 18.1 %copy-start = (bf16[128,2560]{1,0:T(8,128)(2,1)S(1)}, bf16[128,2560]{1,0:T(8,128)(2,1)}, u32[]{:S(2)}) copy-start(bf16[128,2560]{1,0:T(8,128)(2,1)} %x_ref.3) | copy-start | bytes 1966084
  10.3 18.1 %copy-start.3 = (bf16[128,128]{1,0:T(8,128)(2,1)S(1)}, bf16[128,128]{1,0:T(8,128)(2,1)}, u32[]{:S(2)}) copy-start(bf16[128,128]{1,0:T(8,128)(2,1)} %in_ref.3) | copy-start | bytes 98308
  11.5 16.9 %all-to-all-start = ((bf16[4,800,128]{2,1,0:T(8,128)(2,1)}), bf16[4,800,128]{2,1,0:T(8,128)(2,1)S(1)}, u32[]{:S(2)}, u32[]{:S(2)}) async-start(bf16[4,800,128]{2,1,0:T(8,128)(2,1)} %shard_map.86), calls=%async_computation | async-start | bytes 1638400 | tf_op jit(solution)/shard_map/all_to_all | solution.py:221
  30.6 33.2 %all-to-all-start.1 = ((bf16[32,16,768]{2,1,0:T(8,128)(2,1)}), bf16[32,16,768]{2,1,0:T(8,128)(2,1)S(1)}, u32[]{:S(2)}, u32[]{:S(2)}) async-start(bf16[32,16,768]{2,1,0:T(8,128)(2,1)} %shard_map.87), calls=%async_computation.1 | async-start | bytes 1572864 | tf_op jit(solution)/shard_map/all_to_all | solution.py:227
  42.0 54.0 %all-gather.3.cloned.1.call-start = ((), (), s32[]{:S(2)}) async-start(), calls=%async_computation.4 | async-start | bytes 1474560 | tf_op jit(solution)/shard_map/all_gather | solution.py:223
  65.6 46.7 %all-to-all-start.2 = ((bf16[32,16,640]{2,1,0:T(8,128)(2,1)}), bf16[32,16,640]{2,1,0:T(8,128)(2,1)S(1)}, u32[]{:S(2)}, u32[]{:S(2)}) async-start(bf16[32,16,640]{2,1,0:T(8,128)(2,1)} %shard_map.88.after_ref), calls=%async_computation.2 | async-start | bytes 1310720 | tf_op jit(solution)/shard_map/all_to_all | solution.py:231
  95.9 1.3 copy-start.1
  112.3 4.3 %copy-start.4 = (bf16[128,128]{1,0:T(8,128)(2,1)S(1)}, bf16[128,128]{1,0:T(8,128)(2,1)}, u32[]{:S(2)}) copy-start(bf16[128,128]{1,0:T(8,128)(2,1)} %map_ref.1) | copy-start | bytes 98308
  112.3 13.1 %all-to-all-start.3 = ((bf16[4,640,128]{2,1,0:T(8,128)(2,1)}), bf16[4,640,128]{2,1,0:T(8,128)(2,1)S(1)}, u32[]{:S(2)}, u32[]{:S(2)}) async-start(bf16[4,640,128]{2,1,0:T(8,128)(2,1)} %shard_map.90), calls=%async_computation.3 | async-start | bytes 1310720 | tf_op jit(solution)/shard_map/all_to_all | solution.py:244
Sparse Core Ops, SparseCore 0:
  45.5 50.4 all-gather.2

commit v3 on v2

--- a/solution.py
+++ b/solution.py
@@ -19,7 +19,8 @@
 GROUP = QH // KVH
 GDH = GROUP * DH
 NX = 4
-NZ = 8
+NH = 4
+NZ = 2 * NH
 NCTX = NX * NZ
 PIECE_ROWS = 16
 PIECE_COLS = 640
@@ -56,10 +57,16 @@
     rows = lax.broadcasted_iota(jnp.int32, (T, T), 0)
     cols = lax.broadcasted_iota(jnp.int32, (T, T), 1)
     lower = jnp.where(cols <= rows, 1.0, 0.0).astype(F32)
-    return jnp.dot(lower, decay, precision=lax.Precision.HIGHEST, preferred_element_type=F32)
-
-
-def update_kernel(x_ref, in_ref, decay_ref, after_ref, out_ref):
+    return lax.dot_general(
+        lower,
+        decay,
+        (((1,), (1,)), ((), ())),
+        precision=lax.Precision.HIGHEST,
+        preferred_element_type=F32,
+    )
+
+
+def update_kernel(x_ref, in_ref, decay_ref, out_ref):
     cumulative = cumulative_of(decay_ref[...])
     last = cumulative[T - 1 : T, :]
     onehot = head_spread()
@@ -83,7 +90,7 @@
             out_ref[d, :, PIECE_COLS:] = factor
 
 
-def prefix_kernel(place_ref, in_ref, out_ref):
+def prefix_kernel(place_ref, in_ref, after_ref, out_ref):
     first_head = (place_ref[0] % (WIDTH // PIECE_COLS)) * (PIECE_COLS // P_SIZE)
     lane = lax.broadcasted_iota(jnp.int32, (128, PIECE_COLS), 0)
     cols = lax.broadcasted_iota(jnp.int32, (128, PIECE_COLS), 1)
@@ -125,23 +132,34 @@
 
 
 def pack_kernel(q_ref, k_ref, v_ref, out_ref):
-    pad = jnp.zeros((T, 384 - KVH * DH), F32)
-    k = jnp.concatenate([k_ref[...].astype(F32), pad], axis=1).T.astype(BF16)
-    v = jnp.concatenate([v_ref[...].astype(F32), pad], axis=1).T.astype(BF16)
     for g in range(KVH):
         q = q_ref[:, g * GDH : (g + 1) * GDH].astype(F32)
         out_ref[g, :GDH, :] = q.T.astype(BF16)
-        out_ref[g, GDH : GDH + DH, :] = k[g * DH : (g + 1) * DH, :]
-        out_ref[g, GDH + DH :, :] = v[g * DH : (g + 1) * DH, :]
-
-
-def attend_kernel(place_ref, q_ref, kv_ref, after_ref, out_ref, kv_buf, k_buf, v_buf, q_buf, sems):
-    copies = [
-        pltpu.make_async_copy(kv_ref.at[:, c], kv_buf.at[c], sems.at[c]) for c in range(NX)
-    ]
-    for copy in copies:
-        copy.start()
+        out_ref[g, GDH : GDH + DH, :] = k_ref[g * DH : (g + 1) * DH, :]
+        out_ref[g, GDH + DH :, :] = v_ref[g * DH : (g + 1) * DH, :]
+
+
+def attend_kernel(
+    place_ref, q_ref, same_ref, below_ref, above_ref, after_ref, out_ref, kv_buf, k_buf, v_buf, q_buf, sems
+):
     z = place_ref[0]
+    parity = z % 2
+    half = NH // 2
+    copies = []
+    for c in range(NX):
+        copies.append(
+            [
+                pltpu.make_async_copy(same_ref.at[:, c], kv_buf.at[c, :, parity], sems.at[c, 0]),
+                pltpu.make_async_copy(
+                    below_ref.at[:, c], kv_buf.at[c, pl.ds(0, half), 1 - parity], sems.at[c, 1]
+                ),
+                pltpu.make_async_copy(
+                    above_ref.at[:, c], kv_buf.at[c, pl.ds(half, half), 1 - parity], sems.at[c, 2]
+                ),
+            ]
+        )
+        for copy in copies[c]:
+            copy.start()
     scale = math.log2(math.e) / math.sqrt(DH)
     row = lax.broadcasted_iota(jnp.int32, (KEYS, QUERIES), 0)
     col = lax.broadcasted_iota(jnp.int32, (KEYS, QUERIES), 1) % T
@@ -155,12 +173,13 @@
             hi, lo = split2(q_ref[c, h * DH : (h + 1) * DH, :].astype(F32) * scale)
             q_buf[:DH, h * T : (h + 1) * T] = hi
             q_buf[128 : 128 + DH, h * T : (h + 1) * T] = lo
-        copies[c].wait()
+        for copy in copies[c]:
+            copy.wait()
         v_buf[DH:, c * CHUNK : (c + 1) * CHUNK] = ones
         for b in range(NZ):
             at = slice(c * CHUNK + b * T, c * CHUNK + (b + 1) * T)
-            v_buf[:DH, at] = kv_buf[c, b, DH:, :]
-            k = jnp.concatenate([kv_buf[c, b, :DH, :].astype(F32), blank], axis=0).T.astype(BF16)
+            v_buf[:DH, at] = kv_buf[c, b // 2, b % 2, DH:, :]
+            k = jnp.concatenate([kv_buf[c, b // 2, b % 2, :DH, :].astype(F32), blank], axis=0).T.astype(BF16)
             k_buf[at, :128] = k
             k_buf[at, 128:] = k
         q = q_buf[...]
@@ -213,37 +232,38 @@
 
 
 def per_device(mixer_input, input_map, output_map, log_decay, query_rows, key_rows, value_rows):
-    place_z = lax.axis_index("cz").astype(jnp.int32).reshape(1)
-    place = (lax.axis_index("cx") * NZ + lax.axis_index("cz")).astype(jnp.int32).reshape(1)
+    place_z = lax.axis_index(("zh", "zl")).astype(jnp.int32).reshape(1)
+    place = lax.axis_index(("cx", "zh", "zl")).astype(jnp.int32).reshape(1)
     packed = call(pack_kernel, (KVH, GDH + 2 * DH, T), [VMEM_SPEC] * 3)(
-        query_rows, key_rows, value_rows
+        query_rows, key_rows.T, value_rows.T
     )
     packed = lax.all_to_all(packed, "cx", 0, 0)
-    kv_part = packed[:, GDH:, :]
-    kv = lax.all_gather(kv_part, "cz")
+    same = lax.all_gather(packed[:, GDH:, :], "zh")
+    below = lax.ppermute(same[: NH // 2], ("zh", "zl"), [(k, (k + 1) % NZ) for k in range(NZ)])
+    above = lax.ppermute(same[NH // 2 :], ("zh", "zl"), [(k, (k - 1) % NZ) for k in range(NZ)])
     update = call(
-        update_kernel, (NCTX, PIECE_ROWS, PIECE_COLS + 128), [VMEM_SPEC] * 3 + [ANY_SPEC]
-    )(mixer_input, input_map, log_decay, packed)
-    update = lax.all_to_all(update, ("cx", "cz"), 0, 0)
-    prefix = call(prefix_kernel, (NCTX, PIECE_ROWS, PIECE_COLS), [SMEM_SPEC, VMEM_SPEC])(
-        place, update
-    )
-    entering = lax.all_to_all(prefix, ("cx", "cz"), 0, 0)
+        update_kernel, (NCTX, PIECE_ROWS, PIECE_COLS + 128), [VMEM_SPEC] * 3
+    )(mixer_input, input_map, log_decay.T)
+    update = lax.all_to_all(update, ("cx", "zh", "zl"), 0, 0)
+    prefix = call(prefix_kernel, (NCTX, PIECE_ROWS, PIECE_COLS), [SMEM_SPEC, VMEM_SPEC, ANY_SPEC])(
+        place, update, same
+    )
+    entering = lax.all_to_all(prefix, ("cx", "zh", "zl"), 0, 0)
     attended = call(
         attend_kernel,
         (NX, GDH, T),
-        [SMEM_SPEC, VMEM_SPEC, ANY_SPEC, ANY_SPEC],
+        [SMEM_SPEC, VMEM_SPEC] + [ANY_SPEC] * 4,
         [
-            pltpu.VMEM((NX, NZ, 2 * DH, T), BF16),
+            pltpu.VMEM((NX, NH, 2, 2 * DH, T), BF16),
             pltpu.VMEM((NX * CHUNK, 256), BF16),
             pltpu.VMEM((DH + 16, NX * CHUNK), BF16),
             pltpu.VMEM((256, QUERIES), BF16),
-            pltpu.SemaphoreType.DMA((NX,)),
+            pltpu.SemaphoreType.DMA((NX, 3)),
         ],
-    )(place_z, packed, kv, prefix)
+    )(place_z, packed, same, below, above, prefix)
     attended = lax.all_to_all(attended, "cx", 0, 0)
     mixer_output = call(mix_kernel, (T, WIDTH), [VMEM_SPEC] * 5)(
-        mixer_input, input_map, output_map, log_decay, entering
+        mixer_input, input_map, output_map, log_decay.T, entering
     )
     attention_output = call(place_kernel, (T, QH * DH), [VMEM_SPEC, VMEM_SPEC])(
         attended, mixer_output[:16, :128]
@@ -252,8 +272,8 @@
 
 
 def solution(mesh):
-    grid = Mesh(mesh.devices.reshape(-1, NX, NZ), ("dp", "cx", "cz"))
-    spec = P(("dp", "cx", "cz"), None)
+    grid = Mesh(mesh.devices.reshape(-1, NX, NH, 2), ("dp", "cx", "zh", "zl"))
+    spec = P(("dp", "cx", "zh", "zl"), None)
     return jax.shard_map(
         per_device,
         mesh=grid,

time: 134 us -> 126 us (0.940)
  waiting for transfers between devices: 64.2 us -> 28.1 us
  blocking collectives: 0 us -> 33 us
  between operations: 14.1 us -> 0.73 us
  starting transfers between devices: 25 us -> 35.1 us
  local copies, waits for them, and re-layouts: 5.88 us -> 4.44 us
    all_gather x0 -> x1, blocking collectives: none -> 33 us  [per_device(): same = lax.all_gather(packed[:, GDH:, :], 'zh')]
    all_gather x1 -> x0, waiting for transfers between devices: 25.3 us -> none  [per_device(): kv = lax.all_gather(kv_part, 'cz')]
    all_to_all x2, waiting for transfers between devices: 21.1 us -> 0.01 us  [the longest x1 0.01 us: per_device(): entering = lax.all_to_all(prefix, ('cx', 'zh', 'zl'), 0, 0)]
    ppermute x0 -> x2, waiting for transfers between devices: none -> 12.3 us  [the longest x1 12.3 us: per_device(): lax.ppermute(same[:NH // 2], ('zh', 'zl'), [(k, (k + 1) % NZ) for k in ra...]
    ppermute x0 -> x2, starting transfers between devices: none -> 7.05 us  [the longest x1 3.7 us: per_device(): lax.ppermute(same[:NH // 2], ('zh', 'zl'), [(k, (k + 1) % NZ) for k in ra...]
    all_to_all x2, starting transfers between devices: 16.4 us -> 19.2 us  [the longest x1 11.3 us: per_device(): update = lax.all_to_all(update, ('cx', 'zh', 'zl'), 0, 0)]
    all_to_all x1, waiting for transfers between devices: 12.5 us -> 10.4 us  [per_device(): packed = lax.all_to_all(packed, 'cx', 0, 0)]
    unnamed x15 -> x16, local copies, waits for them, and re-layouts: 4.52 us -> 3.7 us
  transfers between devices with their start and end apart: 5 -> 6, of which waited for: 4 -> 3; matrix products, arithmetic and copies ran while one was open for 1% -> 1% of each run, Pallas kernels for 15% -> 16%
where the time goes in v3:
time: 126 us; the launch traced here: 125 us
  starting transfers between devices  35.1 us (28%)
  blocking collectives  33 us (26%)
  waiting for transfers between devices  28.1 us (22%)
  Pallas kernels  23.8 us (19%)
  local copies, waits for them, and re-layouts  4.44 us (4%)
    all_gather x1, blocking collectives, per_device(): same = lax.all_gather(packed[:, GDH:, :], 'zh')  33 us
    pallas_call x1, Pallas kernels, per_device(): call(attend_kernel, (NX, GDH, T), [SMEM_SPEC, VMEM_SPEC] + [ANY_SPEC] * 4...  14.8 us
    ppermute x1, waiting for transfers between devices, per_device(): lax.ppermute(same[:NH // 2], ('zh', 'zl'), [(k, (k + 1) % NZ) for k in ra...  12.3 us
    all_to_all x1, starting transfers between devices, per_device(): update = lax.all_to_all(update, ('cx', 'zh', 'zl'), 0, 0)  11.3 us
    all_to_all x1, waiting for transfers between devices, per_device(): packed = lax.all_to_all(packed, 'cx', 0, 0)  10.4 us
    all_to_all x1, starting transfers between devices, per_device(): entering = lax.all_to_all(prefix, ('cx', 'zh', 'zl'), 0, 0)  7.88 us
    all_to_all x1, waiting for transfers between devices, per_device(): attended = lax.all_to_all(attended, 'cx', 0, 0)  5.35 us
    all_to_all x1, starting transfers between devices, per_device(): packed = lax.all_to_all(packed, 'cx', 0, 0)  4.42 us
  transfers between devices with their start and end apart: 6, of which 3 were waited for; matrix products, arithmetic and copies ran while one was open for 1% of the time, Pallas kernels for 16%

profile of v3, /device:TPU:56, one launch (start us, length us, event | category | flops | bytes accessed | tf_op | source)
XLA Modules:
  0.0 125.2 jit_solution(9970220001410316250)
XLA Ops:
  0.6 0.0 copy-start.2
  0.6 1.1 copy-done.2
  1.7 0.0 copy-start.4
  1.7 0.9 copy-done.4
  2.6 0.0 copy-start.5
  2.6 0.9 copy-done.5
  3.5 1.1 shard_map.87
  4.6 0.0 copy-start
  4.6 0.0 copy-start.3
  4.6 0.0 copy-start.6
  4.6 4.4 %all-to-all-start.1 = ((bf16[4,800,128]{2,1,0:T(8,128)(2,1)}), bf16[4,800,128]{2,1,0:T(8,128)(2,1)S(1)}, u32[]{:S(2)}, u32[]{:S(2)}) async-start(bf16[4,800,128]{2,1,0:T(8,128)(2,1)} %shard_map.87), calls=%async_computation.1 | async-start | bytes 1638400 | tf_op jit(solution)/shard_map/all_to_all | solution.py:240
  9.1 0.0 copy-done
  9.1 0.0 copy-done.3
  9.1 0.0 copy-done.6
  9.1 2.2 %shard_map.86 = bf16[32,16,768]{2,1,0:T(8,128)(2,1)} custom-call(bf16[128,2560]{1,0:T(8,128)(2,1)S(1)} %copy-done, bf16[128,128]{1,0:T(8,128)(2,1)S(1)} %copy-done.3, f32[40,128]{1,0:T(8,128)S(1)} %bitcast.12), custom_call_target="tpu_custom_call" | custom-call | tf_op jit(solution)/shard_map/pallas_call | solution.py:244
  11.3 10.4 %all-to-all-done.1.q_ref = bf16[4,800,128]{2,1,0:T(8,128)(2,1)S(1)} async-done(((bf16[4,800,128]{2,1,0:T(8,128)(2,1)}), bf16[4,800,128]{2,1,0:T(8,128)(2,1)S(1)}, u32[]{:S(2)}, u32[]{:S(2)}) %all-to-all-start.1) | async-done | bytes 819232 | tf_op jit(solution)/shard_map/all_to_all | solution.py:240
  21.7 11.3 %all-to-all-start = ((bf16[32,16,768]{2,1,0:T(8,128)(2,1)}), bf16[32,16,768]{2,1,0:T(8,128)(2,1)S(1)}, u32[]{:S(2)}, u32[]{:S(2)}) async-start(bf16[32,16,768]{2,1,0:T(8,128)(2,1)} %shard_map.86), calls=%async_computation | async-start | bytes 1572864 | tf_op jit(solution)/shard_map/all_to_all | solution.py:247
  33.0 33.0 %all-gather = bf16[16,160,128]{2,1,0:T(8,128)(2,1)S(1)} all-gather(bf16[4,160,128]{2,1,0:T(8,128)(2,1)S(1)} %slice.18), channel_id=2, replica_groups=mesh['dp'=16,'cx'=4,'zh'=4,'zl'=2] {'zh'}, dimensions={0}, use_global_device_ids=true | all-gather | bytes 819200 | tf_op jit(solution)/shard_map/all_gather | solution.py:241
  66.0 0.0 all-to-all-done.in_ref
  66.0 1.8 %shard_map.88.after_ref = bf16[32,16,640]{2,1,0:T(8,128)(2,1)} custom-call(s32[1]{0:T(128)} %bitcast.1.place_ref, bf16[32,16,768]{2,1,0:T(8,128)(2,1)S(1)} %all-to-all-done.in_ref, bf16[4,4,160,128]{3,2,1,0:T(8,128)(2,1)S(1)} %bitcast.8), custom_call_target="tpu_custom_call" | custom-call | tf_op jit(solution)/shard_map/pallas_call | solution.py:248
  67.9 7.9 %all-to-all-start.2 = ((bf16[32,16,640]{2,1,0:T(8,128)(2,1)}), bf16[32,16,640]{2,1,0:T(8,128)(2,1)S(1)}, u32[]{:S(2)}, u32[]{:S(2)}) async-start(bf16[32,16,640]{2,1,0:T(8,128)(2,1)} %shard_map.88.after_ref), calls=%async_computation.2 | async-start | bytes 1310720 | tf_op jit(solution)/shard_map/all_to_all | solution.py:251
  75.8 3.7 %collective-permute-start = (bf16[2,4,160,128]{3,2,1,0:T(8,128)(2,1)S(1)}, bf16[2,4,160,128]{3,2,1,0:T(8,128)(2,1)S(1)}, u32[]{:S(2)}, u32[]{:S(2)}) collective-permute-start(bf16[2,4,160,128]{3,2,1,0:T(8,128)(2,1)S(1)} %bitcast.15), channel_id=1, source_target_pairs={{0,1},{1,2},{2,3},{3,4},{4,5},{5,6},{6,7},{7,0},{8,9},{9,10},{10,1... | collective-permute-start | bytes 983048 | tf_op jit(solution)/shard_map/ppermute | solution.py:242
  79.5 3.4 %collective-permute-start.1 = (bf16[2,4,160,128]{3,2,1,0:T(8,128)(2,1)S(1)}, bf16[2,4,160,128]{3,2,1,0:T(8,128)(2,1)S(1)}, u32[]{:S(2)}, u32[]{:S(2)}) collective-permute-start(bf16[2,4,160,128]{3,2,1,0:T(8,128)(2,1)S(1)} %bitcast.14), channel_id=1, source_target_pairs={{0,7},{1,0},{2,1},{3,2},{4,3},{5,4},{6,5},{7,6},{8,15},{9,8},{10,9... | collective-permute-start | bytes 983048 | tf_op jit(solution)/shard_map/ppermute | solution.py:243
  82.9 12.3 %collective-permute-done.below_ref = bf16[2,4,160,128]{3,2,1,0:T(8,128)(2,1)S(1)} collective-permute-done((bf16[2,4,160,128]{3,2,1,0:T(8,128)(2,1)S(1)}, bf16[2,4,160,128]{3,2,1,0:T(8,128)(2,1)S(1)}, u32[]{:S(2)}, u32[]{:S(2)}) %collective-permute-start) | collective-permute-done | bytes 327712 | tf_op jit(solution)/shard_map/ppermute | solution.py:242
  95.2 0.0 collective-permute-done.1.above_ref
  95.2 14.8 %shard_map.90 = bf16[4,640,128]{2,1,0:T(8,128)(2,1)S(1)} custom-call(s32[1]{0:T(128)} %bitcast.5.place_ref, bf16[4,800,128]{2,1,0:T(8,128)(2,1)S(1)} %all-to-all-done.1.q_ref, bf16[4,4,160,128]{3,2,1,0:T(8,128)(2,1)S(1)} %bitcast.9, bf16[2,4,160,128]{3,2,1,0:T(8,128)(2,1)S(1)} %collective-permute-done.below_ref, ...), custom_call_target="tpu_custom_call" | custom-call | tf_op jit(solution)/shard_map/pallas_call | solution.py:252
  110.0 0.0 copy-start.1
  110.1 0.8 copy-done.1
  110.9 0.0 copy-start.7
  110.9 0.0 all-to-all-done.2.enter_ref
  110.9 4.4 %all-to-all-start.3 = ((bf16[4,640,128]{2,1,0:T(8,128)(2,1)}), bf16[4,640,128]{2,1,0:T(8,128)(2,1)S(1)}, u32[]{:S(2)}, u32[]{:S(2)}) async-start(bf16[4,640,128]{2,1,0:T(8,128)(2,1)} %copy-done.1), calls=%async_computation.3 | async-start | bytes 1310720 | tf_op jit(solution)/shard_map/all_to_all | solution.py:264
  115.3 0.0 copy-done.7
  115.3 2.7 %shard_map.89 = bf16[128,2560]{1,0:T(8,128)(2,1)} custom-call(bf16[128,2560]{1,0:T(8,128)(2,1)S(1)} %copy-done, bf16[128,128]{1,0:T(8,128)(2,1)S(1)} %copy-done.3, bf16[128,128]{1,0:T(8,128)(2,1)S(1)} %copy-done.7, f32[40,128]{1,0:T(8,128)S(1)} %bitcast.13, bf16[32,16,640]{2,1,0:T(8,128)(2,1)S(1)} %all-to-all-done.2.enter_ref), custom_call_target="tpu_custom_call" | custom-call | tf_op jit(solution)/shard_map/pallas_call | solution.py:265
  118.0 0.7 slice.21.after_ref
  118.7 5.4 %all-to-all-done.3.in_ref = bf16[4,640,128]{2,1,0:T(8,128)(2,1)S(1)} async-done(((bf16[4,640,128]{2,1,0:T(8,128)(2,1)}), bf16[4,640,128]{2,1,0:T(8,128)(2,1)S(1)}, u32[]{:S(2)}, u32[]{:S(2)}) %all-to-all-start.3) | async-done | bytes 655392 | tf_op jit(solution)/shard_map/all_to_all | solution.py:264
  124.1 1.1 shard_map.91
  (2 shorter events, 0.1 us)
Async XLA Ops:
  0.6 1.1 copy-start.2
  1.7 0.9 copy-start.4
  2.6 0.9 copy-start.5
  4.6 4.4 %copy-start = (bf16[128,2560]{1,0:T(8,128)(2,1)S(1)}, bf16[128,2560]{1,0:T(8,128)(2,1)}, u32[]{:S(2)}) copy-start(bf16[128,2560]{1,0:T(8,128)(2,1)} %x_ref.3) | copy-start | bytes 1966084
  4.6 4.4 %copy-start.3 = (bf16[128,128]{1,0:T(8,128)(2,1)S(1)}, bf16[128,128]{1,0:T(8,128)(2,1)}, u32[]{:S(2)}) copy-start(bf16[128,128]{1,0:T(8,128)(2,1)} %in_ref.3) | copy-start | bytes 98308
  4.6 4.4 %copy-start.6 = (f32[128,40]{0,1:T(8,128)S(1)}, f32[128,40]{0,1:T(8,128)}, u32[]{:S(2)}) copy-start(f32[128,40]{0,1:T(8,128)} %param.10) | copy-start | bytes 61444
  4.6 17.1 %all-to-all-start.1 = ((bf16[4,800,128]{2,1,0:T(8,128)(2,1)}), bf16[4,800,128]{2,1,0:T(8,128)(2,1)S(1)}, u32[]{:S(2)}, u32[]{:S(2)}) async-start(bf16[4,800,128]{2,1,0:T(8,128)(2,1)} %shard_map.87), calls=%async_computation.1 | async-start | bytes 1638400 | tf_op jit(solution)/shard_map/all_to_all | solution.py:240
  21.7 44.4 %all-to-all-start = ((bf16[32,16,768]{2,1,0:T(8,128)(2,1)}), bf16[32,16,768]{2,1,0:T(8,128)(2,1)S(1)}, u32[]{:S(2)}, u32[]{:S(2)}) async-start(bf16[32,16,768]{2,1,0:T(8,128)(2,1)} %shard_map.86), calls=%async_computation | async-start | bytes 1572864 | tf_op jit(solution)/shard_map/all_to_all | solution.py:247
  67.9 43.0 %all-to-all-start.2 = ((bf16[32,16,640]{2,1,0:T(8,128)(2,1)}), bf16[32,16,640]{2,1,0:T(8,128)(2,1)S(1)}, u32[]{:S(2)}, u32[]{:S(2)}) async-start(bf16[32,16,640]{2,1,0:T(8,128)(2,1)} %shard_map.88.after_ref), calls=%async_computation.2 | async-start | bytes 1310720 | tf_op jit(solution)/shard_map/all_to_all | solution.py:251
  75.8 19.4 %collective-permute-start = (bf16[2,4,160,128]{3,2,1,0:T(8,128)(2,1)S(1)}, bf16[2,4,160,128]{3,2,1,0:T(8,128)(2,1)S(1)}, u32[]{:S(2)}, u32[]{:S(2)}) collective-permute-start(bf16[2,4,160,128]{3,2,1,0:T(8,128)(2,1)S(1)} %bitcast.15), channel_id=1, source_target_pairs={{0,1},{1,2},{2,3},{3,4},{4,5},{5,6},{6,7},{7,0},{8,9},{9,10},{10,1... | collective-permute-start | bytes 983048 | tf_op jit(solution)/shard_map/ppermute | solution.py:242
  79.5 15.7 %collective-permute-start.1 = (bf16[2,4,160,128]{3,2,1,0:T(8,128)(2,1)S(1)}, bf16[2,4,160,128]{3,2,1,0:T(8,128)(2,1)S(1)}, u32[]{:S(2)}, u32[]{:S(2)}) collective-permute-start(bf16[2,4,160,128]{3,2,1,0:T(8,128)(2,1)S(1)} %bitcast.14), channel_id=1, source_target_pairs={{0,7},{1,0},{2,1},{3,2},{4,3},{5,4},{6,5},{7,6},{8,15},{9,8},{10,9... | collective-permute-start | bytes 983048 | tf_op jit(solution)/shard_map/ppermute | solution.py:243
  110.0 0.8 copy-start.1
  110.9 4.4 %copy-start.7 = (bf16[128,128]{1,0:T(8,128)(2,1)S(1)}, bf16[128,128]{1,0:T(8,128)(2,1)}, u32[]{:S(2)}) copy-start(bf16[128,128]{1,0:T(8,128)(2,1)} %map_ref.1) | copy-start | bytes 98308
  110.9 13.2 %all-to-all-start.3 = ((bf16[4,640,128]{2,1,0:T(8,128)(2,1)}), bf16[4,640,128]{2,1,0:T(8,128)(2,1)S(1)}, u32[]{:S(2)}, u32[]{:S(2)}) async-start(bf16[4,640,128]{2,1,0:T(8,128)(2,1)} %copy-done.1), calls=%async_computation.3 | async-start | bytes 1310720 | tf_op jit(solution)/shard_map/all_to_all | solution.py:264

commit v4 on v2

--- a/solution.py
+++ b/solution.py
@@ -56,10 +56,16 @@
     rows = lax.broadcasted_iota(jnp.int32, (T, T), 0)
     cols = lax.broadcasted_iota(jnp.int32, (T, T), 1)
     lower = jnp.where(cols <= rows, 1.0, 0.0).astype(F32)
-    return jnp.dot(lower, decay, precision=lax.Precision.HIGHEST, preferred_element_type=F32)
-
-
-def update_kernel(x_ref, in_ref, decay_ref, after_ref, out_ref):
+    return lax.dot_general(
+        lower,
+        decay,
+        (((1,), (1,)), ((), ())),
+        precision=lax.Precision.HIGHEST,
+        preferred_element_type=F32,
+    )
+
+
+def update_kernel(x_ref, in_ref, decay_ref, out_ref):
     cumulative = cumulative_of(decay_ref[...])
     last = cumulative[T - 1 : T, :]
     onehot = head_spread()
@@ -124,38 +130,56 @@
 KEYS = 512
 
 
-def pack_kernel(q_ref, k_ref, v_ref, out_ref):
-    pad = jnp.zeros((T, 384 - KVH * DH), F32)
-    k = jnp.concatenate([k_ref[...].astype(F32), pad], axis=1).T.astype(BF16)
-    v = jnp.concatenate([v_ref[...].astype(F32), pad], axis=1).T.astype(BF16)
-    for g in range(KVH):
-        q = q_ref[:, g * GDH : (g + 1) * GDH].astype(F32)
-        out_ref[g, :GDH, :] = q.T.astype(BF16)
-        out_ref[g, GDH : GDH + DH, :] = k[g * DH : (g + 1) * DH, :]
-        out_ref[g, GDH + DH :, :] = v[g * DH : (g + 1) * DH, :]
-
-
-def attend_kernel(place_ref, q_ref, kv_ref, after_ref, out_ref, kv_buf, k_buf, v_buf, q_buf, sems):
-    copies = [
-        pltpu.make_async_copy(kv_ref.at[:, c], kv_buf.at[c], sems.at[c]) for c in range(NX)
+def pack_kernel(place_ref, q_ref, k_ref, v_ref, *out_refs):
+    for step, out_ref in enumerate(out_refs):
+        g = (place_ref[0] + step) % NX
+        q = q_ref[:, pl.ds(pl.multiple_of(g * GDH, 128), GDH)].astype(F32)
+        head = pl.ds(pl.multiple_of(g * DH, 16), DH)
+        out_ref[:GDH, :] = q.T.astype(BF16)
+        out_ref[GDH : GDH + DH, :] = k_ref[head, :]
+        out_ref[GDH + DH :, :] = v_ref[head, :]
+
+
+def merge_kernel(*refs):
+    for s in range(NX):
+        refs[NX][s] = refs[s][GDH:, :]
+
+
+def attend_kernel(place_ref, *refs):
+    packs = refs[:NX]
+    kv_ref, after_ref, out_ref, q_all, kv_buf, k_buf, v_buf, q_buf, q_sems, kv_sems = refs[NX:]
+    x = place_ref[0]
+    z = place_ref[1]
+    q_copies = [
+        pltpu.make_async_copy(
+            packs[s].at[pl.ds(0, GDH)], q_all.at[lax.rem(x + (NX - s), NX)], q_sems.at[s]
+        )
+        for s in range(NX)
     ]
-    for copy in copies:
+    kv_copies = [
+        pltpu.make_async_copy(
+            kv_ref.at[:, lax.rem(x + (NX - c), NX)], kv_buf.at[c], kv_sems.at[c]
+        )
+        for c in range(NX)
+    ]
+    for copy in q_copies + kv_copies:
         copy.start()
-    z = place_ref[0]
     scale = math.log2(math.e) / math.sqrt(DH)
     row = lax.broadcasted_iota(jnp.int32, (KEYS, QUERIES), 0)
     col = lax.broadcasted_iota(jnp.int32, (KEYS, QUERIES), 1) % T
     ones = jnp.where(lax.broadcasted_iota(jnp.int32, (16, CHUNK), 0) == 0, 1.0, 0.0).astype(BF16)
     blank = jnp.zeros((128 - DH, T), F32)
     blank_q = jnp.zeros((128 - DH, QUERIES), BF16)
+    for copy in q_copies:
+        copy.wait()
     for c in range(NX):
         q_buf[DH:128, :] = blank_q
         q_buf[128 + DH :, :] = blank_q
         for h in range(GROUP):
-            hi, lo = split2(q_ref[c, h * DH : (h + 1) * DH, :].astype(F32) * scale)
+            hi, lo = split2(q_all[c, h * DH : (h + 1) * DH, :].astype(F32) * scale)
             q_buf[:DH, h * T : (h + 1) * T] = hi
             q_buf[128 : 128 + DH, h * T : (h + 1) * T] = lo
-        copies[c].wait()
+        kv_copies[c].wait()
         v_buf[DH:, c * CHUNK : (c + 1) * CHUNK] = ones
         for b in range(NZ):
             at = slice(c * CHUNK + b * T, c * CHUNK + (b + 1) * T)
@@ -213,17 +237,24 @@
 
 
 def per_device(mixer_input, input_map, output_map, log_decay, query_rows, key_rows, value_rows):
-    place_z = lax.axis_index("cz").astype(jnp.int32).reshape(1)
-    place = (lax.axis_index("cx") * NZ + lax.axis_index("cz")).astype(jnp.int32).reshape(1)
-    packed = call(pack_kernel, (KVH, GDH + 2 * DH, T), [VMEM_SPEC] * 3)(
-        query_rows, key_rows, value_rows
-    )
-    packed = lax.all_to_all(packed, "cx", 0, 0)
-    kv_part = packed[:, GDH:, :]
-    kv = lax.all_gather(kv_part, "cz")
+    x = lax.axis_index("cx").astype(jnp.int32)
+    z = lax.axis_index("cz").astype(jnp.int32)
+    place_xz = jnp.stack([x, z])
+    place = (x * NZ + z).reshape(1)
+    packs = pl.pallas_call(
+        pack_kernel,
+        out_shape=[jax.ShapeDtypeStruct((GDH + 2 * DH, T), BF16)] * NX,
+        in_specs=[SMEM_SPEC] + [VMEM_SPEC] * 3,
+        out_specs=[VMEM_SPEC] * NX,
+    )(place_xz, query_rows, key_rows.T, value_rows.T)
+    packs = [packs[0]] + [
+        lax.ppermute(packs[s], "cx", [(k, (k + s) % NX) for k in range(NX)])
+        for s in range(1, NX)
+    ]
+    kv = lax.all_gather(call(merge_kernel, (NX, 2 * DH, T), [VMEM_SPEC] * NX)(*packs), "cz")
     update = call(
-        update_kernel, (NCTX, PIECE_ROWS, PIECE_COLS + 128), [VMEM_SPEC] * 3 + [ANY_SPEC]
-    )(mixer_input, input_map, log_decay, packed)
+        update_kernel, (NCTX, PIECE_ROWS, PIECE_COLS + 128), [VMEM_SPEC] * 3
+    )(mixer_input, input_map, log_decay.T)
     update = lax.all_to_all(update, ("cx", "cz"), 0, 0)
     prefix = call(prefix_kernel, (NCTX, PIECE_ROWS, PIECE_COLS), [SMEM_SPEC, VMEM_SPEC])(
         place, update
@@ -232,18 +263,20 @@
     attended = call(
         attend_kernel,
         (NX, GDH, T),
-        [SMEM_SPEC, VMEM_SPEC, ANY_SPEC, ANY_SPEC],
+        [SMEM_SPEC] + [ANY_SPEC] * (NX + 2),
         [
+            pltpu.VMEM((NX, GDH, T), BF16),
             pltpu.VMEM((NX, NZ, 2 * DH, T), BF16),
             pltpu.VMEM((NX * CHUNK, 256), BF16),
             pltpu.VMEM((DH + 16, NX * CHUNK), BF16),
             pltpu.VMEM((256, QUERIES), BF16),
             pltpu.SemaphoreType.DMA((NX,)),
+            pltpu.SemaphoreType.DMA((NX,)),
         ],
-    )(place_z, packed, kv, prefix)
+    )(place_xz, *packs, kv, prefix)
     attended = lax.all_to_all(attended, "cx", 0, 0)
     mixer_output = call(mix_kernel, (T, WIDTH), [VMEM_SPEC] * 5)(
-        mixer_input, input_map, output_map, log_decay, entering
+        mixer_input, input_map, output_map, log_decay.T, entering
     )
     attention_output = call(place_kernel, (T, QH * DH), [VMEM_SPEC, VMEM_SPEC])(
         attended, mixer_output[:16, :128]

time: 134 us -> 139 us (1.037)
  starting transfers between devices: 25 us -> 38.8 us
  waiting for transfers between devices: 64.2 us -> 51.8 us
  Pallas kernels: 24.1 us -> 27.3 us
    all_to_all x1, waiting for transfers between devices: 21.1 us -> 0.01 us  [per_device(): update = lax.all_to_all(update, ('cx', 'cz'), 0, 0)]
    all_to_all x1 -> x0, waiting for transfers between devices: 12.5 us -> none  [per_device(): packed = lax.all_to_all(packed, 'cx', 0, 0)]
    ppermute x0 -> x3, starting transfers between devices: none -> 11.6 us  [per_device(): lax.ppermute(packs[s], 'cx', [(k, (k + s) % NX) for k in range(NX)])]
    all_gather x1, waiting for transfers between devices: 25.3 us -> 36.8 us  [per_device(): lax.all_gather(call(merge_kernel, (NX, 2 * DH, T), [VMEM_SPEC] * NX)(*pac...]
    ppermute x0 -> x3, waiting for transfers between devices: none -> 9.63 us  [per_device(): lax.ppermute(packs[s], 'cx', [(k, (k + s) % NX) for k in range(NX)])]
    all_to_all x1 -> x0, starting transfers between devices: 4.29 us -> none  [per_device(): packed = lax.all_to_all(packed, 'cx', 0, 0)]
    all_to_all x1, starting transfers between devices: 5.06 us -> 8.99 us  [per_device(): entering = lax.all_to_all(prefix, ('cx', 'cz'), 0, 0)]
    pallas_call x3 -> x4, Pallas kernels: 18.5 us -> 21.6 us  [the longest x1 16.6 us: per_device(): call(attend_kernel, (NX, GDH, T), [SMEM_SPEC] + [ANY_SPEC] * (NX + 2), [p...]
  transfers between devices with their start and end apart: 5 -> 7, of which waited for: 4 -> 4; matrix products, arithmetic and copies ran while one was open for 1% -> 1% of each run, Pallas kernels for 15% -> 17%
where the time goes in v4:
time: 139 us; the launch traced here: 138 us
  waiting for transfers between devices  51.8 us (37%)
  starting transfers between devices  38.8 us (28%)
  Pallas kernels  27.3 us (20%)
  between operations  14.2 us (10%)
  local copies, waits for them, and re-layouts  5.54 us (4%)
    all_gather x1, waiting for transfers between devices, per_device(): lax.all_gather(call(merge_kernel, (NX, 2 * DH, T), [VMEM_SPEC] * NX)(*pac...  36.8 us
    pallas_call x1, Pallas kernels, per_device(): call(attend_kernel, (NX, GDH, T), [SMEM_SPEC] + [ANY_SPEC] * (NX + 2), [p...  16.6 us
    all_to_all x1, starting transfers between devices, per_device(): update = lax.all_to_all(update, ('cx', 'cz'), 0, 0)  13.2 us
    ppermute x3, starting transfers between devices, per_device(): lax.ppermute(packs[s], 'cx', [(k, (k + s) % NX) for k in range(NX)])  11.6 us
    ppermute x3, waiting for transfers between devices, per_device(): lax.ppermute(packs[s], 'cx', [(k, (k + s) % NX) for k in range(NX)])  9.63 us
    all_to_all x1, starting transfers between devices, per_device(): entering = lax.all_to_all(prefix, ('cx', 'cz'), 0, 0)  8.99 us
    all_to_all x1, waiting for transfers between devices, per_device(): attended = lax.all_to_all(attended, 'cx', 0, 0)  5.34 us
    all_to_all x1, starting transfers between devices, per_device(): attended = lax.all_to_all(attended, 'cx', 0, 0)  4.96 us
  transfers between devices with their start and end apart: 7, of which 4 were waited for; matrix products, arithmetic and copies ran while one was open for 1% of the time, Pallas kernels for 17%

profile of v4, /device:TPU:56, one launch (start us, length us, event | category | flops | bytes accessed | tf_op | source)
XLA Modules:
  0.0 138.2 jit_solution(636996856100383865)
XLA Ops:
  7.2 0.0 copy-start
  7.2 1.1 copy-done
  8.3 0.0 copy-start.5
  8.3 0.8 copy-done.5
  9.0 0.0 copy-start.7
  9.0 0.7 copy-done.7
  9.7 2.2 %shard_map.86 = bf16[32,16,768]{2,1,0:T(8,128)(2,1)} custom-call(bf16[128,2560]{1,0:T(8,128)(2,1)S(1)} %copy-done, bf16[128,128]{1,0:T(8,128)(2,1)S(1)} %copy-done.5, f32[40,128]{1,0:T(8,128)S(1)} %bitcast.8), custom_call_target="tpu_custom_call" | custom-call | tf_op jit(solution)/shard_map/pallas_call | solution.py:255
  11.9 13.2 %all-to-all-start = ((bf16[32,16,768]{2,1,0:T(8,128)(2,1)}), bf16[32,16,768]{2,1,0:T(8,128)(2,1)S(1)}, u32[]{:S(2)}, u32[]{:S(2)}) async-start(bf16[32,16,768]{2,1,0:T(8,128)(2,1)} %shard_map.86), calls=%async_computation | async-start | bytes 1572864 | tf_op jit(solution)/shard_map/all_to_all | solution.py:258
  25.1 0.0 all-gather.3.cloned.1.call-start
  25.2 0.6 pad_add_fusion.place_ref
  25.7 2.2 %shard_map.89 = (bf16[800,128]{1,0:T(8,128)(2,1)}, bf16[800,128]{1,0:T(8,128)(2,1)}, bf16[800,128]{1,0:T(8,128)(2,1)}, bf16[800,128]{1,0:T(8,128)(2,1)}) custom-call(s32[2]{0:T(128)} %pad_add_fusion.place_ref, bf16[128,2560]{1,0:T(8,128)(2,1)} %q_ref.1, bf16[320,128]{1,0:T(8,128)(2,1)} %bitcast.10, bf16[320,128]{1,0:T(8,128)(2,1)} %bitcast.11), custom_call_target="tpu_custom_call" | custom-call | tf_op jit(solution)/shard_map/pallas_call | solution.py:244
  27.9 3.7 %collective-permute-start = (bf16[800,128]{1,0:T(8,128)(2,1)}, bf16[800,128]{1,0:T(8,128)(2,1)S(1)}, u32[]{:S(2)}, u32[]{:S(2)}) collective-permute-start(bf16[800,128]{1,0:T(8,128)(2,1)} %get-tuple-element.7), channel_id=1, source_target_pairs={{0,8},{8,16},{16,24},{24,0},{1,9},{9,17},{17,25},{25,1},{2,10},{10... | collective-permute-start | bytes 614408 | tf_op jit(solution)/shard_map/ppermute | solution.py:251
  31.6 4.6 %collective-permute-start.1 = (bf16[800,128]{1,0:T(8,128)(2,1)}, bf16[800,128]{1,0:T(8,128)(2,1)S(1)}, u32[]{:S(2)}, u32[]{:S(2)}) collective-permute-start(bf16[800,128]{1,0:T(8,128)(2,1)} %get-tuple-element.8), channel_id=1, source_target_pairs={{0,16},{8,24},{16,0},{24,8},{1,17},{9,25},{17,1},{25,9},{2,18},{10... | collective-permute-start | bytes 614408 | tf_op jit(solution)/shard_map/ppermute | solution.py:251
  36.2 3.3 %collective-permute-start.2 = (bf16[800,128]{1,0:T(8,128)(2,1)}, bf16[800,128]{1,0:T(8,128)(2,1)S(1)}, u32[]{:S(2)}, u32[]{:S(2)}) collective-permute-start(bf16[800,128]{1,0:T(8,128)(2,1)} %get-tuple-element.9), channel_id=1, source_target_pairs={{0,24},{8,0},{16,8},{24,16},{1,25},{9,1},{17,9},{25,17},{2,26},{10... | collective-permute-start | bytes 614408 | tf_op jit(solution)/shard_map/ppermute | solution.py:251
  39.6 2.1 %collective-permute-done.refs_1_ = bf16[800,128]{1,0:T(8,128)(2,1)S(1)} collective-permute-done((bf16[800,128]{1,0:T(8,128)(2,1)}, bf16[800,128]{1,0:T(8,128)(2,1)S(1)}, u32[]{:S(2)}, u32[]{:S(2)}) %collective-permute-start) | collective-permute-done | bytes 204832 | tf_op jit(solution)/shard_map/ppermute | solution.py:251
  41.7 7.5 %collective-permute-done.1.refs_2_ = bf16[800,128]{1,0:T(8,128)(2,1)S(1)} collective-permute-done((bf16[800,128]{1,0:T(8,128)(2,1)}, bf16[800,128]{1,0:T(8,128)(2,1)S(1)}, u32[]{:S(2)}, u32[]{:S(2)}) %collective-permute-start.1) | collective-permute-done | bytes 204832 | tf_op jit(solution)/shard_map/ppermute | solution.py:251
  49.2 0.0 collective-permute-done.2.refs_3_
  49.2 0.0 copy-start.3
  49.2 0.9 copy-done.3
  50.1 0.7 shard_map.90
  50.8 0.0 all-gather.3.cloned.1.call-update
  50.9 0.0 all-to-all-done.in_ref
  50.9 0.0 copy-start.4
  50.9 0.0 copy-start.10
  50.9 1.8 %shard_map.87.refs_5_ = bf16[32,16,640]{2,1,0:T(8,128)(2,1)} custom-call(s32[1]{0:T(128)} %bitcast.1.place_ref, bf16[32,16,768]{2,1,0:T(8,128)(2,1)S(1)} %all-to-all-done.in_ref), custom_call_target="tpu_custom_call" | custom-call | tf_op jit(solution)/shard_map/pallas_call | solution.py:259
  52.7 9.0 %all-to-all-start.1 = ((bf16[32,16,640]{2,1,0:T(8,128)(2,1)}), bf16[32,16,640]{2,1,0:T(8,128)(2,1)S(1)}, u32[]{:S(2)}, u32[]{:S(2)}) async-start(bf16[32,16,640]{2,1,0:T(8,128)(2,1)} %shard_map.87.refs_5_), calls=%async_computation.1 | async-start | bytes 1310720 | tf_op jit(solution)/shard_map/all_to_all | solution.py:262
  61.7 36.8 %all-gather.3.cloned.1.call-done = bf16[32,160,128]{2,1,0:T(8,128)(2,1)} async-done(((bf16[4,160,128]{2,1,0:T(8,128)(2,1)}), bf16[32,160,128]{2,1,0:T(8,128)(2,1)}) %all-gather.3.cloned.1.call-update) | async-done | bytes 1310736 | tf_op jit(solution)/shard_map/all_gather | solution.py:254
  98.5 0.0 copy-done.4
  98.6 0.0 copy-done.10
  98.6 0.0 copy-start.2
  98.6 1.3 copy-done.2
  99.9 16.6 %shard_map.91 = bf16[4,640,128]{2,1,0:T(8,128)(2,1)} custom-call(s32[2]{0:T(128)S(1)} %copy-done.10, bf16[800,128]{1,0:T(8,128)(2,1)S(1)} %copy-done.4, bf16[800,128]{1,0:T(8,128)(2,1)S(1)} %collective-permute-done.refs_1_, bf16[800,128]{1,0:T(8,128)(2,1)S(1)} %collective-permute-done.1.refs_2_, bf16[800,128]{1,0:T(8,128)(2,1)S(1)} %collective-permute-done.2.refs_3_, ...), custom_call_target="tpu_custom_call" | custom-call | tf_op jit(solution)/shard_map/pallas_call | solution.py:263
  116.5 0.0 copy-start.1
  116.5 0.0 copy-start.6
  116.5 0.0 copy-start.8
  116.5 0.0 copy-start.9
  116.5 0.0 all-to-all-done.1.enter_ref
  116.5 5.0 %all-to-all-start.2 = ((bf16[4,640,128]{2,1,0:T(8,128)(2,1)}), bf16[4,640,128]{2,1,0:T(8,128)(2,1)S(1)}, u32[]{:S(2)}, u32[]{:S(2)}) async-start(bf16[4,640,128]{2,1,0:T(8,128)(2,1)} %shard_map.91), calls=%async_computation.2 | async-start | bytes 1310720 | tf_op jit(solution)/shard_map/all_to_all | solution.py:277
  121.5 0.0 copy-done.1
  121.5 0.0 copy-done.6
  121.5 0.0 copy-done.8
  121.5 0.0 copy-done.9
  121.5 2.7 %shard_map.88 = bf16[128,2560]{1,0:T(8,128)(2,1)} custom-call(bf16[128,2560]{1,0:T(8,128)(2,1)S(1)} %copy-done.1, bf16[128,128]{1,0:T(8,128)(2,1)S(1)} %copy-done.6, bf16[128,128]{1,0:T(8,128)(2,1)S(1)} %copy-done.9, f32[40,128]{1,0:T(8,128)S(1)} %bitcast.9, bf16[32,16,640]{2,1,0:T(8,128)(2,1)S(1)} %all-to-all-done.1.enter_ref), custom_call_target="tpu_custom_call" | custom-call | tf_op jit(solution)/shard_map/pallas_call | solution.py:278
  124.2 0.7 slice.4.after_ref
  124.9 5.3 %all-to-all-done.2.in_ref = bf16[4,640,128]{2,1,0:T(8,128)(2,1)S(1)} async-done(((bf16[4,640,128]{2,1,0:T(8,128)(2,1)}), bf16[4,640,128]{2,1,0:T(8,128)(2,1)S(1)}, u32[]{:S(2)}, u32[]{:S(2)}) %all-to-all-start.2) | async-done | bytes 655392 | tf_op jit(solution)/shard_map/all_to_all | solution.py:277
  130.3 1.1 shard_map.92
Async XLA Ops:
  7.2 1.1 copy-start
  8.3 0.8 copy-start.5
  9.0 0.7 copy-start.7
  11.9 38.9 %all-to-all-start = ((bf16[32,16,768]{2,1,0:T(8,128)(2,1)}), bf16[32,16,768]{2,1,0:T(8,128)(2,1)S(1)}, u32[]{:S(2)}, u32[]{:S(2)}) async-start(bf16[32,16,768]{2,1,0:T(8,128)(2,1)} %shard_map.86), calls=%async_computation | async-start | bytes 1572864 | tf_op jit(solution)/shard_map/all_to_all | solution.py:258
  25.1 73.4 %all-gather.3.cloned.1.call-start = ((), (), s32[]{:S(2)}) async-start(), calls=%async_computation.3 | async-start | bytes 1474560 | tf_op jit(solution)/shard_map/all_gather | solution.py:254
  27.9 13.8 %collective-permute-start = (bf16[800,128]{1,0:T(8,128)(2,1)}, bf16[800,128]{1,0:T(8,128)(2,1)S(1)}, u32[]{:S(2)}, u32[]{:S(2)}) collective-permute-start(bf16[800,128]{1,0:T(8,128)(2,1)} %get-tuple-element.7), channel_id=1, source_target_pairs={{0,8},{8,16},{16,24},{24,0},{1,9},{9,17},{17,25},{25,1},{2,10},{10... | collective-permute-start | bytes 614408 | tf_op jit(solution)/shard_map/ppermute | solution.py:251
  31.6 17.6 %collective-permute-start.1 = (bf16[800,128]{1,0:T(8,128)(2,1)}, bf16[800,128]{1,0:T(8,128)(2,1)S(1)}, u32[]{:S(2)}, u32[]{:S(2)}) collective-permute-start(bf16[800,128]{1,0:T(8,128)(2,1)} %get-tuple-element.8), channel_id=1, source_target_pairs={{0,16},{8,24},{16,0},{24,8},{1,17},{9,25},{17,1},{25,9},{2,18},{10... | collective-permute-start | bytes 614408 | tf_op jit(solution)/shard_map/ppermute | solution.py:251
  36.2 13.0 %collective-permute-start.2 = (bf16[800,128]{1,0:T(8,128)(2,1)}, bf16[800,128]{1,0:T(8,128)(2,1)S(1)}, u32[]{:S(2)}, u32[]{:S(2)}) collective-permute-start(bf16[800,128]{1,0:T(8,128)(2,1)} %get-tuple-element.9), channel_id=1, source_target_pairs={{0,24},{8,0},{16,8},{24,16},{1,25},{9,1},{17,9},{25,17},{2,26},{10... | collective-permute-start | bytes 614408 | tf_op jit(solution)/shard_map/ppermute | solution.py:251
  49.2 0.9 copy-start.3
  50.9 47.7 %copy-start.4 = (bf16[800,128]{1,0:T(8,128)(2,1)S(1)}, bf16[800,128]{1,0:T(8,128)(2,1)}, u32[]{:S(2)}) copy-start(bf16[800,128]{1,0:T(8,128)(2,1)} %get-tuple-element.6.refs_0_) | copy-start | bytes 614404
  50.9 47.7 %copy-start.10 = (s32[2]{0:T(128)S(1)}, s32[2]{0:T(128)}, u32[]{:S(2)}) copy-start(s32[2]{0:T(128)} %pad_add_fusion.place_ref) | copy-start | bytes 28
  52.7 63.8 %all-to-all-start.1 = ((bf16[32,16,640]{2,1,0:T(8,128)(2,1)}), bf16[32,16,640]{2,1,0:T(8,128)(2,1)S(1)}, u32[]{:S(2)}, u32[]{:S(2)}) async-start(bf16[32,16,640]{2,1,0:T(8,128)(2,1)} %shard_map.87.refs_5_), calls=%async_computation.1 | async-start | bytes 1310720 | tf_op jit(solution)/shard_map/all_to_all | solution.py:262
  98.6 1.3 copy-start.2
  116.5 5.0 %copy-start.1 = (bf16[128,2560]{1,0:T(8,128)(2,1)S(1)}, bf16[128,2560]{1,0:T(8,128)(2,1)}, u32[]{:S(2)}) copy-start(bf16[128,2560]{1,0:T(8,128)(2,1)} %x_ref.3) | copy-start | bytes 1966084
  116.5 5.0 %copy-start.6 = (bf16[128,128]{1,0:T(8,128)(2,1)S(1)}, bf16[128,128]{1,0:T(8,128)(2,1)}, u32[]{:S(2)}) copy-start(bf16[128,128]{1,0:T(8,128)(2,1)} %in_ref.3) | copy-start | bytes 98308
  116.5 5.0 %copy-start.8 = (f32[128,40]{0,1:T(8,128)S(1)}, f32[128,40]{0,1:T(8,128)}, u32[]{:S(2)}) copy-start(f32[128,40]{0,1:T(8,128)} %param.10) | copy-start | bytes 61444
  116.5 5.0 %copy-start.9 = (bf16[128,128]{1,0:T(8,128)(2,1)S(1)}, bf16[128,128]{1,0:T(8,128)(2,1)}, u32[]{:S(2)}) copy-start(bf16[128,128]{1,0:T(8,128)(2,1)} %map_ref.1) | copy-start | bytes 98308
  116.5 13.7 %all-to-all-start.2 = ((bf16[4,640,128]{2,1,0:T(8,128)(2,1)}), bf16[4,640,128]{2,1,0:T(8,128)(2,1)S(1)}, u32[]{:S(2)}, u32[]{:S(2)}) async-start(bf16[4,640,128]{2,1,0:T(8,128)(2,1)} %shard_map.91), calls=%async_computation.2 | async-start | bytes 1310720 | tf_op jit(solution)/shard_map/all_to_all | solution.py:277
Sparse Core Ops, SparseCore 0:
  51.0 47.5 all-gather.2

commit v5 on v3

--- a/solution.py
+++ b/solution.py
@@ -66,7 +66,7 @@
     )
 
 
-def update_kernel(x_ref, in_ref, decay_ref, out_ref):
+def update_kernel(x_ref, in_ref, decay_ref, after_ref, out_ref):
     cumulative = cumulative_of(decay_ref[...])
     last = cumulative[T - 1 : T, :]
     onehot = head_spread()
@@ -90,7 +90,7 @@
             out_ref[d, :, PIECE_COLS:] = factor
 
 
-def prefix_kernel(place_ref, in_ref, after_ref, out_ref):
+def prefix_kernel(place_ref, in_ref, after_ref, below_ref, above_ref, out_ref):
     first_head = (place_ref[0] % (WIDTH // PIECE_COLS)) * (PIECE_COLS // P_SIZE)
     lane = lax.broadcasted_iota(jnp.int32, (128, PIECE_COLS), 0)
     cols = lax.broadcasted_iota(jnp.int32, (128, PIECE_COLS), 1)
@@ -126,9 +126,8 @@
         out_ref[:, cut] = (ahead[:, cut] * (inner[:, cut] + start[:, cut] * carried)).astype(BF16)
 
 
-CHUNK = NZ * T
 QUERIES = GROUP * T
-KEYS = 512
+KEYS = NH * T
 
 
 def pack_kernel(q_ref, k_ref, v_ref, out_ref):
@@ -139,31 +138,13 @@
         out_ref[g, GDH + DH :, :] = v_ref[g * DH : (g + 1) * DH, :]
 
 
-def attend_kernel(
-    place_ref, q_ref, same_ref, below_ref, above_ref, after_ref, out_ref, kv_buf, k_buf, v_buf, q_buf, sems
-):
+def attend(place_ref, q_ref, block, parity, k_buf, v_buf, q_buf, begin, end):
     z = place_ref[0]
-    parity = z % 2
-    half = NH // 2
-    copies = []
-    for c in range(NX):
-        copies.append(
-            [
-                pltpu.make_async_copy(same_ref.at[:, c], kv_buf.at[c, :, parity], sems.at[c, 0]),
-                pltpu.make_async_copy(
-                    below_ref.at[:, c], kv_buf.at[c, pl.ds(0, half), 1 - parity], sems.at[c, 1]
-                ),
-                pltpu.make_async_copy(
-                    above_ref.at[:, c], kv_buf.at[c, pl.ds(half, half), 1 - parity], sems.at[c, 2]
-                ),
-            ]
-        )
-        for copy in copies[c]:
-            copy.start()
     scale = math.log2(math.e) / math.sqrt(DH)
     row = lax.broadcasted_iota(jnp.int32, (KEYS, QUERIES), 0)
+    row = row + row // T * T + parity * T
     col = lax.broadcasted_iota(jnp.int32, (KEYS, QUERIES), 1) % T
-    ones = jnp.where(lax.broadcasted_iota(jnp.int32, (16, CHUNK), 0) == 0, 1.0, 0.0).astype(BF16)
+    ones = jnp.where(lax.broadcasted_iota(jnp.int32, (16, KEYS), 0) == 0, 1.0, 0.0).astype(BF16)
     blank = jnp.zeros((128 - DH, T), F32)
     blank_q = jnp.zeros((128 - DH, QUERIES), BF16)
     for c in range(NX):
@@ -173,42 +154,75 @@
             hi, lo = split2(q_ref[c, h * DH : (h + 1) * DH, :].astype(F32) * scale)
             q_buf[:DH, h * T : (h + 1) * T] = hi
             q_buf[128 : 128 + DH, h * T : (h + 1) * T] = lo
-        for copy in copies[c]:
-            copy.wait()
-        v_buf[DH:, c * CHUNK : (c + 1) * CHUNK] = ones
-        for b in range(NZ):
-            at = slice(c * CHUNK + b * T, c * CHUNK + (b + 1) * T)
-            v_buf[:DH, at] = kv_buf[c, b // 2, b % 2, DH:, :]
-            k = jnp.concatenate([kv_buf[c, b // 2, b % 2, :DH, :].astype(F32), blank], axis=0).T.astype(BF16)
+        v_buf[DH:, c * KEYS : (c + 1) * KEYS] = ones
+        for i in range(NH):
+            at = slice(c * KEYS + i * T, c * KEYS + (i + 1) * T)
+            kv = block(c, i)
+            v_buf[:DH, at] = kv[DH:, :]
+            k = jnp.concatenate([kv[:DH, :].astype(F32), blank], axis=0).T.astype(BF16)
             k_buf[at, :128] = k
             k_buf[at, 128:] = k
         q = q_buf[...]
 
         def scores(j, c=c, q=q):
             found = dot(k_buf[j * KEYS : (j + 1) * KEYS, :], q)
-            if j * KEYS >= c * CHUNK:
-                seen = row + (j * KEYS - c * CHUNK) <= col + z * T
-                found = jnp.where(seen, found, masked_score)
+            if j == c:
+                found = jnp.where(row <= col + z * T, found, masked_score)
             return found
 
-        count = (c + 1) * CHUNK // KEYS
+        total, top = begin(c)
         found = scores(0)
-        top = jnp.max(found, axis=0, keepdims=True)
-        total = None
-        for j in range(count):
-            later = scores(j + 1) if j + 1 < count else None
+        for j in range(c + 1):
+            later = scores(j + 1) if j < c else None
+            highest = jnp.max(found, axis=0, keepdims=True)
+            if top is None:
+                top = highest
+            else:
+                raised = jnp.maximum(top, highest)
+                total = total * jnp.exp2(top - raised)
+                top = raised
             expos = jnp.exp2(found - top).astype(BF16)
             summed = dot(v_buf[:, j * KEYS : (j + 1) * KEYS], expos)
             total = summed if total is None else total + summed
-            if later is not None:
-                raised = jnp.maximum(top, jnp.max(later, axis=0, keepdims=True))
-                total = total * jnp.exp2(top - raised)
-                top = raised
-                found = later
+            found = later
+        end(c, total, top)
+
+
+def attend_same_kernel(place_ref, q_ref, same_ref, total_ref, top_ref, *bufs):
+    def end(c, total, top):
+        total_ref[c] = total
+        top_ref[c] = top
+
+    attend(
+        place_ref,
+        q_ref,
+        lambda c, i: same_ref[i, c],
+        place_ref[0] % 2,
+        *bufs,
+        lambda c: (None, None),
+        end,
+    )
+
+
+def attend_other_kernel(
+    place_ref, q_ref, below_ref, above_ref, total_ref, top_ref, after_ref, out_ref, *bufs
+):
+    def end(c, total, top):
         done = (total[:DH, :] / total[DH : DH + 1, :]).astype(BF16)
         for h in range(GROUP):
             out_ref[c, h * DH : (h + 1) * DH, :] = done[:, h * T : (h + 1) * T]
 
+    half = NH // 2
+    attend(
+        place_ref,
+        q_ref,
+        lambda c, i: below_ref[i, c] if i < half else above_ref[i - half, c],
+        1 - place_ref[0] % 2,
+        *bufs,
+        lambda c: (total_ref[c], top_ref[c]),
+        end,
+    )
+
 
 def place_kernel(in_ref, after_ref, out_ref):
     for g in range(KVH):
@@ -220,7 +234,7 @@
 ANY_SPEC = pl.BlockSpec(memory_space=pl.ANY)
 
 
-def call(kernel, shape, specs, scratch=(), limit=48):
+def call(kernel, shape, specs, scratch=(), limit=24):
     return pl.pallas_call(
         kernel,
         out_shape=jax.ShapeDtypeStruct(shape, BF16),
@@ -242,25 +256,34 @@
     below = lax.ppermute(same[: NH // 2], ("zh", "zl"), [(k, (k + 1) % NZ) for k in range(NZ)])
     above = lax.ppermute(same[NH // 2 :], ("zh", "zl"), [(k, (k - 1) % NZ) for k in range(NZ)])
     update = call(
-        update_kernel, (NCTX, PIECE_ROWS, PIECE_COLS + 128), [VMEM_SPEC] * 3
-    )(mixer_input, input_map, log_decay.T)
+        update_kernel, (NCTX, PIECE_ROWS, PIECE_COLS + 128), [VMEM_SPEC] * 3 + [ANY_SPEC]
+    )(mixer_input, input_map, log_decay.T, same)
     update = lax.all_to_all(update, ("cx", "zh", "zl"), 0, 0)
-    prefix = call(prefix_kernel, (NCTX, PIECE_ROWS, PIECE_COLS), [SMEM_SPEC, VMEM_SPEC, ANY_SPEC])(
-        place, update, same
-    )
+    bufs = [
+        pltpu.VMEM((NX * KEYS, 256), BF16),
+        pltpu.VMEM((DH + 16, NX * KEYS), BF16),
+        pltpu.VMEM((256, QUERIES), BF16),
+    ]
+    total, top = pl.pallas_call(
+        attend_same_kernel,
+        out_shape=[
+            jax.ShapeDtypeStruct((NX, DH + 16, QUERIES), F32),
+            jax.ShapeDtypeStruct((NX, 1, QUERIES), F32),
+        ],
+        in_specs=[SMEM_SPEC, VMEM_SPEC, VMEM_SPEC],
+        out_specs=[VMEM_SPEC, VMEM_SPEC],
+        scratch_shapes=bufs,
+        compiler_params=pltpu.CompilerParams(vmem_limit_bytes=24 << 20),
+    )(place_z, packed, same)
+    prefix = call(
+        prefix_kernel,
+        (NCTX, PIECE_ROWS, PIECE_COLS),
+        [SMEM_SPEC, VMEM_SPEC, VMEM_SPEC, ANY_SPEC, ANY_SPEC],
+    )(place, update, top, below, above)
     entering = lax.all_to_all(prefix, ("cx", "zh", "zl"), 0, 0)
     attended = call(
-        attend_kernel,
-        (NX, GDH, T),
-        [SMEM_SPEC, VMEM_SPEC] + [ANY_SPEC] * 4,
-        [
-            pltpu.VMEM((NX, NH, 2, 2 * DH, T), BF16),
-            pltpu.VMEM((NX * CHUNK, 256), BF16),
-            pltpu.VMEM((DH + 16, NX * CHUNK), BF16),
-            pltpu.VMEM((256, QUERIES), BF16),
-            pltpu.SemaphoreType.DMA((NX, 3)),
-        ],
-    )(place_z, packed, same, below, above, prefix)
+        attend_other_kernel, (NX, GDH, T), [SMEM_SPEC] + [VMEM_SPEC] * 5 + [ANY_SPEC], bufs
+    )(place_z, packed, below, above, total, top, prefix)
     attended = lax.all_to_all(attended, "cx", 0, 0)
     mixer_output = call(mix_kernel, (T, WIDTH), [VMEM_SPEC] * 5)(
         mixer_input, input_map, output_map, log_decay.T, entering

time: 126 us -> 118 us (0.937)
  starting transfers between devices: 35.1 us -> 23.5 us
  waiting for transfers between devices: 28.1 us -> 20.5 us
  blocking collectives: 33 us -> 40.5 us
  local copies, waits for them, and re-layouts: 4.44 us -> 7.02 us
    all_to_all x0 -> x1, blocking collectives: none -> 16.9 us  [per_device(): packed = lax.all_to_all(packed, 'cx', 0, 0)]
    all_to_all x1 -> x0, waiting for transfers between devices: 10.4 us -> none  [per_device(): packed = lax.all_to_all(packed, 'cx', 0, 0)]
    all_gather x1, blocking collectives: 33 us -> 23.6 us  [per_device(): same = lax.all_gather(packed[:, GDH:, :], 'zh')]
    all_to_all x1, waiting for transfers between devices: 0.01 us -> 7.35 us  [per_device(): entering = lax.all_to_all(prefix, ('cx', 'zh', 'zl'), 0, 0)]
    all_to_all x1, starting transfers between devices: 11.3 us -> 5.31 us  [per_device(): update = lax.all_to_all(update, ('cx', 'zh', 'zl'), 0, 0)]
    ppermute x1, waiting for transfers between devices: 12.3 us -> 7.89 us  [per_device(): lax.ppermute(same[:NH // 2], ('zh', 'zl'), [(k, (k + 1) % NZ) for k in ra...]
    all_to_all x1 -> x0, starting transfers between devices: 4.42 us -> none  [per_device(): packed = lax.all_to_all(packed, 'cx', 0, 0)]
    pallas_call x2 -> x3, Pallas kernels: 17 us -> 18.9 us  [the longest x1 9.77 us: per_device(): call(attend_other_kernel, (NX, GDH, T), [SMEM_SPEC] + [VMEM_SPEC] * 5 + [...]
  transfers between devices with their start and end apart: 6 -> 5, of which waited for: 3 -> 3; matrix products, arithmetic and copies ran while one was open for 1% -> 1% of each run, Pallas kernels for 16% -> 17%
where the time goes in v5:
time: 118 us; the launch traced here: 117 us
  blocking collectives  40.5 us (34%)
  Pallas kernels  24.8 us (21%)
  starting transfers between devices  23.5 us (20%)
  waiting for transfers between devices  20.5 us (17%)
  local copies, waits for them, and re-layouts  7.02 us (6%)
    all_gather x1, blocking collectives, per_device(): same = lax.all_gather(packed[:, GDH:, :], 'zh')  23.6 us
    all_to_all x1, blocking collectives, per_device(): packed = lax.all_to_all(packed, 'cx', 0, 0)  16.9 us
    pallas_call x1, Pallas kernels, per_device(): call(attend_other_kernel, (NX, GDH, T), [SMEM_SPEC] + [VMEM_SPEC] * 5 + [...  9.77 us
    ppermute x1, waiting for transfers between devices, per_device(): lax.ppermute(same[:NH // 2], ('zh', 'zl'), [(k, (k + 1) % NZ) for k in ra...  7.89 us
    all_to_all x1, starting transfers between devices, per_device(): entering = lax.all_to_all(prefix, ('cx', 'zh', 'zl'), 0, 0)  7.63 us
    all_to_all x1, waiting for transfers between devices, per_device(): entering = lax.all_to_all(prefix, ('cx', 'zh', 'zl'), 0, 0)  7.35 us
    pallas_call x1, Pallas kernels, per_device(): pl.pallas_call(attend_same_kernel, out_shape=[jax.ShapeDtypeStruct((NX, D...  6.98 us
    unnamed x18, local copies, waits for them, and re-layouts  5.44 us
  transfers between devices with their start and end apart: 5, of which 3 were waited for; matrix products, arithmetic and copies ran while one was open for 1% of the time, Pallas kernels for 17%

profile of v5, /device:TPU:56, one launch (start us, length us, event | category | flops | bytes accessed | tf_op | source)
XLA Modules:
  0.0 117.1 jit_solution(9894161867552575003)
XLA Ops:
  0.6 0.0 copy-start.3
  0.6 1.1 copy-done.3
  1.7 0.0 copy-start.6
  1.7 0.9 copy-done.6
  2.6 0.0 copy-start.7
  2.6 0.9 copy-done.7
  3.5 0.2 shard_map.86
  3.7 0.0 copy-start
  3.7 0.0 copy-start.4
  3.8 0.0 copy-start.5
  3.8 16.9 %all_to_all.20.q_ref = bf16[4,800,128]{2,1,0:T(8,128)(2,1)S(1)} all-to-all(bf16[4,800,128]{2,1,0:T(8,128)(2,1)S(1)} %shard_map.86), channel_id=1, replica_groups=mesh['dp'=16,'cx'=4,'zh'=4,'zl'=2] {'cx'}, dimensions={0} | all-to-all | bytes 1638400 | tf_op jit(solution)/shard_map/all_to_all | solution.py:254
  20.6 23.6 %all-gather = bf16[16,160,128]{2,1,0:T(8,128)(2,1)S(1)} all-gather(bf16[4,160,128]{2,1,0:T(8,128)(2,1)S(1)} %slice.18), channel_id=2, replica_groups=mesh['dp'=16,'cx'=4,'zh'=4,'zl'=2] {'zh'}, dimensions={0}, use_global_device_ids=true | all-gather | bytes 819200 | tf_op jit(solution)/shard_map/all_gather | solution.py:255
  44.3 0.0 copy-done
  44.3 0.0 copy-done.4
  44.3 0.0 copy-done.5
  44.3 2.2 %shard_map.87 = bf16[32,16,768]{2,1,0:T(8,128)(2,1)} custom-call(bf16[128,2560]{1,0:T(8,128)(2,1)S(1)} %copy-done, bf16[128,128]{1,0:T(8,128)(2,1)S(1)} %copy-done.4, f32[40,128]{1,0:T(8,128)S(1)} %bitcast.10, bf16[4,4,160,128]{3,2,1,0:T(8,128)(2,1)S(1)} %bitcast.8), custom_call_target="tpu_custom_call" | custom-call | tf_op jit(solution)/shard_map/pallas_call | solution.py:258
  46.5 5.3 %all-to-all-start.1 = ((bf16[32,16,768]{2,1,0:T(8,128)(2,1)}), bf16[32,16,768]{2,1,0:T(8,128)(2,1)S(1)}, u32[]{:S(2)}, u32[]{:S(2)}) async-start(bf16[32,16,768]{2,1,0:T(8,128)(2,1)} %shard_map.87), calls=%async_computation.1 | async-start | bytes 1572864 | tf_op jit(solution)/shard_map/all_to_all | solution.py:261
  51.8 0.9 fusion
  52.7 3.7 %collective-permute-start = (bf16[2,4,160,128]{3,2,1,0:T(8,128)(2,1)}, bf16[2,4,160,128]{3,2,1,0:T(8,128)(2,1)S(1)}, u32[]{:S(2)}, u32[]{:S(2)}) collective-permute-start(bf16[2,4,160,128]{3,2,1,0:T(8,128)(2,1)} %bitcast.6), channel_id=1, source_target_pairs={{0,1},{1,2},{2,3},{3,4},{4,5},{5,6},{6,7},{7,0},{8,9},{9,10},{10,1... | collective-permute-start | bytes 983048 | tf_op jit(solution)/shard_map/ppermute | solution.py:256
  56.3 3.4 %collective-permute-start.1 = (bf16[2,4,160,128]{3,2,1,0:T(8,128)(2,1)}, bf16[2,4,160,128]{3,2,1,0:T(8,128)(2,1)}, u32[]{:S(2)}, u32[]{:S(2)}) collective-permute-start(bf16[2,4,160,128]{3,2,1,0:T(8,128)(2,1)} %bitcast.7), channel_id=1, source_target_pairs={{0,7},{1,0},{2,1},{3,2},{4,3},{5,4},{6,5},{7,6},{8,15},{9,8},{10,9... | collective-permute-start | bytes 983048 | tf_op jit(solution)/shard_map/ppermute | solution.py:257
  59.7 7.0 %shard_map.88 = (f32[4,96,1024]{2,1,0:T(8,128)S(1)}, f32[4,1,1024]{2,1,0:T(1,128)S(1)}) custom-call(s32[1]{0:T(128)} %bitcast.5.place_ref, bf16[4,800,128]{2,1,0:T(8,128)(2,1)S(1)} %all_to_all.20.q_ref, bf16[4,4,160,128]{3,2,1,0:T(8,128)(2,1)S(1)} %bitcast.9), custom_call_target="tpu_custom_call" | custom-call | tf_op jit(solution)/shard_map/pallas_call | solution.py:267
  66.7 0.0 copy-start.1
  66.7 1.2 copy-done.1
  67.9 7.9 %collective-permute-done.below_ref = bf16[2,4,160,128]{3,2,1,0:T(8,128)(2,1)S(1)} collective-permute-done((bf16[2,4,160,128]{3,2,1,0:T(8,128)(2,1)}, bf16[2,4,160,128]{3,2,1,0:T(8,128)(2,1)S(1)}, u32[]{:S(2)}, u32[]{:S(2)}) %collective-permute-start) | collective-permute-done | bytes 327712 | tf_op jit(solution)/shard_map/ppermute | solution.py:256
  75.8 0.0 collective-permute-done.1.above_ref
  75.8 0.0 all-to-all-done.1.in_ref
  75.8 1.8 %shard_map.89.after_ref = bf16[32,16,640]{2,1,0:T(8,128)(2,1)} custom-call(s32[1]{0:T(128)} %bitcast.1.place_ref, bf16[32,16,768]{2,1,0:T(8,128)(2,1)S(1)} %all-to-all-done.1.in_ref, f32[4,1,1024]{2,1,0:T(1,128)S(1)} %get-tuple-element.4.after_ref.top_ref, bf16[2,4,160,128]{3,2,1,0:T(8,128)(2,1)S(1)} %collective-permute-done.below_ref, ...), custom_call_target="tpu_custom_call" | custom-call | tf_op jit(solution)/shard_map/pallas_call | solution.py:278
  77.6 7.6 %all-to-all-start.2 = ((bf16[32,16,640]{2,1,0:T(8,128)(2,1)}), bf16[32,16,640]{2,1,0:T(8,128)(2,1)S(1)}, u32[]{:S(2)}, u32[]{:S(2)}) async-start(bf16[32,16,640]{2,1,0:T(8,128)(2,1)} %shard_map.89.after_ref), calls=%async_computation.2 | async-start | bytes 1310720 | tf_op jit(solution)/shard_map/all_to_all | solution.py:283
  85.2 0.0 copy-start.2
  85.3 1.4 %copy-done.2 = f32[4,96,1024]{2,1,0:T(8,128)S(1)} copy-done((f32[4,96,1024]{2,1,0:T(8,128)S(1)}, f32[4,96,1024]{2,1,0:T(8,128)}, u32[]{:S(2)}) %copy-start.2) | copy-done | bytes 1572888
  86.7 0.0 copy-start.8
  86.7 9.8 %shard_map.91 = bf16[4,640,128]{2,1,0:T(8,128)(2,1)} custom-call(s32[1]{0:T(128)} %bitcast.5.place_ref, bf16[4,800,128]{2,1,0:T(8,128)(2,1)S(1)} %all_to_all.20.q_ref, bf16[2,4,160,128]{3,2,1,0:T(8,128)(2,1)S(1)} %collective-permute-done.below_ref, bf16[2,4,160,128]{3,2,1,0:T(8,128)(2,1)} %collective-permute-done.1.above_ref, f32[4,96,1024]{2,1,0:T(8,128)S(1)} %copy-done.2, ...), custom_call_target="tpu_custom_call" | custom-call | tf_op jit(solution)/shard_map/pallas_call | solution.py:284
  96.4 7.3 %all-to-all-done.2.enter_ref = bf16[32,16,640]{2,1,0:T(8,128)(2,1)S(1)} async-done(((bf16[32,16,640]{2,1,0:T(8,128)(2,1)}), bf16[32,16,640]{2,1,0:T(8,128)(2,1)S(1)}, u32[]{:S(2)}, u32[]{:S(2)}) %all-to-all-start.2) | async-done | bytes 655392 | tf_op jit(solution)/shard_map/all_to_all | solution.py:283
  103.8 3.5 %all-to-all-start.3 = ((bf16[4,640,128]{2,1,0:T(8,128)(2,1)}), bf16[4,640,128]{2,1,0:T(8,128)(2,1)S(1)}, u32[]{:S(2)}, u32[]{:S(2)}) async-start(bf16[4,640,128]{2,1,0:T(8,128)(2,1)} %shard_map.91), calls=%async_computation.3 | async-start | bytes 1310720 | tf_op jit(solution)/shard_map/all_to_all | solution.py:287
  107.3 0.0 copy-done.8
  107.3 2.7 %shard_map.90 = bf16[128,2560]{1,0:T(8,128)(2,1)} custom-call(bf16[128,2560]{1,0:T(8,128)(2,1)S(1)} %copy-done, bf16[128,128]{1,0:T(8,128)(2,1)S(1)} %copy-done.4, bf16[128,128]{1,0:T(8,128)(2,1)S(1)} %copy-done.8, f32[40,128]{1,0:T(8,128)S(1)} %bitcast.11, bf16[32,16,640]{2,1,0:T(8,128)(2,1)S(1)} %all-to-all-done.2.enter_ref), custom_call_target="tpu_custom_call" | custom-call | tf_op jit(solution)/shard_map/pallas_call | solution.py:288
  110.0 0.7 slice.21.after_ref
  110.7 5.3 %all-to-all-done.3.in_ref = bf16[4,640,128]{2,1,0:T(8,128)(2,1)S(1)} async-done(((bf16[4,640,128]{2,1,0:T(8,128)(2,1)}), bf16[4,640,128]{2,1,0:T(8,128)(2,1)S(1)}, u32[]{:S(2)}, u32[]{:S(2)}) %all-to-all-start.3) | async-done | bytes 655392 | tf_op jit(solution)/shard_map/all_to_all | solution.py:287
  116.0 1.1 shard_map.92
  (1 shorter events, 0.0 us)
Async XLA Ops:
  0.6 1.1 copy-start.3
  1.7 0.9 copy-start.6
  2.6 0.9 copy-start.7
  3.7 40.5 %copy-start = (bf16[128,2560]{1,0:T(8,128)(2,1)S(1)}, bf16[128,2560]{1,0:T(8,128)(2,1)}, u32[]{:S(2)}) copy-start(bf16[128,2560]{1,0:T(8,128)(2,1)} %x_ref.3) | copy-start | bytes 1966084
  3.7 40.5 %copy-start.4 = (bf16[128,128]{1,0:T(8,128)(2,1)S(1)}, bf16[128,128]{1,0:T(8,128)(2,1)}, u32[]{:S(2)}) copy-start(bf16[128,128]{1,0:T(8,128)(2,1)} %in_ref.3) | copy-start | bytes 98308
  3.8 40.5 %copy-start.5 = (f32[128,40]{0,1:T(8,128)S(1)}, f32[128,40]{0,1:T(8,128)}, u32[]{:S(2)}) copy-start(f32[128,40]{0,1:T(8,128)} %param.10) | copy-start | bytes 61444
  46.5 29.3 %all-to-all-start.1 = ((bf16[32,16,768]{2,1,0:T(8,128)(2,1)}), bf16[32,16,768]{2,1,0:T(8,128)(2,1)S(1)}, u32[]{:S(2)}, u32[]{:S(2)}) async-start(bf16[32,16,768]{2,1,0:T(8,128)(2,1)} %shard_map.87), calls=%async_computation.1 | async-start | bytes 1572864 | tf_op jit(solution)/shard_map/all_to_all | solution.py:261
  52.7 23.1 %collective-permute-start = (bf16[2,4,160,128]{3,2,1,0:T(8,128)(2,1)}, bf16[2,4,160,128]{3,2,1,0:T(8,128)(2,1)S(1)}, u32[]{:S(2)}, u32[]{:S(2)}) collective-permute-start(bf16[2,4,160,128]{3,2,1,0:T(8,128)(2,1)} %bitcast.6), channel_id=1, source_target_pairs={{0,1},{1,2},{2,3},{3,4},{4,5},{5,6},{6,7},{7,0},{8,9},{9,10},{10,1... | collective-permute-start | bytes 983048 | tf_op jit(solution)/shard_map/ppermute | solution.py:256
  56.3 19.4 %collective-permute-start.1 = (bf16[2,4,160,128]{3,2,1,0:T(8,128)(2,1)}, bf16[2,4,160,128]{3,2,1,0:T(8,128)(2,1)}, u32[]{:S(2)}, u32[]{:S(2)}) collective-permute-start(bf16[2,4,160,128]{3,2,1,0:T(8,128)(2,1)} %bitcast.7), channel_id=1, source_target_pairs={{0,7},{1,0},{2,1},{3,2},{4,3},{5,4},{6,5},{7,6},{8,15},{9,8},{10,9... | collective-permute-start | bytes 983048 | tf_op jit(solution)/shard_map/ppermute | solution.py:257
  66.7 1.2 %copy-start.1 = (f32[4,96,1024]{2,1,0:T(8,128)}, f32[4,96,1024]{2,1,0:T(8,128)S(1)}, u32[]{:S(2)}) copy-start(f32[4,96,1024]{2,1,0:T(8,128)S(1)} %get-tuple-element.5.total_ref) | copy-start | bytes 4718596
  77.6 26.2 %all-to-all-start.2 = ((bf16[32,16,640]{2,1,0:T(8,128)(2,1)}), bf16[32,16,640]{2,1,0:T(8,128)(2,1)S(1)}, u32[]{:S(2)}, u32[]{:S(2)}) async-start(bf16[32,16,640]{2,1,0:T(8,128)(2,1)} %shard_map.89.after_ref), calls=%async_computation.2 | async-start | bytes 1310720 | tf_op jit(solution)/shard_map/all_to_all | solution.py:283
  85.2 1.4 %copy-start.2 = (f32[4,96,1024]{2,1,0:T(8,128)S(1)}, f32[4,96,1024]{2,1,0:T(8,128)}, u32[]{:S(2)}) copy-start(f32[4,96,1024]{2,1,0:T(8,128)} %copy-done.1) | copy-start | bytes 4718596
  86.7 20.6 %copy-start.8 = (bf16[128,128]{1,0:T(8,128)(2,1)S(1)}, bf16[128,128]{1,0:T(8,128)(2,1)}, u32[]{:S(2)}) copy-start(bf16[128,128]{1,0:T(8,128)(2,1)} %map_ref.1) | copy-start | bytes 98308
  103.8 12.2 %all-to-all-start.3 = ((bf16[4,640,128]{2,1,0:T(8,128)(2,1)}), bf16[4,640,128]{2,1,0:T(8,128)(2,1)S(1)}, u32[]{:S(2)}, u32[]{:S(2)}) async-start(bf16[4,640,128]{2,1,0:T(8,128)(2,1)} %shard_map.91), calls=%async_computation.3 | async-start | bytes 1310720 | tf_op jit(solution)/shard_map/all_to_all | solution.py:287

commit v6 on v5

--- a/solution.py
+++ b/solution.py
@@ -130,30 +130,42 @@
 KEYS = NH * T
 
 
-def pack_kernel(q_ref, k_ref, v_ref, out_ref):
+def pack_kernel(k_ref, v_ref, out_ref):
     for g in range(KVH):
-        q = q_ref[:, g * GDH : (g + 1) * GDH].astype(F32)
-        out_ref[g, :GDH, :] = q.T.astype(BF16)
-        out_ref[g, GDH : GDH + DH, :] = k_ref[g * DH : (g + 1) * DH, :]
-        out_ref[g, GDH + DH :, :] = v_ref[g * DH : (g + 1) * DH, :]
-
-
-def attend(place_ref, q_ref, block, parity, k_buf, v_buf, q_buf, begin, end):
+        for i in range(NH):
+            out_ref[i * NX + g, :DH, :] = k_ref[g * DH : (g + 1) * DH, :]
+            out_ref[i * NX + g, DH:, :] = v_ref[g * DH : (g + 1) * DH, :]
+
+
+def turn_kernel(place_ref, q_ref, *out_refs):
+    for step, out_ref in enumerate(out_refs):
+        g = lax.rem(place_ref[0] + step, NX)
+        q = q_ref[:, pl.ds(pl.multiple_of(g * GDH, 128), GDH)].astype(F32)
+        out_ref[...] = q.T.astype(BF16)
+
+
+def scale_kernel(place_ref, *refs):
+    scale = math.log2(math.e) / math.sqrt(DH)
+    out_ref = refs[NX]
+    blank = jnp.zeros((128 - DH, QUERIES), BF16)
+    for s in range(NX):
+        c = lax.rem(place_ref[0] + (NX - s), NX)
+        out_ref[c, DH:128, :] = blank
+        out_ref[c, 128 + DH :, :] = blank
+        for h in range(GROUP):
+            hi, lo = split2(refs[s][h * DH : (h + 1) * DH, :].astype(F32) * scale)
+            out_ref[c, :DH, h * T : (h + 1) * T] = hi
+            out_ref[c, 128 : 128 + DH, h * T : (h + 1) * T] = lo
+
+
+def attend(place_ref, q_ref, block, parity, k_buf, v_buf, begin, end):
     z = place_ref[0]
-    scale = math.log2(math.e) / math.sqrt(DH)
     row = lax.broadcasted_iota(jnp.int32, (KEYS, QUERIES), 0)
     row = row + row // T * T + parity * T
     col = lax.broadcasted_iota(jnp.int32, (KEYS, QUERIES), 1) % T
     ones = jnp.where(lax.broadcasted_iota(jnp.int32, (16, KEYS), 0) == 0, 1.0, 0.0).astype(BF16)
     blank = jnp.zeros((128 - DH, T), F32)
-    blank_q = jnp.zeros((128 - DH, QUERIES), BF16)
     for c in range(NX):
-        q_buf[DH:128, :] = blank_q
-        q_buf[128 + DH :, :] = blank_q
-        for h in range(GROUP):
-            hi, lo = split2(q_ref[c, h * DH : (h + 1) * DH, :].astype(F32) * scale)
-            q_buf[:DH, h * T : (h + 1) * T] = hi
-            q_buf[128 : 128 + DH, h * T : (h + 1) * T] = lo
         v_buf[DH:, c * KEYS : (c + 1) * KEYS] = ones
         for i in range(NH):
             at = slice(c * KEYS + i * T, c * KEYS + (i + 1) * T)
@@ -162,7 +174,7 @@
             k = jnp.concatenate([kv[:DH, :].astype(F32), blank], axis=0).T.astype(BF16)
             k_buf[at, :128] = k
             k_buf[at, 128:] = k
-        q = q_buf[...]
+        q = q_ref[c]
 
         def scores(j, c=c, q=q):
             found = dot(k_buf[j * KEYS : (j + 1) * KEYS, :], q)
@@ -196,7 +208,7 @@
     attend(
         place_ref,
         q_ref,
-        lambda c, i: same_ref[i, c],
+        lambda c, i: same_ref[i * NX + c],
         place_ref[0] % 2,
         *bufs,
         lambda c: (None, None),
@@ -216,7 +228,9 @@
     attend(
         place_ref,
         q_ref,
-        lambda c, i: below_ref[i, c] if i < half else above_ref[i - half, c],
+        lambda c, i: (
+            below_ref[i * NX + c] if i < half else above_ref[(i - half) * NX + c]
+        ),
         1 - place_ref[0] % 2,
         *bufs,
         lambda c: (total_ref[c], top_ref[c]),
@@ -246,23 +260,32 @@
 
 
 def per_device(mixer_input, input_map, output_map, log_decay, query_rows, key_rows, value_rows):
-    place_z = lax.axis_index(("zh", "zl")).astype(jnp.int32).reshape(1)
-    place = lax.axis_index(("cx", "zh", "zl")).astype(jnp.int32).reshape(1)
-    packed = call(pack_kernel, (KVH, GDH + 2 * DH, T), [VMEM_SPEC] * 3)(
-        query_rows, key_rows.T, value_rows.T
-    )
-    packed = lax.all_to_all(packed, "cx", 0, 0)
-    same = lax.all_gather(packed[:, GDH:, :], "zh")
-    below = lax.ppermute(same[: NH // 2], ("zh", "zl"), [(k, (k + 1) % NZ) for k in range(NZ)])
-    above = lax.ppermute(same[NH // 2 :], ("zh", "zl"), [(k, (k - 1) % NZ) for k in range(NZ)])
+    x = lax.axis_index("cx").astype(jnp.int32).reshape(1)
+    z = lax.axis_index(("zh", "zl")).astype(jnp.int32).reshape(1)
+    place = x * NZ + z
+    pack = call(pack_kernel, (NH * NX, 2 * DH, T), [VMEM_SPEC] * 2)(key_rows.T, value_rows.T)
+    same = lax.all_to_all(pack, ("zh", "cx"), 0, 0)
+    half = NH * NX // 2
+    below = lax.ppermute(same[:half], ("zh", "zl"), [(k, (k + 1) % NZ) for k in range(NZ)])
+    above = lax.ppermute(same[half:], ("zh", "zl"), [(k, (k - 1) % NZ) for k in range(NZ)])
+    turned = pl.pallas_call(
+        turn_kernel,
+        out_shape=[jax.ShapeDtypeStruct((GDH, T), BF16)] * NX,
+        in_specs=[SMEM_SPEC, VMEM_SPEC],
+        out_specs=[VMEM_SPEC] * NX,
+    )(x, query_rows)
+    turned = [turned[0]] + [
+        lax.ppermute(turned[s], "cx", [(k, (k + s) % NX) for k in range(NX)])
+        for s in range(1, NX)
+    ]
+    queries = call(scale_kernel, (NX, 256, QUERIES), [SMEM_SPEC] + [VMEM_SPEC] * NX)(x, *turned)
     update = call(
         update_kernel, (NCTX, PIECE_ROWS, PIECE_COLS + 128), [VMEM_SPEC] * 3 + [ANY_SPEC]
-    )(mixer_input, input_map, log_decay.T, same)
+    )(mixer_input, input_map, log_decay.T, queries)
     update = lax.all_to_all(update, ("cx", "zh", "zl"), 0, 0)
     bufs = [
         pltpu.VMEM((NX * KEYS, 256), BF16),
         pltpu.VMEM((DH + 16, NX * KEYS), BF16),
-        pltpu.VMEM((256, QUERIES), BF16),
     ]
     total, top = pl.pallas_call(
         attend_same_kernel,
@@ -274,7 +297,7 @@
         out_specs=[VMEM_SPEC, VMEM_SPEC],
         scratch_shapes=bufs,
         compiler_params=pltpu.CompilerParams(vmem_limit_bytes=24 << 20),
-    )(place_z, packed, same)
+    )(z, queries, same)
     prefix = call(
         prefix_kernel,
         (NCTX, PIECE_ROWS, PIECE_COLS),
@@ -283,7 +306,7 @@
     entering = lax.all_to_all(prefix, ("cx", "zh", "zl"), 0, 0)
     attended = call(
         attend_other_kernel, (NX, GDH, T), [SMEM_SPEC] + [VMEM_SPEC] * 5 + [ANY_SPEC], bufs
-    )(place_z, packed, below, above, total, top, prefix)
+    )(z, queries, below, above, total, top, prefix)
     attended = lax.all_to_all(attended, "cx", 0, 0)
     mixer_output = call(mix_kernel, (T, WIDTH), [VMEM_SPEC] * 5)(
         mixer_input, input_map, output_map, log_decay.T, entering

time: 118 us -> 121 us (1.025)
  blocking collectives: 40.5 us -> 0 us
  starting transfers between devices: 23.5 us -> 52.2 us
  waiting for transfers between devices: 20.5 us -> 31.8 us
  local copies, waits for them, and re-layouts: 7.02 us -> 8.83 us
  Pallas kernels: 24.8 us -> 26.5 us
    all_gather x1 -> x0, blocking collectives: 23.6 us -> none  [per_device(): same = lax.all_gather(packed[:, GDH:, :], 'zh')]
    all_to_all x1 -> x0, blocking collectives: 16.9 us -> none  [per_device(): packed = lax.all_to_all(packed, 'cx', 0, 0)]
    all_to_all x0 -> x1, starting transfers between devices: none -> 13 us  [per_device(): same = lax.all_to_all(pack, ('zh', 'cx'), 0, 0)]
    ppermute x2 -> x5, starting transfers between devices: 7.04 us -> 18.6 us  [the longest x3 11.8 us: per_device(): lax.ppermute(turned[s], 'cx', [(k, (k + s) % NX) for k in range(NX)])]
    ppermute x2 -> x5, waiting for transfers between devices: 7.89 us -> 18.2 us  [the longest x1 10.4 us: per_device(): lax.ppermute(same[half:], ('zh', 'zl'), [(k, (k - 1) % NZ) for k in range...]
    all_to_all x1, starting transfers between devices: 5.31 us -> 9.64 us  [per_device(): update = lax.all_to_all(update, ('cx', 'zh', 'zl'), 0, 0)]
    pallas_call x1 -> x3, Pallas kernels: 0.24 us -> 3.36 us  [the longest x1 2.06 us: per_device(): pl.pallas_call(turn_kernel, out_shape=[jax.ShapeDtypeStruct((GDH, T), BF1...]
    all_to_all x1, waiting for transfers between devices: 7.35 us -> 9.41 us  [per_device(): entering = lax.all_to_all(prefix, ('cx', 'zh', 'zl'), 0, 0)]
  transfers between devices with their start and end apart: 5 -> 9, of which waited for: 3 -> 6; matrix products, arithmetic and copies ran while one was open for 1% -> 1% of each run, Pallas kernels for 17% -> 19%
where the time goes in v6:
time: 121 us; the launch traced here: 120 us
  starting transfers between devices  52.2 us (43%)
  waiting for transfers between devices  31.8 us (26%)
  Pallas kernels  26.5 us (22%)
  local copies, waits for them, and re-layouts  8.83 us (7%)
    all_to_all x1, starting transfers between devices, per_device(): same = lax.all_to_all(pack, ('zh', 'cx'), 0, 0)  13 us
    ppermute x3, starting transfers between devices, per_device(): lax.ppermute(turned[s], 'cx', [(k, (k + s) % NX) for k in range(NX)])  11.8 us
    ppermute x1, waiting for transfers between devices, per_device(): lax.ppermute(same[half:], ('zh', 'zl'), [(k, (k - 1) % NZ) for k in range...  10.4 us
    all_to_all x1, starting transfers between devices, per_device(): update = lax.all_to_all(update, ('cx', 'zh', 'zl'), 0, 0)  9.64 us
    pallas_call x1, Pallas kernels, per_device(): call(attend_other_kernel, (NX, GDH, T), [SMEM_SPEC] + [VMEM_SPEC] * 5 + [...  9.51 us
    all_to_all x1, waiting for transfers between devices, per_device(): entering = lax.all_to_all(prefix, ('cx', 'zh', 'zl'), 0, 0)  9.41 us
    all_to_all x1, starting transfers between devices, per_device(): entering = lax.all_to_all(prefix, ('cx', 'zh', 'zl'), 0, 0)  7.53 us
    unnamed x26, local copies, waits for them, and re-layouts  7.26 us
  transfers between devices with their start and end apart: 9, of which 6 were waited for; matrix products, arithmetic and copies ran while one was open for 1% of the time, Pallas kernels for 19%

profile of v6, /device:TPU:56, one launch (start us, length us, event | category | flops | bytes accessed | tf_op | source)
XLA Modules:
  0.0 120.3 jit_solution(12783448380421061481)
XLA Ops:
  0.6 0.0 copy-start.8
  0.6 0.9 copy-done.8
  1.5 0.0 copy-start.9
  1.5 0.9 copy-done.9
  2.4 0.9 shard_map.89
  3.3 0.0 copy-start.1
  3.3 0.0 copy-start.6
  3.3 0.0 copy-start.10
  3.3 13.0 %all-to-all-start.1 = ((bf16[16,160,128]{2,1,0:T(8,128)(2,1)}), bf16[16,160,128]{2,1,0:T(8,128)(2,1)S(1)}, u32[]{:S(2)}, u32[]{:S(2)}) async-start(bf16[16,160,128]{2,1,0:T(8,128)(2,1)} %shard_map.89), calls=%async_computation.1 | async-start | bytes 1310720 | tf_op jit(solution)/shard_map/all_to_all | solution.py:267
  16.3 2.1 %shard_map.86 = (bf16[640,128]{1,0:T(8,128)(2,1)}, bf16[640,128]{1,0:T(8,128)(2,1)}, bf16[640,128]{1,0:T(8,128)(2,1)}, bf16[640,128]{1,0:T(8,128)(2,1)}) custom-call(s32[1]{0:T(128)} %bitcast.1.place_ref, bf16[128,2560]{1,0:T(8,128)(2,1)} %q_ref.1), custom_call_target="tpu_custom_call" | custom-call | tf_op jit(solution)/shard_map/pallas_call | solution.py:271
  18.4 3.8 %collective-permute-start = (bf16[640,128]{1,0:T(8,128)(2,1)}, bf16[640,128]{1,0:T(8,128)(2,1)S(1)}, u32[]{:S(2)}, u32[]{:S(2)}) collective-permute-start(bf16[640,128]{1,0:T(8,128)(2,1)} %get-tuple-element.9), channel_id=1, source_target_pairs={{0,8},{8,16},{16,24},{24,0},{1,9},{9,17},{17,25},{25,1},{2,10},{10... | collective-permute-start | bytes 491528 | tf_op jit(solution)/shard_map/ppermute | solution.py:278
  22.2 4.6 %collective-permute-start.1 = (bf16[640,128]{1,0:T(8,128)(2,1)}, bf16[640,128]{1,0:T(8,128)(2,1)S(1)}, u32[]{:S(2)}, u32[]{:S(2)}) collective-permute-start(bf16[640,128]{1,0:T(8,128)(2,1)} %get-tuple-element.10), channel_id=1, source_target_pairs={{0,16},{8,24},{16,0},{24,8},{1,17},{9,25},{17,1},{25,9},{2,18},{10... | collective-permute-start | bytes 491528 | tf_op jit(solution)/shard_map/ppermute | solution.py:278
  26.8 3.4 %collective-permute-start.2 = (bf16[640,128]{1,0:T(8,128)(2,1)}, bf16[640,128]{1,0:T(8,128)(2,1)S(1)}, u32[]{:S(2)}, u32[]{:S(2)}) collective-permute-start(bf16[640,128]{1,0:T(8,128)(2,1)} %get-tuple-element.11), channel_id=1, source_target_pairs={{0,24},{8,0},{16,8},{24,16},{1,25},{9,1},{17,9},{25,17},{2,26},{10... | collective-permute-start | bytes 491528 | tf_op jit(solution)/shard_map/ppermute | solution.py:278
  30.2 0.9 collective-permute-done.refs_1_
  31.1 5.8 %collective-permute-done.1.refs_2_ = bf16[640,128]{1,0:T(8,128)(2,1)S(1)} collective-permute-done((bf16[640,128]{1,0:T(8,128)(2,1)}, bf16[640,128]{1,0:T(8,128)(2,1)S(1)}, u32[]{:S(2)}, u32[]{:S(2)}) %collective-permute-start.1) | collective-permute-done | bytes 163872 | tf_op jit(solution)/shard_map/ppermute | solution.py:278
  36.9 0.0 collective-permute-done.2.refs_3_
  36.9 0.0 copy-start.5
  36.9 0.9 copy-done.5
  37.8 0.4 shard_map.87.after_ref.q_ref
  38.2 0.0 copy-done.1
  38.2 0.0 copy-done.6
  38.2 0.0 copy-done.10
  38.2 1.3 %shard_map.88 = bf16[32,16,768]{2,1,0:T(8,128)(2,1)S(1)} custom-call(bf16[128,2560]{1,0:T(8,128)(2,1)S(1)} %copy-done.1, bf16[128,128]{1,0:T(8,128)(2,1)S(1)} %copy-done.6, f32[40,128]{1,0:T(8,128)S(1)} %bitcast.7, bf16[4,256,1024]{2,1,0:T(8,128)(2,1)S(1)} %shard_map.87.after_ref.q_ref), custom_call_target="tpu_custom_call" | custom-call | tf_op jit(solution)/shard_map/pallas_call | solution.py:282
  39.5 0.0 copy-start
  39.5 0.9 copy-done
  40.4 0.0 all-to-all-done.1.same_ref
  40.4 9.6 %all-to-all-start = ((bf16[32,16,768]{2,1,0:T(8,128)(2,1)}), bf16[32,16,768]{2,1,0:T(8,128)(2,1)S(1)}, u32[]{:S(2)}, u32[]{:S(2)}) async-start(bf16[32,16,768]{2,1,0:T(8,128)(2,1)} %copy-done), calls=%async_computation | async-start | bytes 1572864 | tf_op jit(solution)/shard_map/all_to_all | solution.py:285
  50.1 0.9 fusion
  50.9 4.9 %collective-permute-start.4 = (bf16[8,160,128]{2,1,0:T(8,128)(2,1)}, bf16[8,160,128]{2,1,0:T(8,128)(2,1)}, u32[]{:S(2)}, u32[]{:S(2)}) collective-permute-start(bf16[8,160,128]{2,1,0:T(8,128)(2,1)} %get-tuple-element.14), channel_id=1, source_target_pairs={{0,7},{1,0},{2,1},{3,2},{4,3},{5,4},{6,5},{7,6},{8,15},{9,8},{10,9... | collective-permute-start | bytes 983048 | tf_op jit(solution)/shard_map/ppermute | solution.py:270
  55.9 1.9 %collective-permute-start.3 = (bf16[8,160,128]{2,1,0:T(8,128)(2,1)}, bf16[8,160,128]{2,1,0:T(8,128)(2,1)}, u32[]{:S(2)}, u32[]{:S(2)}) collective-permute-start(bf16[8,160,128]{2,1,0:T(8,128)(2,1)} %get-tuple-element.15), channel_id=1, source_target_pairs={{0,1},{1,2},{2,3},{3,4},{4,5},{5,6},{6,7},{7,0},{8,9},{9,10},{10,1... | collective-permute-start | bytes 983048 | tf_op jit(solution)/shard_map/ppermute | solution.py:269
  57.8 6.7 %shard_map.90 = (f32[4,96,1024]{2,1,0:T(8,128)S(1)}, f32[4,1,1024]{2,1,0:T(1,128)S(1)}) custom-call(s32[1]{0:T(128)} %bitcast.2.place_ref, bf16[4,256,1024]{2,1,0:T(8,128)(2,1)S(1)} %shard_map.87.after_ref.q_ref, bf16[16,160,128]{2,1,0:T(8,128)(2,1)S(1)} %all-to-all-done.1.same_ref), custom_call_target="tpu_custom_call" | custom-call | tf_op jit(solution)/shard_map/pallas_call | solution.py:290
  64.5 0.0 copy-start.3
  64.6 1.2 copy-done.3
  65.7 10.4 %collective-permute-done.4.above_ref = bf16[8,160,128]{2,1,0:T(8,128)(2,1)} collective-permute-done((bf16[8,160,128]{2,1,0:T(8,128)(2,1)}, bf16[8,160,128]{2,1,0:T(8,128)(2,1)}, u32[]{:S(2)}, u32[]{:S(2)}) %collective-permute-start.4) | collective-permute-done | bytes 327712 | tf_op jit(solution)/shard_map/ppermute | solution.py:270
  76.1 1.2 collective-permute-done.3.below_ref
  77.3 0.0 all-to-all-done.in_ref
  77.3 1.8 %shard_map.91.after_ref = bf16[32,16,640]{2,1,0:T(8,128)(2,1)} custom-call(s32[1]{0:T(128)S(6)} %add.7.place_ref, bf16[32,16,768]{2,1,0:T(8,128)(2,1)S(1)} %all-to-all-done.in_ref, f32[4,1,1024]{2,1,0:T(1,128)S(1)} %get-tuple-element.12.after_ref.top_ref, bf16[8,160,128]{2,1,0:T(8,128)(2,1)} %collective-permute-done.3.below_ref, ...), custom_call_target="tpu_custom_call" | custom-call | tf_op jit(solution)/shard_map/pallas_call | solution.py:301
  79.1 7.5 %all-to-all-start.2 = ((bf16[32,16,640]{2,1,0:T(8,128)(2,1)}), bf16[32,16,640]{2,1,0:T(8,128)(2,1)S(1)}, u32[]{:S(2)}, u32[]{:S(2)}) async-start(bf16[32,16,640]{2,1,0:T(8,128)(2,1)} %shard_map.91.after_ref), calls=%async_computation.2 | async-start | bytes 1310720 | tf_op jit(solution)/shard_map/all_to_all | solution.py:306
  86.6 0.0 copy-start.4
  86.6 1.4 %copy-done.4 = f32[4,96,1024]{2,1,0:T(8,128)S(1)} copy-done((f32[4,96,1024]{2,1,0:T(8,128)S(1)}, f32[4,96,1024]{2,1,0:T(8,128)}, u32[]{:S(2)}) %copy-start.4) | copy-done | bytes 1572888
  88.0 0.0 copy-start.7
  88.0 0.0 copy-start.11
  88.0 0.0 copy-start.12
  88.0 9.5 %shard_map.93 = bf16[4,640,128]{2,1,0:T(8,128)(2,1)} custom-call(s32[1]{0:T(128)} %bitcast.2.place_ref, bf16[4,256,1024]{2,1,0:T(8,128)(2,1)S(1)} %shard_map.87.after_ref.q_ref, bf16[8,160,128]{2,1,0:T(8,128)(2,1)} %collective-permute-done.3.below_ref, bf16[8,160,128]{2,1,0:T(8,128)(2,1)} %collective-permute-done.4.above_ref, f32[4,96,1024]{2,1,0:T(8,128)S(1)} %copy-done.4, ...), custom_call_target="tpu_custom_call" | custom-call | tf_op jit(solution)/shard_map/pallas_call | solution.py:307
  97.5 9.4 %all-to-all-done.2.enter_ref = bf16[32,16,640]{2,1,0:T(8,128)(2,1)S(1)} async-done(((bf16[32,16,640]{2,1,0:T(8,128)(2,1)}), bf16[32,16,640]{2,1,0:T(8,128)(2,1)S(1)}, u32[]{:S(2)}, u32[]{:S(2)}) %all-to-all-start.2) | async-done | bytes 655392 | tf_op jit(solution)/shard_map/all_to_all | solution.py:306
  107.0 3.5 %all-to-all-start.3 = ((bf16[4,640,128]{2,1,0:T(8,128)(2,1)}), bf16[4,640,128]{2,1,0:T(8,128)(2,1)S(1)}, u32[]{:S(2)}, u32[]{:S(2)}) async-start(bf16[4,640,128]{2,1,0:T(8,128)(2,1)} %shard_map.93), calls=%async_computation.3 | async-start | bytes 1310720 | tf_op jit(solution)/shard_map/all_to_all | solution.py:310
  110.4 0.0 copy-done.7
  110.5 0.0 copy-done.11
  110.5 0.0 copy-done.12
  110.5 0.0 copy-start.2
  110.5 1.1 copy-done.2
  111.6 2.7 %shard_map.92 = bf16[128,2560]{1,0:T(8,128)(2,1)} custom-call(bf16[128,2560]{1,0:T(8,128)(2,1)S(1)} %copy-done.2, bf16[128,128]{1,0:T(8,128)(2,1)S(1)} %copy-done.7, bf16[128,128]{1,0:T(8,128)(2,1)S(1)} %copy-done.12, f32[40,128]{1,0:T(8,128)S(1)} %bitcast.8, bf16[32,16,640]{2,1,0:T(8,128)(2,1)S(1)} %all-to-all-done.2.enter_ref), custom_call_target="tpu_custom_call" | custom-call | tf_op jit(solution)/shard_map/pallas_call | solution.py:311
  114.3 0.7 slice.14.after_ref
  115.0 4.2 %all-to-all-done.3.in_ref = bf16[4,640,128]{2,1,0:T(8,128)(2,1)S(1)} async-done(((bf16[4,640,128]{2,1,0:T(8,128)(2,1)}), bf16[4,640,128]{2,1,0:T(8,128)(2,1)S(1)}, u32[]{:S(2)}, u32[]{:S(2)}) %all-to-all-start.3) | async-done | bytes 655392 | tf_op jit(solution)/shard_map/all_to_all | solution.py:310
  119.2 1.1 shard_map.94
Async XLA Ops:
  0.6 0.9 copy-start.8
  1.5 0.9 copy-start.9
  3.3 34.9 %copy-start.1 = (bf16[128,2560]{1,0:T(8,128)(2,1)S(1)}, bf16[128,2560]{1,0:T(8,128)(2,1)}, u32[]{:S(2)}) copy-start(bf16[128,2560]{1,0:T(8,128)(2,1)} %x_ref.3) | copy-start | bytes 1966084
  3.3 34.9 %copy-start.6 = (bf16[128,128]{1,0:T(8,128)(2,1)S(1)}, bf16[128,128]{1,0:T(8,128)(2,1)}, u32[]{:S(2)}) copy-start(bf16[128,128]{1,0:T(8,128)(2,1)} %in_ref.3) | copy-start | bytes 98308
  3.3 34.9 %copy-start.10 = (f32[128,40]{0,1:T(8,128)S(1)}, f32[128,40]{0,1:T(8,128)}, u32[]{:S(2)}) copy-start(f32[128,40]{0,1:T(8,128)} %param.10) | copy-start | bytes 61444
  3.3 37.1 %all-to-all-start.1 = ((bf16[16,160,128]{2,1,0:T(8,128)(2,1)}), bf16[16,160,128]{2,1,0:T(8,128)(2,1)S(1)}, u32[]{:S(2)}, u32[]{:S(2)}) async-start(bf16[16,160,128]{2,1,0:T(8,128)(2,1)} %shard_map.89), calls=%async_computation.1 | async-start | bytes 1310720 | tf_op jit(solution)/shard_map/all_to_all | solution.py:267
  18.4 12.6 %collective-permute-start = (bf16[640,128]{1,0:T(8,128)(2,1)}, bf16[640,128]{1,0:T(8,128)(2,1)S(1)}, u32[]{:S(2)}, u32[]{:S(2)}) collective-permute-start(bf16[640,128]{1,0:T(8,128)(2,1)} %get-tuple-element.9), channel_id=1, source_target_pairs={{0,8},{8,16},{16,24},{24,0},{1,9},{9,17},{17,25},{25,1},{2,10},{10... | collective-permute-start | bytes 491528 | tf_op jit(solution)/shard_map/ppermute | solution.py:278
  22.2 14.6 %collective-permute-start.1 = (bf16[640,128]{1,0:T(8,128)(2,1)}, bf16[640,128]{1,0:T(8,128)(2,1)S(1)}, u32[]{:S(2)}, u32[]{:S(2)}) collective-permute-start(bf16[640,128]{1,0:T(8,128)(2,1)} %get-tuple-element.10), channel_id=1, source_target_pairs={{0,16},{8,24},{16,0},{24,8},{1,17},{9,25},{17,1},{25,9},{2,18},{10... | collective-permute-start | bytes 491528 | tf_op jit(solution)/shard_map/ppermute | solution.py:278
  26.8 10.1 %collective-permute-start.2 = (bf16[640,128]{1,0:T(8,128)(2,1)}, bf16[640,128]{1,0:T(8,128)(2,1)S(1)}, u32[]{:S(2)}, u32[]{:S(2)}) collective-permute-start(bf16[640,128]{1,0:T(8,128)(2,1)} %get-tuple-element.11), channel_id=1, source_target_pairs={{0,24},{8,0},{16,8},{24,16},{1,25},{9,1},{17,9},{25,17},{2,26},{10... | collective-permute-start | bytes 491528 | tf_op jit(solution)/shard_map/ppermute | solution.py:278
  36.9 0.9 copy-start.5
  39.5 0.9 copy-start
  40.4 36.8 %all-to-all-start = ((bf16[32,16,768]{2,1,0:T(8,128)(2,1)}), bf16[32,16,768]{2,1,0:T(8,128)(2,1)S(1)}, u32[]{:S(2)}, u32[]{:S(2)}) async-start(bf16[32,16,768]{2,1,0:T(8,128)(2,1)} %copy-done), calls=%async_computation | async-start | bytes 1572864 | tf_op jit(solution)/shard_map/all_to_all | solution.py:285
  50.9 25.1 %collective-permute-start.4 = (bf16[8,160,128]{2,1,0:T(8,128)(2,1)}, bf16[8,160,128]{2,1,0:T(8,128)(2,1)}, u32[]{:S(2)}, u32[]{:S(2)}) collective-permute-start(bf16[8,160,128]{2,1,0:T(8,128)(2,1)} %get-tuple-element.14), channel_id=1, source_target_pairs={{0,7},{1,0},{2,1},{3,2},{4,3},{5,4},{6,5},{7,6},{8,15},{9,8},{10,9... | collective-permute-start | bytes 983048 | tf_op jit(solution)/shard_map/ppermute | solution.py:270
  55.9 21.4 %collective-permute-start.3 = (bf16[8,160,128]{2,1,0:T(8,128)(2,1)}, bf16[8,160,128]{2,1,0:T(8,128)(2,1)}, u32[]{:S(2)}, u32[]{:S(2)}) collective-permute-start(bf16[8,160,128]{2,1,0:T(8,128)(2,1)} %get-tuple-element.15), channel_id=1, source_target_pairs={{0,1},{1,2},{2,3},{3,4},{4,5},{5,6},{6,7},{7,0},{8,9},{9,10},{10,1... | collective-permute-start | bytes 983048 | tf_op jit(solution)/shard_map/ppermute | solution.py:269
  64.5 1.2 copy-start.3
  79.1 27.9 %all-to-all-start.2 = ((bf16[32,16,640]{2,1,0:T(8,128)(2,1)}), bf16[32,16,640]{2,1,0:T(8,128)(2,1)S(1)}, u32[]{:S(2)}, u32[]{:S(2)}) async-start(bf16[32,16,640]{2,1,0:T(8,128)(2,1)} %shard_map.91.after_ref), calls=%async_computation.2 | async-start | bytes 1310720 | tf_op jit(solution)/shard_map/all_to_all | solution.py:306
  86.6 1.4 %copy-start.4 = (f32[4,96,1024]{2,1,0:T(8,128)S(1)}, f32[4,96,1024]{2,1,0:T(8,128)}, u32[]{:S(2)}) copy-start(f32[4,96,1024]{2,1,0:T(8,128)} %copy-done.3) | copy-start | bytes 4718596
  88.0 22.4 %copy-start.7 = (bf16[128,128]{1,0:T(8,128)(2,1)S(1)}, bf16[128,128]{1,0:T(8,128)(2,1)}, u32[]{:S(2)}) copy-start(bf16[128,128]{1,0:T(8,128)(2,1)} %in_ref.3) | copy-start | bytes 98308
  88.0 22.4 %copy-start.11 = (f32[128,40]{0,1:T(8,128)S(1)}, f32[128,40]{0,1:T(8,128)}, u32[]{:S(2)}) copy-start(f32[128,40]{0,1:T(8,128)} %param.10) | copy-start | bytes 61444
  88.0 22.4 %copy-start.12 = (bf16[128,128]{1,0:T(8,128)(2,1)S(1)}, bf16[128,128]{1,0:T(8,128)(2,1)}, u32[]{:S(2)}) copy-start(bf16[128,128]{1,0:T(8,128)(2,1)} %map_ref.1) | copy-start | bytes 98308
  107.0 12.2 %all-to-all-start.3 = ((bf16[4,640,128]{2,1,0:T(8,128)(2,1)}), bf16[4,640,128]{2,1,0:T(8,128)(2,1)S(1)}, u32[]{:S(2)}, u32[]{:S(2)}) async-start(bf16[4,640,128]{2,1,0:T(8,128)(2,1)} %shard_map.93), calls=%async_computation.3 | async-start | bytes 1310720 | tf_op jit(solution)/shard_map/all_to_all | solution.py:310
  110.5 1.1 copy-start.2

commit v7 on v6

--- a/solution.py
+++ b/solution.py
@@ -66,7 +66,7 @@
     )
 
 
-def update_kernel(x_ref, in_ref, decay_ref, after_ref, out_ref):
+def update_kernel(x_ref, in_ref, decay_ref, out_ref):
     cumulative = cumulative_of(decay_ref[...])
     last = cumulative[T - 1 : T, :]
     onehot = head_spread()
@@ -90,7 +90,7 @@
             out_ref[d, :, PIECE_COLS:] = factor
 
 
-def prefix_kernel(place_ref, in_ref, after_ref, below_ref, above_ref, out_ref):
+def prefix_kernel(place_ref, in_ref, after_ref, out_ref):
     first_head = (place_ref[0] % (WIDTH // PIECE_COLS)) * (PIECE_COLS // P_SIZE)
     lane = lax.broadcasted_iota(jnp.int32, (128, PIECE_COLS), 0)
     cols = lax.broadcasted_iota(jnp.int32, (128, PIECE_COLS), 1)
@@ -130,7 +130,7 @@
 KEYS = NH * T
 
 
-def pack_kernel(k_ref, v_ref, out_ref):
+def pack_kernel(k_ref, v_ref, after_ref, out_ref):
     for g in range(KVH):
         for i in range(NH):
             out_ref[i * NX + g, :DH, :] = k_ref[g * DH : (g + 1) * DH, :]
@@ -200,7 +200,7 @@
         end(c, total, top)
 
 
-def attend_same_kernel(place_ref, q_ref, same_ref, total_ref, top_ref, *bufs):
+def attend_same_kernel(place_ref, q_ref, same_ref, after_ref, total_ref, top_ref, *bufs):
     def end(c, total, top):
         total_ref[c] = total
         top_ref[c] = top
@@ -217,7 +217,7 @@
 
 
 def attend_other_kernel(
-    place_ref, q_ref, below_ref, above_ref, total_ref, top_ref, after_ref, out_ref, *bufs
+    place_ref, q_ref, below_ref, above_ref, total_ref, top_ref, out_ref, *bufs
 ):
     def end(c, total, top):
         done = (total[:DH, :] / total[DH : DH + 1, :]).astype(BF16)
@@ -248,7 +248,7 @@
 ANY_SPEC = pl.BlockSpec(memory_space=pl.ANY)
 
 
-def call(kernel, shape, specs, scratch=(), limit=24):
+def call(kernel, shape, specs, scratch=(), limit=12):
     return pl.pallas_call(
         kernel,
         out_shape=jax.ShapeDtypeStruct(shape, BF16),
@@ -263,26 +263,33 @@
     x = lax.axis_index("cx").astype(jnp.int32).reshape(1)
     z = lax.axis_index(("zh", "zl")).astype(jnp.int32).reshape(1)
     place = x * NZ + z
-    pack = call(pack_kernel, (NH * NX, 2 * DH, T), [VMEM_SPEC] * 2)(key_rows.T, value_rows.T)
-    same = lax.all_to_all(pack, ("zh", "cx"), 0, 0)
-    half = NH * NX // 2
-    below = lax.ppermute(same[:half], ("zh", "zl"), [(k, (k + 1) % NZ) for k in range(NZ)])
-    above = lax.ppermute(same[half:], ("zh", "zl"), [(k, (k - 1) % NZ) for k in range(NZ)])
     turned = pl.pallas_call(
         turn_kernel,
         out_shape=[jax.ShapeDtypeStruct((GDH, T), BF16)] * NX,
         in_specs=[SMEM_SPEC, VMEM_SPEC],
         out_specs=[VMEM_SPEC] * NX,
+        compiler_params=pltpu.CompilerParams(vmem_limit_bytes=12 << 20),
     )(x, query_rows)
+    pack = call(pack_kernel, (NH * NX, 2 * DH, T), [VMEM_SPEC] * 2 + [ANY_SPEC])(
+        key_rows.T, value_rows.T, turned[0]
+    )
+    same = lax.all_to_all(pack, ("zh", "cx"), 0, 0)
+    half = NH * NX // 2
+    below = lax.ppermute(same[:half], ("zh", "zl"), [(k, (k + 1) % NZ) for k in range(NZ)])
+    above = lax.ppermute(same[half:], ("zh", "zl"), [(k, (k - 1) % NZ) for k in range(NZ)])
     turned = [turned[0]] + [
         lax.ppermute(turned[s], "cx", [(k, (k + s) % NX) for k in range(NX)])
         for s in range(1, NX)
     ]
     queries = call(scale_kernel, (NX, 256, QUERIES), [SMEM_SPEC] + [VMEM_SPEC] * NX)(x, *turned)
     update = call(
-        update_kernel, (NCTX, PIECE_ROWS, PIECE_COLS + 128), [VMEM_SPEC] * 3 + [ANY_SPEC]
-    )(mixer_input, input_map, log_decay.T, queries)
+        update_kernel, (NCTX, PIECE_ROWS, PIECE_COLS + 128), [VMEM_SPEC] * 3
+    )(mixer_input, input_map, log_decay.T)
     update = lax.all_to_all(update, ("cx", "zh", "zl"), 0, 0)
+    prefix = call(prefix_kernel, (NCTX, PIECE_ROWS, PIECE_COLS), [SMEM_SPEC, VMEM_SPEC, ANY_SPEC])(
+        place, update, queries
+    )
+    entering = lax.all_to_all(prefix, ("cx", "zh", "zl"), 0, 0)
     bufs = [
         pltpu.VMEM((NX * KEYS, 256), BF16),
         pltpu.VMEM((DH + 16, NX * KEYS), BF16),
@@ -293,20 +300,14 @@
             jax.ShapeDtypeStruct((NX, DH + 16, QUERIES), F32),
             jax.ShapeDtypeStruct((NX, 1, QUERIES), F32),
         ],
-        in_specs=[SMEM_SPEC, VMEM_SPEC, VMEM_SPEC],
+        in_specs=[SMEM_SPEC, VMEM_SPEC, VMEM_SPEC, ANY_SPEC],
         out_specs=[VMEM_SPEC, VMEM_SPEC],
         scratch_shapes=bufs,
         compiler_params=pltpu.CompilerParams(vmem_limit_bytes=24 << 20),
-    )(z, queries, same)
-    prefix = call(
-        prefix_kernel,
-        (NCTX, PIECE_ROWS, PIECE_COLS),
-        [SMEM_SPEC, VMEM_SPEC, VMEM_SPEC, ANY_SPEC, ANY_SPEC],
-    )(place, update, top, below, above)
-    entering = lax.all_to_all(prefix, ("cx", "zh", "zl"), 0, 0)
+    )(z, queries, same, prefix)
     attended = call(
-        attend_other_kernel, (NX, GDH, T), [SMEM_SPEC] + [VMEM_SPEC] * 5 + [ANY_SPEC], bufs
-    )(z, queries, below, above, total, top, prefix)
+        attend_other_kernel, (NX, GDH, T), [SMEM_SPEC] + [VMEM_SPEC] * 5, bufs, 24
+    )(z, queries, below, above, total, top)
     attended = lax.all_to_all(attended, "cx", 0, 0)
     mixer_output = call(mix_kernel, (T, WIDTH), [VMEM_SPEC] * 5)(
         mixer_input, input_map, output_map, log_decay.T, entering

time: 121 us -> 131 us (1.083)
  waiting for transfers between devices: 31.8 us -> 44.5 us
  starting transfers between devices: 52.2 us -> 50 us
  Pallas kernels: 26.5 us -> 24.8 us
    all_to_all x1, waiting for transfers between devices: 0.01 us -> 21.5 us  [per_device(): update = lax.all_to_all(update, ('cx', 'zh', 'zl'), 0, 0)]
    ppermute x1, waiting for transfers between devices: 10.4 us -> 0.01 us  [per_device(): lax.ppermute(same[half:], ('zh', 'zl'), [(k, (k - 1) % NZ) for k in range...]
    all_to_all x1, waiting for transfers between devices: 9.41 us -> 0.01 us  [per_device(): entering = lax.all_to_all(prefix, ('cx', 'zh', 'zl'), 0, 0)]
    all_to_all x1, starting transfers between devices: 13 us -> 3.91 us  [per_device(): same = lax.all_to_all(pack, ('zh', 'cx'), 0, 0)]
    ppermute x1, waiting for transfers between devices: 1.17 us -> 10.2 us  [per_device(): lax.ppermute(same[:half], ('zh', 'zl'), [(k, (k + 1) % NZ) for k in range...]
    all_to_all x1, starting transfers between devices: 9.64 us -> 13.2 us  [per_device(): update = lax.all_to_all(update, ('cx', 'zh', 'zl'), 0, 0)]
    all_to_all x1, waiting for transfers between devices: 4.21 us -> 6.67 us  [per_device(): attended = lax.all_to_all(attended, 'cx', 0, 0)]
    all_to_all x1, starting transfers between devices: 7.53 us -> 9.69 us  [per_device(): entering = lax.all_to_all(prefix, ('cx', 'zh', 'zl'), 0, 0)]
  transfers between devices with their start and end apart: 9 -> 9, of which waited for: 6 -> 6; matrix products, arithmetic and copies ran while one was open for 1% -> 1% of each run, Pallas kernels for 19% -> 17%
where the time goes in v7:
time: 131 us; the launch traced here: 130 us
  starting transfers between devices  50 us (38%)
  waiting for transfers between devices  44.5 us (34%)
  Pallas kernels  24.8 us (19%)
  local copies, waits for them, and re-layouts  9.63 us (7%)
    all_to_all x1, waiting for transfers between devices, per_device(): update = lax.all_to_all(update, ('cx', 'zh', 'zl'), 0, 0)  21.5 us
    all_to_all x1, starting transfers between devices, per_device(): update = lax.all_to_all(update, ('cx', 'zh', 'zl'), 0, 0)  13.2 us
    ppermute x3, starting transfers between devices, per_device(): lax.ppermute(turned[s], 'cx', [(k, (k + s) % NX) for k in range(NX)])  11.8 us
    ppermute x1, waiting for transfers between devices, per_device(): lax.ppermute(same[:half], ('zh', 'zl'), [(k, (k + 1) % NZ) for k in range...  10.2 us
    all_to_all x1, starting transfers between devices, per_device(): entering = lax.all_to_all(prefix, ('cx', 'zh', 'zl'), 0, 0)  9.69 us
    unnamed x36, local copies, waits for them, and re-layouts  8.9 us
    pallas_call x1, Pallas kernels, per_device(): call(attend_other_kernel, (NX, GDH, T), [SMEM_SPEC] + [VMEM_SPEC] * 5, bu...  8.65 us
    pallas_call x1, Pallas kernels, per_device(): pl.pallas_call(attend_same_kernel, out_shape=[jax.ShapeDtypeStruct((NX, D...  6.75 us
  transfers between devices with their start and end apart: 9, of which 6 were waited for; matrix products, arithmetic and copies ran while one was open for 1% of the time, Pallas kernels for 17%

profile of v7, /device:TPU:56, one launch (start us, length us, event | category | flops | bytes accessed | tf_op | source)
XLA Modules:
  0.0 129.8 jit_solution(17297063303119669858)
XLA Ops:
  0.6 0.0 copy-start
  0.6 1.1 copy-done
  1.7 0.0 copy-start.11
  1.7 0.8 copy-done.11
  2.5 0.0 copy-start.13
  2.5 0.7 copy-done.13
  3.2 0.0 copy-start.4
  3.2 0.0 copy-start.15
  3.2 0.0 copy-start.16
  3.2 2.2 %shard_map.86 = bf16[32,16,768]{2,1,0:T(8,128)(2,1)} custom-call(bf16[128,2560]{1,0:T(8,128)(2,1)S(1)} %copy-done, bf16[128,128]{1,0:T(8,128)(2,1)S(1)} %copy-done.11, f32[40,128]{1,0:T(8,128)S(1)} %bitcast.5), custom_call_target="tpu_custom_call" | custom-call | tf_op jit(solution)/shard_map/pallas_call | solution.py:285
  5.4 13.2 %all-to-all-start = ((bf16[32,16,768]{2,1,0:T(8,128)(2,1)}), bf16[32,16,768]{2,1,0:T(8,128)(2,1)S(1)}, u32[]{:S(2)}, u32[]{:S(2)}) async-start(bf16[32,16,768]{2,1,0:T(8,128)(2,1)} %shard_map.86), calls=%async_computation | async-start | bytes 1572864 | tf_op jit(solution)/shard_map/all_to_all | solution.py:288
  18.6 0.0 copy-done.4
  18.6 0.2 shard_map.87
  18.9 0.0 copy-done.15
  18.9 0.0 copy-done.16
  18.9 0.9 shard_map.91
  19.8 0.0 copy-start.2
  19.8 0.7 copy-done.2
  20.5 21.5 %all-to-all-done.in_ref = bf16[32,16,768]{2,1,0:T(8,128)(2,1)S(1)} async-done(((bf16[32,16,768]{2,1,0:T(8,128)(2,1)}), bf16[32,16,768]{2,1,0:T(8,128)(2,1)S(1)}, u32[]{:S(2)}, u32[]{:S(2)}) %all-to-all-start) | async-done | bytes 786464 | tf_op jit(solution)/shard_map/all_to_all | solution.py:288
  42.0 3.9 %all-to-all-start.2 = ((bf16[16,160,128]{2,1,0:T(8,128)(2,1)}), bf16[16,160,128]{2,1,0:T(8,128)(2,1)S(1)}, u32[]{:S(2)}, u32[]{:S(2)}) async-start(bf16[16,160,128]{2,1,0:T(8,128)(2,1)} %shard_map.91), calls=%async_computation.2 | async-start | bytes 1310720 | tf_op jit(solution)/shard_map/all_to_all | solution.py:276
  45.9 3.8 %collective-permute-start = (bf16[640,128]{1,0:T(8,128)(2,1)S(1)}, bf16[640,128]{1,0:T(8,128)(2,1)S(1)}, u32[]{:S(2)}, u32[]{:S(2)}) collective-permute-start(bf16[640,128]{1,0:T(8,128)(2,1)S(1)} %get-tuple-element.9), channel_id=1, source_target_pairs={{0,8},{8,16},{16,24},{24,0},{1,9},{9,17},{17,25},{25,1},{2,10},{10... | collective-permute-start | bytes 491528 | tf_op jit(solution)/shard_map/ppermute | solution.py:281
  49.7 4.6 %collective-permute-start.1 = (bf16[640,128]{1,0:T(8,128)(2,1)S(1)}, bf16[640,128]{1,0:T(8,128)(2,1)S(1)}, u32[]{:S(2)}, u32[]{:S(2)}) collective-permute-start(bf16[640,128]{1,0:T(8,128)(2,1)S(1)} %get-tuple-element.10), channel_id=1, source_target_pairs={{0,16},{8,24},{16,0},{24,8},{1,17},{9,25},{17,1},{25,9},{2,18},{10... | collective-permute-start | bytes 491528 | tf_op jit(solution)/shard_map/ppermute | solution.py:281
  54.3 3.4 %collective-permute-start.2 = (bf16[640,128]{1,0:T(8,128)(2,1)S(1)}, bf16[640,128]{1,0:T(8,128)(2,1)S(1)}, u32[]{:S(2)}, u32[]{:S(2)}) collective-permute-start(bf16[640,128]{1,0:T(8,128)(2,1)S(1)} %get-tuple-element.11), channel_id=1, source_target_pairs={{0,24},{8,0},{16,8},{24,16},{1,25},{9,1},{17,9},{25,17},{2,26},{10... | collective-permute-start | bytes 491528 | tf_op jit(solution)/shard_map/ppermute | solution.py:281
  57.7 3.5 %collective-permute-done.refs_1_ = bf16[640,128]{1,0:T(8,128)(2,1)S(1)} collective-permute-done((bf16[640,128]{1,0:T(8,128)(2,1)S(1)}, bf16[640,128]{1,0:T(8,128)(2,1)S(1)}, u32[]{:S(2)}, u32[]{:S(2)}) %collective-permute-start) | collective-permute-done | bytes 163872 | tf_op jit(solution)/shard_map/ppermute | solution.py:281
  61.1 0.0 copy-start.5
  61.2 0.7 copy-done.5
  61.8 2.4 %collective-permute-done.1.refs_2_ = bf16[640,128]{1,0:T(8,128)(2,1)S(1)} collective-permute-done((bf16[640,128]{1,0:T(8,128)(2,1)S(1)}, bf16[640,128]{1,0:T(8,128)(2,1)S(1)}, u32[]{:S(2)}, u32[]{:S(2)}) %collective-permute-start.1) | collective-permute-done | bytes 163872 | tf_op jit(solution)/shard_map/ppermute | solution.py:281
  64.2 0.0 copy-start.7
  64.2 0.7 copy-done.7
  64.9 0.3 collective-permute-done.2.refs_3_
  65.2 0.0 copy-start.9
  65.2 0.7 copy-done.9
  65.8 0.0 copy-start.3
  65.8 0.9 copy-done.3
  66.7 0.0 copy-start.6
  66.7 0.9 copy-done.6
  67.7 0.0 copy-start.8
  67.7 0.9 copy-done.8
  68.6 0.0 copy-start.10
  68.6 0.9 copy-done.10
  69.5 0.4 shard_map.88.after_ref.q_ref
  69.9 1.8 %shard_map.89.after_ref = bf16[32,16,640]{2,1,0:T(8,128)(2,1)} custom-call(s32[1]{0:T(128)S(6)} %add.7.place_ref, bf16[32,16,768]{2,1,0:T(8,128)(2,1)S(1)} %all-to-all-done.in_ref, bf16[4,256,1024]{2,1,0:T(8,128)(2,1)S(1)} %shard_map.88.after_ref.q_ref), custom_call_target="tpu_custom_call" | custom-call | tf_op jit(solution)/shard_map/pallas_call | solution.py:289
  71.7 0.0 all-to-all-done.2.same_ref
  71.7 9.7 %all-to-all-start.1 = ((bf16[32,16,640]{2,1,0:T(8,128)(2,1)}), bf16[32,16,640]{2,1,0:T(8,128)(2,1)S(1)}, u32[]{:S(2)}, u32[]{:S(2)}) async-start(bf16[32,16,640]{2,1,0:T(8,128)(2,1)} %shard_map.89.after_ref), calls=%async_computation.1 | async-start | bytes 1310720 | tf_op jit(solution)/shard_map/all_to_all | solution.py:292
  81.5 3.7 %collective-permute-start.3 = (bf16[8,160,128]{2,1,0:T(8,128)(2,1)S(1)}, bf16[8,160,128]{2,1,0:T(8,128)(2,1)S(1)}, u32[]{:S(2)}, u32[]{:S(2)}) collective-permute-start(bf16[8,160,128]{2,1,0:T(8,128)(2,1)S(1)} %get-tuple-element.15), channel_id=1, source_target_pairs={{0,1},{1,2},{2,3},{3,4},{4,5},{5,6},{6,7},{7,0},{8,9},{9,10},{10,1... | collective-permute-start | bytes 983048 | tf_op jit(solution)/shard_map/ppermute | solution.py:278
  85.2 3.5 %collective-permute-start.4 = (bf16[8,160,128]{2,1,0:T(8,128)(2,1)S(1)}, bf16[8,160,128]{2,1,0:T(8,128)(2,1)S(1)}, u32[]{:S(2)}, u32[]{:S(2)}) collective-permute-start(bf16[8,160,128]{2,1,0:T(8,128)(2,1)S(1)} %get-tuple-element.14), channel_id=1, source_target_pairs={{0,7},{1,0},{2,1},{3,2},{4,3},{5,4},{6,5},{7,6},{8,15},{9,8},{10,9... | collective-permute-start | bytes 983048 | tf_op jit(solution)/shard_map/ppermute | solution.py:279
  88.7 6.7 %shard_map.92 = (f32[4,96,1024]{2,1,0:T(8,128)S(1)}, f32[4,1,1024]{2,1,0:T(1,128)S(1)}) custom-call(s32[1]{0:T(128)} %bitcast.2.place_ref, bf16[4,256,1024]{2,1,0:T(8,128)(2,1)S(1)} %shard_map.88.after_ref.q_ref, bf16[16,160,128]{2,1,0:T(8,128)(2,1)S(1)} %all-to-all-done.2.same_ref, bf16[32,16,640]{2,1,0:T(8,128)(2,1)} %shard_map.89.after_ref), custom_call_target="tpu_custom_call" | custom-call | tf_op jit(solution)/shard_map/pallas_call | solution.py:297
  95.4 10.2 %collective-permute-done.3.below_ref = bf16[8,160,128]{2,1,0:T(8,128)(2,1)S(1)} collective-permute-done((bf16[8,160,128]{2,1,0:T(8,128)(2,1)S(1)}, bf16[8,160,128]{2,1,0:T(8,128)(2,1)S(1)}, u32[]{:S(2)}, u32[]{:S(2)}) %collective-permute-start.3) | collective-permute-done | bytes 327712 | tf_op jit(solution)/shard_map/ppermute | solution.py:278
  105.7 0.0 collective-permute-done.4.above_ref
  105.7 0.0 copy-start.1
  105.7 0.0 copy-start.12
  105.7 0.0 copy-start.14
  105.7 0.0 copy-start.17
  105.7 8.6 %shard_map.93 = bf16[4,640,128]{2,1,0:T(8,128)(2,1)} custom-call(s32[1]{0:T(128)} %bitcast.2.place_ref, bf16[4,256,1024]{2,1,0:T(8,128)(2,1)S(1)} %shard_map.88.after_ref.q_ref, bf16[8,160,128]{2,1,0:T(8,128)(2,1)S(1)} %collective-permute-done.3.below_ref, bf16[8,160,128]{2,1,0:T(8,128)(2,1)S(1)} %collective-permute-done.4.above_ref, ...), custom_call_target="tpu_custom_call" | custom-call | tf_op jit(solution)/shard_map/pallas_call | solution.py:308
  114.3 0.0 all-to-all-done.1.enter_ref
  114.3 4.3 %all-to-all-start.3 = ((bf16[4,640,128]{2,1,0:T(8,128)(2,1)}), bf16[4,640,128]{2,1,0:T(8,128)(2,1)S(1)}, u32[]{:S(2)}, u32[]{:S(2)}) async-start(bf16[4,640,128]{2,1,0:T(8,128)(2,1)} %shard_map.93), calls=%async_computation.3 | async-start | bytes 1310720 | tf_op jit(solution)/shard_map/all_to_all | solution.py:311
  118.6 0.0 copy-done.1
  118.6 0.0 copy-done.12
  118.6 0.0 copy-done.14
  118.6 0.0 copy-done.17
  118.6 2.7 %shard_map.90 = bf16[128,2560]{1,0:T(8,128)(2,1)} custom-call(bf16[128,2560]{1,0:T(8,128)(2,1)S(1)} %copy-done.1, bf16[128,128]{1,0:T(8,128)(2,1)S(1)} %copy-done.12, bf16[128,128]{1,0:T(8,128)(2,1)S(1)} %copy-done.17, f32[40,128]{1,0:T(8,128)S(1)} %bitcast.6, bf16[32,16,640]{2,1,0:T(8,128)(2,1)S(1)} %all-to-all-done.1.enter_ref), custom_call_target="tpu_custom_call" | custom-call | tf_op jit(solution)/shard_map/pallas_call | solution.py:312
  121.4 0.7 slice.14.after_ref
  122.1 6.7 %all-to-all-done.3.in_ref = bf16[4,640,128]{2,1,0:T(8,128)(2,1)S(1)} async-done(((bf16[4,640,128]{2,1,0:T(8,128)(2,1)}), bf16[4,640,128]{2,1,0:T(8,128)(2,1)S(1)}, u32[]{:S(2)}, u32[]{:S(2)}) %all-to-all-start.3) | async-done | bytes 655392 | tf_op jit(solution)/shard_map/all_to_all | solution.py:311
  128.7 1.1 shard_map.94
  (1 shorter events, 0.0 us)
Async XLA Ops:
  0.6 1.1 copy-start
  1.7 0.8 copy-start.11
  2.5 0.7 copy-start.13
  3.2 15.4 %copy-start.4 = (bf16[128,2560]{1,0:T(8,128)(2,1)S(1)}, bf16[128,2560]{1,0:T(8,128)(2,1)}, u32[]{:S(2)}) copy-start(bf16[128,2560]{1,0:T(8,128)(2,1)} %q_ref.1) | copy-start | bytes 1966084
  3.2 15.7 %copy-start.15 = (bf16[128,320]{0,1:T(8,128)(2,1)S(1)}, bf16[128,320]{0,1:T(8,128)(2,1)}, u32[]{:S(2)}) copy-start(bf16[128,320]{0,1:T(8,128)(2,1)} %param.12) | copy-start | bytes 245764
  3.2 15.7 %copy-start.16 = (bf16[128,320]{0,1:T(8,128)(2,1)S(1)}, bf16[128,320]{0,1:T(8,128)(2,1)}, u32[]{:S(2)}) copy-start(bf16[128,320]{0,1:T(8,128)(2,1)} %param.13) | copy-start | bytes 245764
  5.4 36.5 %all-to-all-start = ((bf16[32,16,768]{2,1,0:T(8,128)(2,1)}), bf16[32,16,768]{2,1,0:T(8,128)(2,1)S(1)}, u32[]{:S(2)}, u32[]{:S(2)}) async-start(bf16[32,16,768]{2,1,0:T(8,128)(2,1)} %shard_map.86), calls=%async_computation | async-start | bytes 1572864 | tf_op jit(solution)/shard_map/all_to_all | solution.py:288
  19.8 0.7 copy-start.2
  42.0 29.7 %all-to-all-start.2 = ((bf16[16,160,128]{2,1,0:T(8,128)(2,1)}), bf16[16,160,128]{2,1,0:T(8,128)(2,1)S(1)}, u32[]{:S(2)}, u32[]{:S(2)}) async-start(bf16[16,160,128]{2,1,0:T(8,128)(2,1)} %shard_map.91), calls=%async_computation.2 | async-start | bytes 1310720 | tf_op jit(solution)/shard_map/all_to_all | solution.py:276
  45.9 15.3 %collective-permute-start = (bf16[640,128]{1,0:T(8,128)(2,1)S(1)}, bf16[640,128]{1,0:T(8,128)(2,1)S(1)}, u32[]{:S(2)}, u32[]{:S(2)}) collective-permute-start(bf16[640,128]{1,0:T(8,128)(2,1)S(1)} %get-tuple-element.9), channel_id=1, source_target_pairs={{0,8},{8,16},{16,24},{24,0},{1,9},{9,17},{17,25},{25,1},{2,10},{10... | collective-permute-start | bytes 491528 | tf_op jit(solution)/shard_map/ppermute | solution.py:281
  49.7 14.5 %collective-permute-start.1 = (bf16[640,128]{1,0:T(8,128)(2,1)S(1)}, bf16[640,128]{1,0:T(8,128)(2,1)S(1)}, u32[]{:S(2)}, u32[]{:S(2)}) collective-permute-start(bf16[640,128]{1,0:T(8,128)(2,1)S(1)} %get-tuple-element.10), channel_id=1, source_target_pairs={{0,16},{8,24},{16,0},{24,8},{1,17},{9,25},{17,1},{25,9},{2,18},{10... | collective-permute-start | bytes 491528 | tf_op jit(solution)/shard_map/ppermute | solution.py:281
  54.3 10.9 %collective-permute-start.2 = (bf16[640,128]{1,0:T(8,128)(2,1)S(1)}, bf16[640,128]{1,0:T(8,128)(2,1)S(1)}, u32[]{:S(2)}, u32[]{:S(2)}) collective-permute-start(bf16[640,128]{1,0:T(8,128)(2,1)S(1)} %get-tuple-element.11), channel_id=1, source_target_pairs={{0,24},{8,0},{16,8},{24,16},{1,25},{9,1},{17,9},{25,17},{2,26},{10... | collective-permute-start | bytes 491528 | tf_op jit(solution)/shard_map/ppermute | solution.py:281
  61.1 0.7 copy-start.5
  64.2 0.7 copy-start.7
  65.2 0.7 copy-start.9
  65.8 0.9 copy-start.3
  66.7 0.9 copy-start.6
  67.7 0.9 copy-start.8
  68.6 0.9 copy-start.10
  71.7 42.7 %all-to-all-start.1 = ((bf16[32,16,640]{2,1,0:T(8,128)(2,1)}), bf16[32,16,640]{2,1,0:T(8,128)(2,1)S(1)}, u32[]{:S(2)}, u32[]{:S(2)}) async-start(bf16[32,16,640]{2,1,0:T(8,128)(2,1)} %shard_map.89.after_ref), calls=%async_computation.1 | async-start | bytes 1310720 | tf_op jit(solution)/shard_map/all_to_all | solution.py:292
  81.5 24.2 %collective-permute-start.3 = (bf16[8,160,128]{2,1,0:T(8,128)(2,1)S(1)}, bf16[8,160,128]{2,1,0:T(8,128)(2,1)S(1)}, u32[]{:S(2)}, u32[]{:S(2)}) collective-permute-start(bf16[8,160,128]{2,1,0:T(8,128)(2,1)S(1)} %get-tuple-element.15), channel_id=1, source_target_pairs={{0,1},{1,2},{2,3},{3,4},{4,5},{5,6},{6,7},{7,0},{8,9},{9,10},{10,1... | collective-permute-start | bytes 983048 | tf_op jit(solution)/shard_map/ppermute | solution.py:278
  85.2 20.5 %collective-permute-start.4 = (bf16[8,160,128]{2,1,0:T(8,128)(2,1)S(1)}, bf16[8,160,128]{2,1,0:T(8,128)(2,1)S(1)}, u32[]{:S(2)}, u32[]{:S(2)}) collective-permute-start(bf16[8,160,128]{2,1,0:T(8,128)(2,1)S(1)} %get-tuple-element.14), channel_id=1, source_target_pairs={{0,7},{1,0},{2,1},{3,2},{4,3},{5,4},{6,5},{7,6},{8,15},{9,8},{10,9... | collective-permute-start | bytes 983048 | tf_op jit(solution)/shard_map/ppermute | solution.py:279
  105.7 13.0 %copy-start.1 = (bf16[128,2560]{1,0:T(8,128)(2,1)S(1)}, bf16[128,2560]{1,0:T(8,128)(2,1)}, u32[]{:S(2)}) copy-start(bf16[128,2560]{1,0:T(8,128)(2,1)} %x_ref.3) | copy-start | bytes 1966084
  105.7 13.0 %copy-start.12 = (bf16[128,128]{1,0:T(8,128)(2,1)S(1)}, bf16[128,128]{1,0:T(8,128)(2,1)}, u32[]{:S(2)}) copy-start(bf16[128,128]{1,0:T(8,128)(2,1)} %in_ref.3) | copy-start | bytes 98308
  105.7 13.0 %copy-start.14 = (f32[128,40]{0,1:T(8,128)S(1)}, f32[128,40]{0,1:T(8,128)}, u32[]{:S(2)}) copy-start(f32[128,40]{0,1:T(8,128)} %param.10) | copy-start | bytes 61444
  105.7 13.0 %copy-start.17 = (bf16[128,128]{1,0:T(8,128)(2,1)S(1)}, bf16[128,128]{1,0:T(8,128)(2,1)}, u32[]{:S(2)}) copy-start(bf16[128,128]{1,0:T(8,128)(2,1)} %map_ref.1) | copy-start | bytes 98308
  114.3 14.4 %all-to-all-start.3 = ((bf16[4,640,128]{2,1,0:T(8,128)(2,1)}), bf16[4,640,128]{2,1,0:T(8,128)(2,1)S(1)}, u32[]{:S(2)}, u32[]{:S(2)}) async-start(bf16[4,640,128]{2,1,0:T(8,128)(2,1)} %shard_map.93), calls=%async_computation.3 | async-start | bytes 1310720 | tf_op jit(solution)/shard_map/all_to_all | solution.py:311

commit v8 on v5

--- a/solution.py
+++ b/solution.py
@@ -66,7 +66,7 @@
     )
 
 
-def update_kernel(x_ref, in_ref, decay_ref, after_ref, out_ref):
+def update_kernel(x_ref, in_ref, decay_ref, out_ref):
     cumulative = cumulative_of(decay_ref[...])
     last = cumulative[T - 1 : T, :]
     onehot = head_spread()
@@ -103,7 +103,8 @@
         state = factor * state + in_ref[k, :, :PIECE_COLS].astype(F32)
 
 
-def mix_kernel(x_ref, in_ref, map_ref, decay_ref, enter_ref, out_ref):
+def mix_kernel(x_ref, in_ref, map_ref, decay_ref, enter_ref, out_ref, end_ref):
+    end_ref[...] = jnp.zeros(end_ref.shape, F32)
     cumulative = cumulative_of(decay_ref[...])
     middle = 0.5 * cumulative[T - 1 : T, :]
     onehot = head_spread()
@@ -130,7 +131,16 @@
 KEYS = NH * T
 
 
-def pack_kernel(q_ref, k_ref, v_ref, out_ref):
+def pack_kernel(q_hbm, k_hbm, v_hbm, out_ref, q_ref, k_ref, v_ref, sems):
+    copies = [
+        pltpu.make_async_copy(q_hbm, q_ref, sems.at[0]),
+        pltpu.make_async_copy(k_hbm, k_ref, sems.at[1]),
+        pltpu.make_async_copy(v_hbm, v_ref, sems.at[2]),
+    ]
+    for copy in copies:
+        copy.start()
+    for copy in copies:
+        copy.wait()
     for g in range(KVH):
         q = q_ref[:, g * GDH : (g + 1) * GDH].astype(F32)
         out_ref[g, :GDH, :] = q.T.astype(BF16)
@@ -229,12 +239,18 @@
         out_ref[:, g * GDH : (g + 1) * GDH] = in_ref[g].astype(F32).T.astype(BF16)
 
 
+PACK_BUFS = [
+    pltpu.VMEM((T, QH * DH), BF16),
+    pltpu.VMEM((KVH * DH, T), BF16),
+    pltpu.VMEM((KVH * DH, T), BF16),
+    pltpu.SemaphoreType.DMA((3,)),
+]
 VMEM_SPEC = pl.BlockSpec(memory_space=pltpu.VMEM)
 SMEM_SPEC = pl.BlockSpec(memory_space=pltpu.SMEM)
 ANY_SPEC = pl.BlockSpec(memory_space=pl.ANY)
 
 
-def call(kernel, shape, specs, scratch=(), limit=24):
+def call(kernel, shape, specs, scratch=(), limit=12):
     return pl.pallas_call(
         kernel,
         out_shape=jax.ShapeDtypeStruct(shape, BF16),
@@ -248,16 +264,17 @@
 def per_device(mixer_input, input_map, output_map, log_decay, query_rows, key_rows, value_rows):
     place_z = lax.axis_index(("zh", "zl")).astype(jnp.int32).reshape(1)
     place = lax.axis_index(("cx", "zh", "zl")).astype(jnp.int32).reshape(1)
-    packed = call(pack_kernel, (KVH, GDH + 2 * DH, T), [VMEM_SPEC] * 3)(
+    packed = call(pack_kernel, (KVH, GDH + 2 * DH, T), [ANY_SPEC] * 3, PACK_BUFS)(
         query_rows, key_rows.T, value_rows.T
     )
     packed = lax.all_to_all(packed, "cx", 0, 0)
-    same = lax.all_gather(packed[:, GDH:, :], "zh")
+    kv = packed[:, GDH:, :]
+    same = lax.all_to_all(jnp.broadcast_to(kv[None], (NH,) + kv.shape), "zh", 0, 0)
     below = lax.ppermute(same[: NH // 2], ("zh", "zl"), [(k, (k + 1) % NZ) for k in range(NZ)])
     above = lax.ppermute(same[NH // 2 :], ("zh", "zl"), [(k, (k - 1) % NZ) for k in range(NZ)])
     update = call(
-        update_kernel, (NCTX, PIECE_ROWS, PIECE_COLS + 128), [VMEM_SPEC] * 3 + [ANY_SPEC]
-    )(mixer_input, input_map, log_decay.T, same)
+        update_kernel, (NCTX, PIECE_ROWS, PIECE_COLS + 128), [VMEM_SPEC] * 3
+    )(mixer_input, input_map, log_decay.T)
     update = lax.all_to_all(update, ("cx", "zh", "zl"), 0, 0)
     bufs = [
         pltpu.VMEM((NX * KEYS, 256), BF16),
@@ -282,15 +299,20 @@
     )(place, update, top, below, above)
     entering = lax.all_to_all(prefix, ("cx", "zh", "zl"), 0, 0)
     attended = call(
-        attend_other_kernel, (NX, GDH, T), [SMEM_SPEC] + [VMEM_SPEC] * 5 + [ANY_SPEC], bufs
+        attend_other_kernel, (NX, GDH, T), [SMEM_SPEC] + [VMEM_SPEC] * 5 + [ANY_SPEC], bufs, 24
     )(place_z, packed, below, above, total, top, prefix)
     attended = lax.all_to_all(attended, "cx", 0, 0)
-    mixer_output = call(mix_kernel, (T, WIDTH), [VMEM_SPEC] * 5)(
-        mixer_input, input_map, output_map, log_decay.T, entering
-    )
-    attention_output = call(place_kernel, (T, QH * DH), [VMEM_SPEC, VMEM_SPEC])(
-        attended, mixer_output[:16, :128]
-    )
+    mixer_output, end = pl.pallas_call(
+        mix_kernel,
+        out_shape=[
+            jax.ShapeDtypeStruct((T, WIDTH), BF16),
+            jax.ShapeDtypeStruct((8, 128), F32),
+        ],
+        in_specs=[VMEM_SPEC] * 5,
+        out_specs=[VMEM_SPEC] * 2,
+        compiler_params=pltpu.CompilerParams(vmem_limit_bytes=12 << 20),
+    )(mixer_input, input_map, output_map, log_decay.T, entering)
+    attention_output = call(place_kernel, (T, QH * DH), [VMEM_SPEC, VMEM_SPEC])(attended, end)
     return mixer_output, attention_output
 
 

time: 118 us -> 125 us (1.059)
  blocking collectives: 40.5 us -> 16.7 us
  waiting for transfers between devices: 20.5 us -> 39.7 us
  starting transfers between devices: 23.5 us -> 34.5 us
    all_gather x1 -> x0, blocking collectives: 23.6 us -> none  [per_device(): same = lax.all_gather(packed[:, GDH:, :], 'zh')]
    all_to_all x0 -> x1, waiting for transfers between devices: none -> 13.3 us  [per_device(): lax.all_to_all(jnp.broadcast_to(kv[None], (NH,) + kv.shape), 'zh', 0, 0)]
    all_to_all x0 -> x1, starting transfers between devices: none -> 10.3 us  [per_device(): lax.all_to_all(jnp.broadcast_to(kv[None], (NH,) + kv.shape), 'zh', 0, 0)]
    all_to_all x1, waiting for transfers between devices: 0.01 us -> 8.52 us  [per_device(): update = lax.all_to_all(update, ('cx', 'zh', 'zl'), 0, 0)]
    ppermute x1, waiting for transfers between devices: 7.89 us -> 1.27 us  [per_device(): lax.ppermute(same[:NH // 2], ('zh', 'zl'), [(k, (k + 1) % NZ) for k in ra...]
    all_to_all x1, waiting for transfers between devices: 7.35 us -> 9.14 us  [per_device(): entering = lax.all_to_all(prefix, ('cx', 'zh', 'zl'), 0, 0)]
    ppermute x1, starting transfers between devices: 3.69 us -> 1.92 us  [per_device(): lax.ppermute(same[:NH // 2], ('zh', 'zl'), [(k, (k + 1) % NZ) for k in ra...]
    ppermute x1, starting transfers between devices: 3.36 us -> 4.9 us  [per_device(): lax.ppermute(same[NH // 2:], ('zh', 'zl'), [(k, (k - 1) % NZ) for k in ra...]
  transfers between devices with their start and end apart: 5 -> 6, of which waited for: 3 -> 6; matrix products, arithmetic and copies ran while one was open for 1% -> 1% of each run, Pallas kernels for 17% -> 17%
where the time goes in v8:
time: 125 us; the launch traced here: 124 us
  waiting for transfers between devices  39.7 us (32%)
  starting transfers between devices  34.5 us (28%)
  Pallas kernels  25.3 us (20%)
  blocking collectives  16.7 us (13%)
  local copies, waits for them, and re-layouts  7.25 us (6%)
    all_to_all x1, blocking collectives, per_device(): packed = lax.all_to_all(packed, 'cx', 0, 0)  16.7 us
    all_to_all x1, waiting for transfers between devices, per_device(): lax.all_to_all(jnp.broadcast_to(kv[None], (NH,) + kv.shape), 'zh', 0, 0)  13.3 us
    all_to_all x1, starting transfers between devices, per_device(): lax.all_to_all(jnp.broadcast_to(kv[None], (NH,) + kv.shape), 'zh', 0, 0)  10.3 us
    pallas_call x1, Pallas kernels, per_device(): call(attend_other_kernel, (NX, GDH, T), [SMEM_SPEC] + [VMEM_SPEC] * 5 + [...  9.79 us
    all_to_all x1, waiting for transfers between devices, per_device(): entering = lax.all_to_all(prefix, ('cx', 'zh', 'zl'), 0, 0)  9.14 us
    all_to_all x1, waiting for transfers between devices, per_device(): update = lax.all_to_all(update, ('cx', 'zh', 'zl'), 0, 0)  8.52 us
    all_to_all x1, starting transfers between devices, per_device(): entering = lax.all_to_all(prefix, ('cx', 'zh', 'zl'), 0, 0)  7.52 us
    pallas_call x1, Pallas kernels, per_device(): pl.pallas_call(attend_same_kernel, out_shape=[jax.ShapeDtypeStruct((NX, D...  6.98 us
  transfers between devices with their start and end apart: 6, of which 6 were waited for; matrix products, arithmetic and copies ran while one was open for 1% of the time, Pallas kernels for 17%

profile of v8, /device:TPU:56, one launch (start us, length us, event | category | flops | bytes accessed | tf_op | source)
XLA Modules:
  0.0 124.1 jit_solution(15754170421010480193)
XLA Ops:
  0.6 0.0 copy-start.3
  0.6 1.1 copy-done.3
  1.7 0.0 copy-start.5
  1.7 0.9 copy-done.5
  2.6 0.0 copy-start.6
  2.6 0.9 copy-done.6
  3.5 0.7 shard_map.87
  4.2 16.7 %all_to_all.25.q_ref = bf16[4,800,128]{2,1,0:T(8,128)(2,1)S(1)} all-to-all(bf16[4,800,128]{2,1,0:T(8,128)(2,1)S(1)} %shard_map.87), channel_id=1, replica_groups=mesh['dp'=16,'cx'=4,'zh'=4,'zl'=2] {'cx'}, dimensions={0} | all-to-all | bytes 1638400 | tf_op jit(solution)/shard_map/all_to_all | solution.py:270
  20.9 0.0 copy-start
  20.9 0.0 copy-start.4
  20.9 0.0 copy-start.7
  20.9 0.9 broadcast_in_dim.2
  21.9 10.3 %all-to-all-start.2 = ((bf16[4,4,160,128]{3,2,1,0:T(8,128)(2,1)}), bf16[4,4,160,128]{3,2,1,0:T(8,128)(2,1)S(1)}, u32[]{:S(2)}, u32[]{:S(2)}) async-start(bf16[4,4,160,128]{3,2,1,0:T(8,128)(2,1)} %broadcast_in_dim.2), calls=%async_computation.2 | async-start | bytes 1310720 | tf_op jit(solution)/shard_map/all_to_all | solution.py:272
  32.2 0.0 copy-done
  32.2 0.0 copy-done.4
  32.2 0.0 copy-done.7
  32.2 2.2 %shard_map.86 = bf16[32,16,768]{2,1,0:T(8,128)(2,1)} custom-call(bf16[128,2560]{1,0:T(8,128)(2,1)S(1)} %copy-done, bf16[128,128]{1,0:T(8,128)(2,1)S(1)} %copy-done.4, f32[40,128]{1,0:T(8,128)S(1)} %bitcast.7), custom_call_target="tpu_custom_call" | custom-call | tf_op jit(solution)/shard_map/pallas_call | solution.py:275
  34.3 13.3 %all-to-all-done.2.same_ref = bf16[4,4,160,128]{3,2,1,0:T(8,128)(2,1)S(1)} async-done(((bf16[4,4,160,128]{3,2,1,0:T(8,128)(2,1)}), bf16[4,4,160,128]{3,2,1,0:T(8,128)(2,1)S(1)}, u32[]{:S(2)}, u32[]{:S(2)}) %all-to-all-start.2) | async-done | bytes 655392 | tf_op jit(solution)/shard_map/all_to_all | solution.py:272
  47.7 6.3 %all-to-all-start = ((bf16[32,16,768]{2,1,0:T(8,128)(2,1)}), bf16[32,16,768]{2,1,0:T(8,128)(2,1)S(1)}, u32[]{:S(2)}, u32[]{:S(2)}) async-start(bf16[32,16,768]{2,1,0:T(8,128)(2,1)} %shard_map.86), calls=%async_computation | async-start | bytes 1572864 | tf_op jit(solution)/shard_map/all_to_all | solution.py:278
  54.0 0.9 fusion
  54.9 4.9 %collective-permute-start.1 = (bf16[2,4,160,128]{3,2,1,0:T(8,128)(2,1)}, bf16[2,4,160,128]{3,2,1,0:T(8,128)(2,1)S(1)}, u32[]{:S(2)}, u32[]{:S(2)}) collective-permute-start(bf16[2,4,160,128]{3,2,1,0:T(8,128)(2,1)} %get-tuple-element.10), channel_id=1, source_target_pairs={{0,7},{1,0},{2,1},{3,2},{4,3},{5,4},{6,5},{7,6},{8,15},{9,8},{10,9... | collective-permute-start | bytes 983048 | tf_op jit(solution)/shard_map/ppermute | solution.py:274
  59.8 1.9 %collective-permute-start = (bf16[2,4,160,128]{3,2,1,0:T(8,128)(2,1)}, bf16[2,4,160,128]{3,2,1,0:T(8,128)(2,1)}, u32[]{:S(2)}, u32[]{:S(2)}) collective-permute-start(bf16[2,4,160,128]{3,2,1,0:T(8,128)(2,1)} %get-tuple-element.11), channel_id=1, source_target_pairs={{0,1},{1,2},{2,3},{3,4},{4,5},{5,6},{6,7},{7,0},{8,9},{9,10},{10,1... | collective-permute-start | bytes 983048 | tf_op jit(solution)/shard_map/ppermute | solution.py:273
  61.7 7.0 %shard_map.88 = (f32[4,96,1024]{2,1,0:T(8,128)S(1)}, f32[4,1,1024]{2,1,0:T(1,128)S(1)}) custom-call(s32[1]{0:T(128)} %bitcast.2.place_ref, bf16[4,800,128]{2,1,0:T(8,128)(2,1)S(1)} %all_to_all.25.q_ref, bf16[4,4,160,128]{3,2,1,0:T(8,128)(2,1)S(1)} %all-to-all-done.2.same_ref), custom_call_target="tpu_custom_call" | custom-call | tf_op jit(solution)/shard_map/pallas_call | solution.py:284
  68.7 0.0 copy-start.1
  68.7 1.2 copy-done.1
  69.9 8.5 %all-to-all-done.in_ref = bf16[32,16,768]{2,1,0:T(8,128)(2,1)S(1)} async-done(((bf16[32,16,768]{2,1,0:T(8,128)(2,1)}), bf16[32,16,768]{2,1,0:T(8,128)(2,1)S(1)}, u32[]{:S(2)}, u32[]{:S(2)}) %all-to-all-start) | async-done | bytes 786464 | tf_op jit(solution)/shard_map/all_to_all | solution.py:278
  78.4 1.5 %collective-permute-done.1.above_ref = bf16[2,4,160,128]{3,2,1,0:T(8,128)(2,1)S(1)} collective-permute-done((bf16[2,4,160,128]{3,2,1,0:T(8,128)(2,1)}, bf16[2,4,160,128]{3,2,1,0:T(8,128)(2,1)S(1)}, u32[]{:S(2)}, u32[]{:S(2)}) %collective-permute-start.1) | collective-permute-done | bytes 327712 | tf_op jit(solution)/shard_map/ppermute | solution.py:274
  79.9 1.3 %collective-permute-done.below_ref = bf16[2,4,160,128]{3,2,1,0:T(8,128)(2,1)} collective-permute-done((bf16[2,4,160,128]{3,2,1,0:T(8,128)(2,1)}, bf16[2,4,160,128]{3,2,1,0:T(8,128)(2,1)}, u32[]{:S(2)}, u32[]{:S(2)}) %collective-permute-start) | collective-permute-done | bytes 327712 | tf_op jit(solution)/shard_map/ppermute | solution.py:273
  81.1 1.8 %shard_map.89.after_ref = bf16[32,16,640]{2,1,0:T(8,128)(2,1)} custom-call(s32[1]{0:T(128)} %bitcast.1.place_ref, bf16[32,16,768]{2,1,0:T(8,128)(2,1)S(1)} %all-to-all-done.in_ref, f32[4,1,1024]{2,1,0:T(1,128)S(1)} %get-tuple-element.6.after_ref.top_ref, bf16[2,4,160,128]{3,2,1,0:T(8,128)(2,1)} %collective-permute-done.below_ref, ...), custom_call_target="tpu_custom_call" | custom-call | tf_op jit(solution)/shard_map/pallas_call | solution.py:295
  83.0 7.5 %all-to-all-start.3 = ((bf16[32,16,640]{2,1,0:T(8,128)(2,1)}), bf16[32,16,640]{2,1,0:T(8,128)(2,1)S(1)}, u32[]{:S(2)}, u32[]{:S(2)}) async-start(bf16[32,16,640]{2,1,0:T(8,128)(2,1)} %shard_map.89.after_ref), calls=%async_computation.3 | async-start | bytes 1310720 | tf_op jit(solution)/shard_map/all_to_all | solution.py:300
  90.5 0.0 copy-start.2
  90.5 1.4 %copy-done.2 = f32[4,96,1024]{2,1,0:T(8,128)S(1)} copy-done((f32[4,96,1024]{2,1,0:T(8,128)S(1)}, f32[4,96,1024]{2,1,0:T(8,128)}, u32[]{:S(2)}) %copy-start.2) | copy-done | bytes 1572888
  91.9 0.0 copy-start.8
  91.9 9.8 %shard_map.91 = bf16[4,640,128]{2,1,0:T(8,128)(2,1)} custom-call(s32[1]{0:T(128)} %bitcast.2.place_ref, bf16[4,800,128]{2,1,0:T(8,128)(2,1)S(1)} %all_to_all.25.q_ref, bf16[2,4,160,128]{3,2,1,0:T(8,128)(2,1)} %collective-permute-done.below_ref, bf16[2,4,160,128]{3,2,1,0:T(8,128)(2,1)S(1)} %collective-permute-done.1.above_ref, f32[4,96,1024]{2,1,0:T(8,128)S(1)} %copy-done.2, ...), custom_call_target="tpu_custom_call" | custom-call | tf_op jit(solution)/shard_map/pallas_call | solution.py:301
  101.7 9.1 %all-to-all-done.3.enter_ref = bf16[32,16,640]{2,1,0:T(8,128)(2,1)S(1)} async-done(((bf16[32,16,640]{2,1,0:T(8,128)(2,1)}), bf16[32,16,640]{2,1,0:T(8,128)(2,1)S(1)}, u32[]{:S(2)}, u32[]{:S(2)}) %all-to-all-start.3) | async-done | bytes 655392 | tf_op jit(solution)/shard_map/all_to_all | solution.py:300
  110.8 3.5 %all-to-all-start.4 = ((bf16[4,640,128]{2,1,0:T(8,128)(2,1)}), bf16[4,640,128]{2,1,0:T(8,128)(2,1)S(1)}, u32[]{:S(2)}, u32[]{:S(2)}) async-start(bf16[4,640,128]{2,1,0:T(8,128)(2,1)} %shard_map.91), calls=%async_computation.4 | async-start | bytes 1310720 | tf_op jit(solution)/shard_map/all_to_all | solution.py:304
  114.3 0.0 copy-done.8
  114.3 2.7 %shard_map.90 = (bf16[128,2560]{1,0:T(8,128)(2,1)}, f32[8,128]{1,0:T(8,128)S(1)}) custom-call(bf16[128,2560]{1,0:T(8,128)(2,1)S(1)} %copy-done, bf16[128,128]{1,0:T(8,128)(2,1)S(1)} %copy-done.4, bf16[128,128]{1,0:T(8,128)(2,1)S(1)} %copy-done.8, f32[40,128]{1,0:T(8,128)S(1)} %bitcast.8, bf16[32,16,640]{2,1,0:T(8,128)(2,1)S(1)} %all-to-all-done.3.enter_ref), custom_call_target="tpu_custom_call" | custom-call | tf_op jit(solution)/shard_map/pallas_call | solution.py:305
  117.1 6.0 %all-to-all-done.4.in_ref = bf16[4,640,128]{2,1,0:T(8,128)(2,1)S(1)} async-done(((bf16[4,640,128]{2,1,0:T(8,128)(2,1)}), bf16[4,640,128]{2,1,0:T(8,128)(2,1)S(1)}, u32[]{:S(2)}, u32[]{:S(2)}) %all-to-all-start.4) | async-done | bytes 655392 | tf_op jit(solution)/shard_map/all_to_all | solution.py:304
  123.1 1.1 shard_map.92
  (1 shorter events, 0.0 us)
Async XLA Ops:
  0.6 1.1 copy-start.3
  1.7 0.9 copy-start.5
  2.6 0.9 copy-start.6
  20.9 11.2 %copy-start = (bf16[128,2560]{1,0:T(8,128)(2,1)S(1)}, bf16[128,2560]{1,0:T(8,128)(2,1)}, u32[]{:S(2)}) copy-start(bf16[128,2560]{1,0:T(8,128)(2,1)} %x_ref.3) | copy-start | bytes 1966084
  20.9 11.2 %copy-start.4 = (bf16[128,128]{1,0:T(8,128)(2,1)S(1)}, bf16[128,128]{1,0:T(8,128)(2,1)}, u32[]{:S(2)}) copy-start(bf16[128,128]{1,0:T(8,128)(2,1)} %in_ref.3) | copy-start | bytes 98308
  20.9 11.2 %copy-start.7 = (f32[128,40]{0,1:T(8,128)S(1)}, f32[128,40]{0,1:T(8,128)}, u32[]{:S(2)}) copy-start(f32[128,40]{0,1:T(8,128)} %param.10) | copy-start | bytes 61444
  21.9 25.8 %all-to-all-start.2 = ((bf16[4,4,160,128]{3,2,1,0:T(8,128)(2,1)}), bf16[4,4,160,128]{3,2,1,0:T(8,128)(2,1)S(1)}, u32[]{:S(2)}, u32[]{:S(2)}) async-start(bf16[4,4,160,128]{3,2,1,0:T(8,128)(2,1)} %broadcast_in_dim.2), calls=%async_computation.2 | async-start | bytes 1310720 | tf_op jit(solution)/shard_map/all_to_all | solution.py:272
  47.7 30.7 %all-to-all-start = ((bf16[32,16,768]{2,1,0:T(8,128)(2,1)}), bf16[32,16,768]{2,1,0:T(8,128)(2,1)S(1)}, u32[]{:S(2)}, u32[]{:S(2)}) async-start(bf16[32,16,768]{2,1,0:T(8,128)(2,1)} %shard_map.86), calls=%async_computation | async-start | bytes 1572864 | tf_op jit(solution)/shard_map/all_to_all | solution.py:278
  54.9 25.0 %collective-permute-start.1 = (bf16[2,4,160,128]{3,2,1,0:T(8,128)(2,1)}, bf16[2,4,160,128]{3,2,1,0:T(8,128)(2,1)S(1)}, u32[]{:S(2)}, u32[]{:S(2)}) collective-permute-start(bf16[2,4,160,128]{3,2,1,0:T(8,128)(2,1)} %get-tuple-element.10), channel_id=1, source_target_pairs={{0,7},{1,0},{2,1},{3,2},{4,3},{5,4},{6,5},{7,6},{8,15},{9,8},{10,9... | collective-permute-start | bytes 983048 | tf_op jit(solution)/shard_map/ppermute | solution.py:274
  59.8 21.3 %collective-permute-start = (bf16[2,4,160,128]{3,2,1,0:T(8,128)(2,1)}, bf16[2,4,160,128]{3,2,1,0:T(8,128)(2,1)}, u32[]{:S(2)}, u32[]{:S(2)}) collective-permute-start(bf16[2,4,160,128]{3,2,1,0:T(8,128)(2,1)} %get-tuple-element.11), channel_id=1, source_target_pairs={{0,1},{1,2},{2,3},{3,4},{4,5},{5,6},{6,7},{7,0},{8,9},{9,10},{10,1... | collective-permute-start | bytes 983048 | tf_op jit(solution)/shard_map/ppermute | solution.py:273
  68.7 1.2 copy-start.1
  83.0 27.9 %all-to-all-start.3 = ((bf16[32,16,640]{2,1,0:T(8,128)(2,1)}), bf16[32,16,640]{2,1,0:T(8,128)(2,1)S(1)}, u32[]{:S(2)}, u32[]{:S(2)}) async-start(bf16[32,16,640]{2,1,0:T(8,128)(2,1)} %shard_map.89.after_ref), calls=%async_computation.3 | async-start | bytes 1310720 | tf_op jit(solution)/shard_map/all_to_all | solution.py:300
  90.5 1.4 %copy-start.2 = (f32[4,96,1024]{2,1,0:T(8,128)S(1)}, f32[4,96,1024]{2,1,0:T(8,128)}, u32[]{:S(2)}) copy-start(f32[4,96,1024]{2,1,0:T(8,128)} %copy-done.1) | copy-start | bytes 4718596
  91.9 22.4 %copy-start.8 = (bf16[128,128]{1,0:T(8,128)(2,1)S(1)}, bf16[128,128]{1,0:T(8,128)(2,1)}, u32[]{:S(2)}) copy-start(bf16[128,128]{1,0:T(8,128)(2,1)} %map_ref.1) | copy-start | bytes 98308
  110.8 12.2 %all-to-all-start.4 = ((bf16[4,640,128]{2,1,0:T(8,128)(2,1)}), bf16[4,640,128]{2,1,0:T(8,128)(2,1)S(1)}, u32[]{:S(2)}, u32[]{:S(2)}) async-start(bf16[4,640,128]{2,1,0:T(8,128)(2,1)} %shard_map.91), calls=%async_computation.4 | async-start | bytes 1310720 | tf_op jit(solution)/shard_map/all_to_all | solution.py:304

commit v9 on v8

--- a/solution.py
+++ b/solution.py
@@ -69,38 +69,37 @@
 def update_kernel(x_ref, in_ref, decay_ref, out_ref):
     cumulative = cumulative_of(decay_ref[...])
     last = cumulative[T - 1 : T, :]
-    onehot = head_spread()
-    tail = spread(jnp.exp(last - cumulative), onehot)
+    tail = spread(jnp.exp(last - cumulative), head_spread())
     hi, lo = split2(x_ref[...].astype(F32) * tail)
     in_t = in_ref[...].astype(F32).T.astype(BF16)
-    update = (dot(in_t, hi) + dot(in_t, lo)).astype(BF16)
-    total = jnp.broadcast_to(jnp.exp(last), (PIECE_ROWS, MIXER_HEADS))
-    total_hi, total_lo = split2(total)
-    head = lax.broadcasted_iota(jnp.int32, (MIXER_HEADS, 128), 0)
-    lane = lax.broadcasted_iota(jnp.int32, (MIXER_HEADS, 128), 1)
-    place_hi = jnp.where(lane == head, 1.0, 0.0).astype(BF16)
-    place_lo = jnp.where(lane == head + 64, 1.0, 0.0).astype(BF16)
-    factor = (dot(total_hi, place_hi) + dot(total_lo, place_lo)).astype(BF16)
+    out_ref[...] = (dot(in_t, hi) + dot(in_t, lo)).astype(BF16)
+
+
+def cut_kernel(in_ref, after_ref, out_ref):
+    across = WIDTH // PIECE_COLS
     for i in range(N // PIECE_ROWS):
-        for j in range(WIDTH // PIECE_COLS):
-            d = i * (WIDTH // PIECE_COLS) + j
-            out_ref[d, :, :PIECE_COLS] = update[
+        for j in range(across):
+            out_ref[i * across + j] = in_ref[
                 i * PIECE_ROWS : (i + 1) * PIECE_ROWS, j * PIECE_COLS : (j + 1) * PIECE_COLS
             ]
-            out_ref[d, :, PIECE_COLS:] = factor
-
-
-def prefix_kernel(place_ref, in_ref, after_ref, below_ref, above_ref, out_ref):
+
+
+def prefix_kernel(place_ref, in_ref, same_ref, below_ref, above_ref, after_ref, out_ref):
     first_head = (place_ref[0] % (WIDTH // PIECE_COLS)) * (PIECE_COLS // P_SIZE)
+    parity = place_ref[0] % 2
     lane = lax.broadcasted_iota(jnp.int32, (128, PIECE_COLS), 0)
     cols = lax.broadcasted_iota(jnp.int32, (128, PIECE_COLS), 1)
     head = first_head + cols // P_SIZE
     onehot = jnp.where((lane == head) | (lane == head + 64), 1.0, 0.0).astype(BF16)
     state = jnp.zeros((PIECE_ROWS, PIECE_COLS), F32)
+    half = NH // 2
     for k in range(NCTX):
         out_ref[k] = state.astype(BF16)
-        factor = dot(in_ref[k, :, PIECE_COLS:], onehot)
-        state = factor * state + in_ref[k, :, :PIECE_COLS].astype(F32)
+        c, i = k // NZ, k % NZ // 2
+        mine = same_ref[i, c, 2 * DH :, :].astype(F32)
+        other = below_ref[i, c, 2 * DH :, :] if i < half else above_ref[i - half, c, 2 * DH :, :]
+        decay = jnp.where(parity == k % 2, mine, other.astype(F32)).astype(BF16)
+        state = dot(decay, onehot) * state + in_ref[k].astype(F32)
 
 
 def mix_kernel(x_ref, in_ref, map_ref, decay_ref, enter_ref, out_ref, end_ref):
@@ -131,21 +130,26 @@
 KEYS = NH * T
 
 
-def pack_kernel(q_hbm, k_hbm, v_hbm, out_ref, q_ref, k_ref, v_ref, sems):
-    copies = [
-        pltpu.make_async_copy(q_hbm, q_ref, sems.at[0]),
-        pltpu.make_async_copy(k_hbm, k_ref, sems.at[1]),
-        pltpu.make_async_copy(v_hbm, v_ref, sems.at[2]),
-    ]
-    for copy in copies:
-        copy.start()
-    for copy in copies:
-        copy.wait()
+def pack_kernel(q_ref, k_ref, v_ref, decay_ref, out_ref):
+    total = lax.dot_general(
+        jnp.ones((PIECE_ROWS, T), F32),
+        decay_ref[...],
+        (((1,), (1,)), ((), ())),
+        precision=lax.Precision.HIGHEST,
+        preferred_element_type=F32,
+    )
+    total_hi, total_lo = split2(jnp.exp(total))
+    head = lax.broadcasted_iota(jnp.int32, (MIXER_HEADS, 128), 0)
+    lane = lax.broadcasted_iota(jnp.int32, (MIXER_HEADS, 128), 1)
+    place_hi = jnp.where(lane == head, 1.0, 0.0).astype(BF16)
+    place_lo = jnp.where(lane == head + 64, 1.0, 0.0).astype(BF16)
+    decay = (dot(total_hi, place_hi) + dot(total_lo, place_lo)).astype(BF16)
     for g in range(KVH):
         q = q_ref[:, g * GDH : (g + 1) * GDH].astype(F32)
         out_ref[g, :GDH, :] = q.T.astype(BF16)
         out_ref[g, GDH : GDH + DH, :] = k_ref[g * DH : (g + 1) * DH, :]
-        out_ref[g, GDH + DH :, :] = v_ref[g * DH : (g + 1) * DH, :]
+        out_ref[g, GDH + DH : GDH + 2 * DH, :] = v_ref[g * DH : (g + 1) * DH, :]
+        out_ref[g, GDH + 2 * DH :, :] = decay
 
 
 def attend(place_ref, q_ref, block, parity, k_buf, v_buf, q_buf, begin, end):
@@ -168,7 +172,7 @@
         for i in range(NH):
             at = slice(c * KEYS + i * T, c * KEYS + (i + 1) * T)
             kv = block(c, i)
-            v_buf[:DH, at] = kv[DH:, :]
+            v_buf[:DH, at] = kv[DH : 2 * DH, :]
             k = jnp.concatenate([kv[:DH, :].astype(F32), blank], axis=0).T.astype(BF16)
             k_buf[at, :128] = k
             k_buf[at, 128:] = k
@@ -239,12 +243,6 @@
         out_ref[:, g * GDH : (g + 1) * GDH] = in_ref[g].astype(F32).T.astype(BF16)
 
 
-PACK_BUFS = [
-    pltpu.VMEM((T, QH * DH), BF16),
-    pltpu.VMEM((KVH * DH, T), BF16),
-    pltpu.VMEM((KVH * DH, T), BF16),
-    pltpu.SemaphoreType.DMA((3,)),
-]
 VMEM_SPEC = pl.BlockSpec(memory_space=pltpu.VMEM)
 SMEM_SPEC = pl.BlockSpec(memory_space=pltpu.SMEM)
 ANY_SPEC = pl.BlockSpec(memory_space=pl.ANY)
@@ -264,17 +262,17 @@
 def per_device(mixer_input, input_map, output_map, log_decay, query_rows, key_rows, value_rows):
     place_z = lax.axis_index(("zh", "zl")).astype(jnp.int32).reshape(1)
     place = lax.axis_index(("cx", "zh", "zl")).astype(jnp.int32).reshape(1)
-    packed = call(pack_kernel, (KVH, GDH + 2 * DH, T), [ANY_SPEC] * 3, PACK_BUFS)(
-        query_rows, key_rows.T, value_rows.T
+    packed = call(pack_kernel, (KVH, GDH + 2 * DH + PIECE_ROWS, T), [VMEM_SPEC] * 4)(
+        query_rows, key_rows.T, value_rows.T, log_decay.T
     )
     packed = lax.all_to_all(packed, "cx", 0, 0)
-    kv = packed[:, GDH:, :]
-    same = lax.all_to_all(jnp.broadcast_to(kv[None], (NH,) + kv.shape), "zh", 0, 0)
+    same = lax.all_gather(packed[:, GDH:, :], "zh")
     below = lax.ppermute(same[: NH // 2], ("zh", "zl"), [(k, (k + 1) % NZ) for k in range(NZ)])
     above = lax.ppermute(same[NH // 2 :], ("zh", "zl"), [(k, (k - 1) % NZ) for k in range(NZ)])
-    update = call(
-        update_kernel, (NCTX, PIECE_ROWS, PIECE_COLS + 128), [VMEM_SPEC] * 3
-    )(mixer_input, input_map, log_decay.T)
+    update = call(update_kernel, (N, WIDTH), [VMEM_SPEC] * 3)(
+        mixer_input, input_map, log_decay.T
+    )
+    update = call(cut_kernel, (NCTX, PIECE_ROWS, PIECE_COLS), [VMEM_SPEC, ANY_SPEC])(update, same)
     update = lax.all_to_all(update, ("cx", "zh", "zl"), 0, 0)
     bufs = [
         pltpu.VMEM((NX * KEYS, 256), BF16),
@@ -292,11 +290,9 @@
         scratch_shapes=bufs,
         compiler_params=pltpu.CompilerParams(vmem_limit_bytes=24 << 20),
     )(place_z, packed, same)
-    prefix = call(
-        prefix_kernel,
-        (NCTX, PIECE_ROWS, PIECE_COLS),
-        [SMEM_SPEC, VMEM_SPEC, VMEM_SPEC, ANY_SPEC, ANY_SPEC],
-    )(place, update, top, below, above)
+    prefix = call(prefix_kernel, (NCTX, PIECE_ROWS, PIECE_COLS), [SMEM_SPEC] + [VMEM_SPEC] * 5)(
+        place, update, same, below, above, top
+    )
     entering = lax.all_to_all(prefix, ("cx", "zh", "zl"), 0, 0)
     attended = call(
         attend_other_kernel, (NX, GDH, T), [SMEM_SPEC] + [VMEM_SPEC] * 5 + [ANY_SPEC], bufs, 24

time: 125 us -> 118 us (0.944)
  waiting for transfers between devices: 39.7 us -> 30.8 us
  blocking collectives: 16.7 us -> 23.4 us
  starting transfers between devices: 34.5 us -> 28.4 us
  Pallas kernels: 25.3 us -> 26.7 us
    all_gather x0 -> x1, blocking collectives: none -> 23.4 us  [per_device(): same = lax.all_gather(packed[:, GDH:, :], 'zh')]
    all_to_all x1 -> x0, blocking collectives: 16.7 us -> none  [per_device(): packed = lax.all_to_all(packed, 'cx', 0, 0)]
    all_to_all x1, waiting for transfers between devices: 8.52 us -> 0.01 us  [per_device(): update = lax.all_to_all(update, ('cx', 'zh', 'zl'), 0, 0)]
    all_to_all x1, starting transfers between devices: 10.3 us -> 4.29 us  [per_device(): packed = lax.all_to_all(packed, 'cx', 0, 0)]
    ppermute x1, waiting for transfers between devices: 1.27 us -> 5.88 us  [per_device(): lax.ppermute(same[:NH // 2], ('zh', 'zl'), [(k, (k + 1) % NZ) for k in ra...]
    all_to_all x1, waiting for transfers between devices: 13.3 us -> 11.5 us  [per_device(): packed = lax.all_to_all(packed, 'cx', 0, 0)]
    ppermute x1, starting transfers between devices: 1.92 us -> 3.69 us  [per_device(): lax.ppermute(same[:NH // 2], ('zh', 'zl'), [(k, (k + 1) % NZ) for k in ra...]
    all_to_all x1, waiting for transfers between devices: 9.14 us -> 7.39 us  [per_device(): entering = lax.all_to_all(prefix, ('cx', 'zh', 'zl'), 0, 0)]
  transfers between devices with their start and end apart: 6 -> 6, of which waited for: 6 -> 4; matrix products, arithmetic and copies ran while one was open for 1% -> 1% of each run, Pallas kernels for 17% -> 18%
where the time goes in v9:
time: 118 us; the launch traced here: 117 us
  waiting for transfers between devices  30.8 us (26%)
  starting transfers between devices  28.4 us (24%)
  Pallas kernels  26.7 us (23%)
  blocking collectives  23.4 us (20%)
  local copies, waits for them, and re-layouts  7.07 us (6%)
    all_gather x1, blocking collectives, per_device(): same = lax.all_gather(packed[:, GDH:, :], 'zh')  23.4 us
    all_to_all x1, waiting for transfers between devices, per_device(): packed = lax.all_to_all(packed, 'cx', 0, 0)  11.5 us
    pallas_call x1, Pallas kernels, per_device(): call(attend_other_kernel, (NX, GDH, T), [SMEM_SPEC] + [VMEM_SPEC] * 5 + [...  9.79 us
    all_to_all x1, starting transfers between devices, per_device(): entering = lax.all_to_all(prefix, ('cx', 'zh', 'zl'), 0, 0)  7.63 us
    all_to_all x1, waiting for transfers between devices, per_device(): entering = lax.all_to_all(prefix, ('cx', 'zh', 'zl'), 0, 0)  7.39 us
    pallas_call x1, Pallas kernels, per_device(): pl.pallas_call(attend_same_kernel, out_shape=[jax.ShapeDtypeStruct((NX, D...  6.98 us
    unnamed x20, local copies, waits for them, and re-layouts  6.16 us
    all_to_all x1, waiting for transfers between devices, per_device(): attended = lax.all_to_all(attended, 'cx', 0, 0)  6 us
  transfers between devices with their start and end apart: 6, of which 4 were waited for; matrix products, arithmetic and copies ran while one was open for 1% of the time, Pallas kernels for 18%

profile of v9, /device:TPU:56, one launch (start us, length us, event | category | flops | bytes accessed | tf_op | source)
XLA Modules:
  0.0 117.1 jit_solution(2235411902796020604)
XLA Ops:
  0.6 0.0 copy-start.3
  0.6 1.1 copy-done.3
  1.7 0.0 copy-start.4
  1.7 0.7 copy-done.4
  2.4 0.0 copy-start.7
  2.5 0.9 copy-done.7
  3.3 0.0 copy-start.8
  3.3 0.9 copy-done.8
  4.2 0.0 copy-start
  4.2 0.0 copy-start.5
  4.2 0.0 copy-start.6
  4.2 1.2 %shard_map.87 = bf16[4,816,128]{2,1,0:T(8,128)(2,1)} custom-call(bf16[128,2560]{1,0:T(8,128)(2,1)S(1)} %copy-done.3, bf16[320,128]{1,0:T(8,128)(2,1)S(1)} %bitcast.14, bf16[320,128]{1,0:T(8,128)(2,1)S(1)} %bitcast.15, f32[40,128]{1,0:T(8,128)S(1)} %bitcast.11), custom_call_target="tpu_custom_call" | custom-call | tf_op jit(solution)/shard_map/pallas_call | solution.py:265
  5.4 4.3 %all-to-all-start = ((bf16[4,816,128]{2,1,0:T(8,128)(2,1)}), bf16[4,816,128]{2,1,0:T(8,128)(2,1)S(1)}, u32[]{:S(2)}, u32[]{:S(2)}) async-start(bf16[4,816,128]{2,1,0:T(8,128)(2,1)} %shard_map.87), calls=%async_computation | async-start | bytes 1671168 | tf_op jit(solution)/shard_map/all_to_all | solution.py:268
  9.7 0.0 copy-done
  9.7 0.0 copy-done.5
  9.7 0.0 copy-done.6
  9.7 1.3 %shard_map.86.in_ref = bf16[128,2560]{1,0:T(8,128)(2,1)S(1)} custom-call(bf16[128,2560]{1,0:T(8,128)(2,1)S(1)} %copy-done, bf16[128,128]{1,0:T(8,128)(2,1)S(1)} %copy-done.6, f32[40,128]{1,0:T(8,128)S(1)} %bitcast.12), custom_call_target="tpu_custom_call" | custom-call | tf_op jit(solution)/shard_map/pallas_call | solution.py:272
  11.0 11.5 %all-to-all-done.q_ref = bf16[4,816,128]{2,1,0:T(8,128)(2,1)S(1)} async-done(((bf16[4,816,128]{2,1,0:T(8,128)(2,1)}), bf16[4,816,128]{2,1,0:T(8,128)(2,1)S(1)}, u32[]{:S(2)}, u32[]{:S(2)}) %all-to-all-start) | async-done | bytes 835616 | tf_op jit(solution)/shard_map/all_to_all | solution.py:268
  22.5 23.4 %all-gather = bf16[16,176,128]{2,1,0:T(8,128)(2,1)S(1)} all-gather(bf16[4,176,128]{2,1,0:T(8,128)(2,1)S(1)} %slice.14), channel_id=2, replica_groups=mesh['dp'=16,'cx'=4,'zh'=4,'zl'=2] {'zh'}, dimensions={0}, use_global_device_ids=true | all-gather | bytes 901120 | tf_op jit(solution)/shard_map/all_gather | solution.py:269
  45.9 0.9 shard_map.88
  46.8 5.9 %all-to-all-start.1 = ((bf16[32,16,640]{2,1,0:T(8,128)(2,1)}), bf16[32,16,640]{2,1,0:T(8,128)(2,1)S(1)}, u32[]{:S(2)}, u32[]{:S(2)}) async-start(bf16[32,16,640]{2,1,0:T(8,128)(2,1)} %shard_map.88), calls=%async_computation.1 | async-start | bytes 1310720 | tf_op jit(solution)/shard_map/all_to_all | solution.py:276
  52.8 0.9 fusion
  53.7 3.7 %collective-permute-start = (bf16[2,4,176,128]{3,2,1,0:T(8,128)(2,1)}, bf16[2,4,176,128]{3,2,1,0:T(8,128)(2,1)S(1)}, u32[]{:S(2)}, u32[]{:S(2)}) collective-permute-start(bf16[2,4,176,128]{3,2,1,0:T(8,128)(2,1)} %bitcast.5), channel_id=1, source_target_pairs={{0,1},{1,2},{2,3},{3,4},{4,5},{5,6},{6,7},{7,0},{8,9},{9,10},{10,1... | collective-permute-start | bytes 1081352 | tf_op jit(solution)/shard_map/ppermute | solution.py:270
  57.4 3.4 %collective-permute-start.1 = (bf16[2,4,176,128]{3,2,1,0:T(8,128)(2,1)}, bf16[2,4,176,128]{3,2,1,0:T(8,128)(2,1)}, u32[]{:S(2)}, u32[]{:S(2)}) collective-permute-start(bf16[2,4,176,128]{3,2,1,0:T(8,128)(2,1)} %bitcast.6), channel_id=1, source_target_pairs={{0,7},{1,0},{2,1},{3,2},{4,3},{5,4},{6,5},{7,6},{8,15},{9,8},{10,9... | collective-permute-start | bytes 1081352 | tf_op jit(solution)/shard_map/ppermute | solution.py:271
  60.7 7.0 %shard_map.89 = (f32[4,96,1024]{2,1,0:T(8,128)S(1)}, f32[4,1,1024]{2,1,0:T(1,128)S(1)}) custom-call(s32[1]{0:T(128)} %bitcast.7.place_ref, bf16[4,816,128]{2,1,0:T(8,128)(2,1)S(1)} %all-to-all-done.q_ref, bf16[4,4,176,128]{3,2,1,0:T(8,128)(2,1)S(1)} %bitcast.9), custom_call_target="tpu_custom_call" | custom-call | tf_op jit(solution)/shard_map/pallas_call | solution.py:282
  67.7 0.0 copy-start.1
  67.7 1.2 copy-done.1
  68.9 5.9 %collective-permute-done.below_ref = bf16[2,4,176,128]{3,2,1,0:T(8,128)(2,1)S(1)} collective-permute-done((bf16[2,4,176,128]{3,2,1,0:T(8,128)(2,1)}, bf16[2,4,176,128]{3,2,1,0:T(8,128)(2,1)S(1)}, u32[]{:S(2)}, u32[]{:S(2)}) %collective-permute-start) | collective-permute-done | bytes 360480 | tf_op jit(solution)/shard_map/ppermute | solution.py:270
  74.8 0.0 collective-permute-done.1.above_ref
  74.8 0.0 all-to-all-done.1.in_ref
  74.8 2.8 %shard_map.90.after_ref = bf16[32,16,640]{2,1,0:T(8,128)(2,1)} custom-call(s32[1]{0:T(128)} %bitcast.1.place_ref, bf16[32,16,640]{2,1,0:T(8,128)(2,1)S(1)} %all-to-all-done.1.in_ref, bf16[4,4,176,128]{3,2,1,0:T(8,128)(2,1)S(1)} %bitcast.10, bf16[2,4,176,128]{3,2,1,0:T(8,128)(2,1)S(1)} %collective-permute-done.below_ref, ...), custom_call_target="tpu_custom_call" | custom-call | tf_op jit(solution)/shard_map/pallas_call | solution.py:293
  77.6 7.6 %all-to-all-start.2 = ((bf16[32,16,640]{2,1,0:T(8,128)(2,1)}), bf16[32,16,640]{2,1,0:T(8,128)(2,1)S(1)}, u32[]{:S(2)}, u32[]{:S(2)}) async-start(bf16[32,16,640]{2,1,0:T(8,128)(2,1)} %shard_map.90.after_ref), calls=%async_computation.2 | async-start | bytes 1310720 | tf_op jit(solution)/shard_map/all_to_all | solution.py:296
  85.2 0.0 copy-start.2
  85.2 1.4 %copy-done.2 = f32[4,96,1024]{2,1,0:T(8,128)S(1)} copy-done((f32[4,96,1024]{2,1,0:T(8,128)S(1)}, f32[4,96,1024]{2,1,0:T(8,128)}, u32[]{:S(2)}) %copy-start.2) | copy-done | bytes 1572888
  86.6 0.0 copy-start.9
  86.6 9.8 %shard_map.92 = bf16[4,640,128]{2,1,0:T(8,128)(2,1)} custom-call(s32[1]{0:T(128)} %bitcast.7.place_ref, bf16[4,816,128]{2,1,0:T(8,128)(2,1)S(1)} %all-to-all-done.q_ref, bf16[2,4,176,128]{3,2,1,0:T(8,128)(2,1)S(1)} %collective-permute-done.below_ref, bf16[2,4,176,128]{3,2,1,0:T(8,128)(2,1)} %collective-permute-done.1.above_ref, ...), custom_call_target="tpu_custom_call" | custom-call | tf_op jit(solution)/shard_map/pallas_call | solution.py:297
  96.4 7.4 %all-to-all-done.2.enter_ref = bf16[32,16,640]{2,1,0:T(8,128)(2,1)S(1)} async-done(((bf16[32,16,640]{2,1,0:T(8,128)(2,1)}), bf16[32,16,640]{2,1,0:T(8,128)(2,1)S(1)}, u32[]{:S(2)}, u32[]{:S(2)}) %all-to-all-start.2) | async-done | bytes 655392 | tf_op jit(solution)/shard_map/all_to_all | solution.py:296
  103.8 3.5 %all-to-all-start.3 = ((bf16[4,640,128]{2,1,0:T(8,128)(2,1)}), bf16[4,640,128]{2,1,0:T(8,128)(2,1)S(1)}, u32[]{:S(2)}, u32[]{:S(2)}) async-start(bf16[4,640,128]{2,1,0:T(8,128)(2,1)} %shard_map.92), calls=%async_computation.3 | async-start | bytes 1310720 | tf_op jit(solution)/shard_map/all_to_all | solution.py:300
  107.3 0.0 copy-done.9
  107.3 2.7 %shard_map.91 = (bf16[128,2560]{1,0:T(8,128)(2,1)}, f32[8,128]{1,0:T(8,128)S(1)}) custom-call(bf16[128,2560]{1,0:T(8,128)(2,1)S(1)} %copy-done, bf16[128,128]{1,0:T(8,128)(2,1)S(1)} %copy-done.6, bf16[128,128]{1,0:T(8,128)(2,1)S(1)} %copy-done.9, f32[40,128]{1,0:T(8,128)S(1)} %bitcast.13, bf16[32,16,640]{2,1,0:T(8,128)(2,1)S(1)} %all-to-all-done.2.enter_ref), custom_call_target="tpu_custom_call" | custom-call | tf_op jit(solution)/shard_map/pallas_call | solution.py:301
  110.0 6.0 %all-to-all-done.3.in_ref = bf16[4,640,128]{2,1,0:T(8,128)(2,1)S(1)} async-done(((bf16[4,640,128]{2,1,0:T(8,128)(2,1)}), bf16[4,640,128]{2,1,0:T(8,128)(2,1)S(1)}, u32[]{:S(2)}, u32[]{:S(2)}) %all-to-all-start.3) | async-done | bytes 655392 | tf_op jit(solution)/shard_map/all_to_all | solution.py:300
  116.1 1.1 shard_map.93
  (1 shorter events, 0.0 us)
Async XLA Ops:
  0.6 1.1 copy-start.3
  1.7 0.7 copy-start.4
  2.4 0.9 copy-start.7
  3.3 0.9 copy-start.8
  4.2 5.5 %copy-start = (bf16[128,2560]{1,0:T(8,128)(2,1)S(1)}, bf16[128,2560]{1,0:T(8,128)(2,1)}, u32[]{:S(2)}) copy-start(bf16[128,2560]{1,0:T(8,128)(2,1)} %x_ref.3) | copy-start | bytes 1966084
  4.2 5.5 %copy-start.5 = (f32[128,40]{0,1:T(8,128)S(1)}, f32[128,40]{0,1:T(8,128)}, u32[]{:S(2)}) copy-start(f32[128,40]{0,1:T(8,128)} %param.10) | copy-start | bytes 61444
  4.2 5.5 %copy-start.6 = (bf16[128,128]{1,0:T(8,128)(2,1)S(1)}, bf16[128,128]{1,0:T(8,128)(2,1)}, u32[]{:S(2)}) copy-start(bf16[128,128]{1,0:T(8,128)(2,1)} %in_ref.3) | copy-start | bytes 98308
  5.4 17.1 %all-to-all-start = ((bf16[4,816,128]{2,1,0:T(8,128)(2,1)}), bf16[4,816,128]{2,1,0:T(8,128)(2,1)S(1)}, u32[]{:S(2)}, u32[]{:S(2)}) async-start(bf16[4,816,128]{2,1,0:T(8,128)(2,1)} %shard_map.87), calls=%async_computation | async-start | bytes 1671168 | tf_op jit(solution)/shard_map/all_to_all | solution.py:268
  46.8 28.0 %all-to-all-start.1 = ((bf16[32,16,640]{2,1,0:T(8,128)(2,1)}), bf16[32,16,640]{2,1,0:T(8,128)(2,1)S(1)}, u32[]{:S(2)}, u32[]{:S(2)}) async-start(bf16[32,16,640]{2,1,0:T(8,128)(2,1)} %shard_map.88), calls=%async_computation.1 | async-start | bytes 1310720 | tf_op jit(solution)/shard_map/all_to_all | solution.py:276
  53.7 21.1 %collective-permute-start = (bf16[2,4,176,128]{3,2,1,0:T(8,128)(2,1)}, bf16[2,4,176,128]{3,2,1,0:T(8,128)(2,1)S(1)}, u32[]{:S(2)}, u32[]{:S(2)}) collective-permute-start(bf16[2,4,176,128]{3,2,1,0:T(8,128)(2,1)} %bitcast.5), channel_id=1, source_target_pairs={{0,1},{1,2},{2,3},{3,4},{4,5},{5,6},{6,7},{7,0},{8,9},{9,10},{10,1... | collective-permute-start | bytes 1081352 | tf_op jit(solution)/shard_map/ppermute | solution.py:270
  57.4 17.4 %collective-permute-start.1 = (bf16[2,4,176,128]{3,2,1,0:T(8,128)(2,1)}, bf16[2,4,176,128]{3,2,1,0:T(8,128)(2,1)}, u32[]{:S(2)}, u32[]{:S(2)}) collective-permute-start(bf16[2,4,176,128]{3,2,1,0:T(8,128)(2,1)} %bitcast.6), channel_id=1, source_target_pairs={{0,7},{1,0},{2,1},{3,2},{4,3},{5,4},{6,5},{7,6},{8,15},{9,8},{10,9... | collective-permute-start | bytes 1081352 | tf_op jit(solution)/shard_map/ppermute | solution.py:271
  67.7 1.2 copy-start.1
  77.6 26.2 %all-to-all-start.2 = ((bf16[32,16,640]{2,1,0:T(8,128)(2,1)}), bf16[32,16,640]{2,1,0:T(8,128)(2,1)S(1)}, u32[]{:S(2)}, u32[]{:S(2)}) async-start(bf16[32,16,640]{2,1,0:T(8,128)(2,1)} %shard_map.90.after_ref), calls=%async_computation.2 | async-start | bytes 1310720 | tf_op jit(solution)/shard_map/all_to_all | solution.py:296
  85.2 1.4 %copy-start.2 = (f32[4,96,1024]{2,1,0:T(8,128)S(1)}, f32[4,96,1024]{2,1,0:T(8,128)}, u32[]{:S(2)}) copy-start(f32[4,96,1024]{2,1,0:T(8,128)} %copy-done.1) | copy-start | bytes 4718596
  86.6 20.7 %copy-start.9 = (bf16[128,128]{1,0:T(8,128)(2,1)S(1)}, bf16[128,128]{1,0:T(8,128)(2,1)}, u32[]{:S(2)}) copy-start(bf16[128,128]{1,0:T(8,128)(2,1)} %map_ref.1) | copy-start | bytes 98308
  103.8 12.2 %all-to-all-start.3 = ((bf16[4,640,128]{2,1,0:T(8,128)(2,1)}), bf16[4,640,128]{2,1,0:T(8,128)(2,1)S(1)}, u32[]{:S(2)}, u32[]{:S(2)}) async-start(bf16[4,640,128]{2,1,0:T(8,128)(2,1)} %shard_map.92), calls=%async_computation.3 | async-start | bytes 1310720 | tf_op jit(solution)/shard_map/all_to_all | solution.py:300

commit v10 on v9

--- a/solution.py
+++ b/solution.py
@@ -219,12 +219,19 @@
 
 
 def attend_other_kernel(
-    place_ref, q_ref, below_ref, above_ref, total_ref, top_ref, after_ref, out_ref, *bufs
+    place_ref, q_ref, below_ref, above_ref, total_ref, top_ref, after_ref, *refs
 ):
+    out_refs, bufs = refs[:NX], refs[NX:]
+
     def end(c, total, top):
         done = (total[:DH, :] / total[DH : DH + 1, :]).astype(BF16)
-        for h in range(GROUP):
-            out_ref[c, h * DH : (h + 1) * DH, :] = done[:, h * T : (h + 1) * T]
+        step = lax.rem(c + NX - place_ref[1], NX)
+        for s in range(NX):
+
+            @pl.when(step == s)
+            def _(out_ref=out_refs[s]):
+                for h in range(GROUP):
+                    out_ref[h * DH : (h + 1) * DH, :] = done[:, h * T : (h + 1) * T]
 
     half = NH // 2
     attend(
@@ -238,9 +245,12 @@
     )
 
 
-def place_kernel(in_ref, after_ref, out_ref):
-    for g in range(KVH):
-        out_ref[:, g * GDH : (g + 1) * GDH] = in_ref[g].astype(F32).T.astype(BF16)
+def place_kernel(place_ref, *refs):
+    out_ref = refs[-1]
+    for s in range(NX):
+        g = lax.rem(place_ref[1] + (NX - s), NX)
+        cols = pl.ds(pl.multiple_of(g * GDH, 128), GDH)
+        out_ref[:, cols] = refs[s][...].astype(F32).T.astype(BF16)
 
 
 VMEM_SPEC = pl.BlockSpec(memory_space=pltpu.VMEM)
@@ -260,7 +270,7 @@
 
 
 def per_device(mixer_input, input_map, output_map, log_decay, query_rows, key_rows, value_rows):
-    place_z = lax.axis_index(("zh", "zl")).astype(jnp.int32).reshape(1)
+    place_zx = jnp.stack([lax.axis_index(("zh", "zl")), lax.axis_index("cx")]).astype(jnp.int32)
     place = lax.axis_index(("cx", "zh", "zl")).astype(jnp.int32).reshape(1)
     packed = call(pack_kernel, (KVH, GDH + 2 * DH + PIECE_ROWS, T), [VMEM_SPEC] * 4)(
         query_rows, key_rows.T, value_rows.T, log_decay.T
@@ -289,15 +299,23 @@
         out_specs=[VMEM_SPEC, VMEM_SPEC],
         scratch_shapes=bufs,
         compiler_params=pltpu.CompilerParams(vmem_limit_bytes=24 << 20),
-    )(place_z, packed, same)
+    )(place_zx, packed, same)
     prefix = call(prefix_kernel, (NCTX, PIECE_ROWS, PIECE_COLS), [SMEM_SPEC] + [VMEM_SPEC] * 5)(
         place, update, same, below, above, top
     )
     entering = lax.all_to_all(prefix, ("cx", "zh", "zl"), 0, 0)
-    attended = call(
-        attend_other_kernel, (NX, GDH, T), [SMEM_SPEC] + [VMEM_SPEC] * 5 + [ANY_SPEC], bufs, 24
-    )(place_z, packed, below, above, total, top, prefix)
-    attended = lax.all_to_all(attended, "cx", 0, 0)
+    attended = pl.pallas_call(
+        attend_other_kernel,
+        out_shape=[jax.ShapeDtypeStruct((GDH, T), BF16)] * NX,
+        in_specs=[SMEM_SPEC] + [VMEM_SPEC] * 5 + [ANY_SPEC],
+        out_specs=[VMEM_SPEC] * NX,
+        scratch_shapes=bufs,
+        compiler_params=pltpu.CompilerParams(vmem_limit_bytes=24 << 20),
+    )(place_zx, packed, below, above, total, top, prefix)
+    attended = [attended[0]] + [
+        lax.ppermute(attended[s], "cx", [(k, (k + s) % NX) for k in range(NX)])
+        for s in range(1, NX)
+    ]
     mixer_output, end = pl.pallas_call(
         mix_kernel,
         out_shape=[
@@ -308,7 +326,9 @@
         out_specs=[VMEM_SPEC] * 2,
         compiler_params=pltpu.CompilerParams(vmem_limit_bytes=12 << 20),
     )(mixer_input, input_map, output_map, log_decay.T, entering)
-    attention_output = call(place_kernel, (T, QH * DH), [VMEM_SPEC, VMEM_SPEC])(attended, end)
+    attention_output = call(
+        place_kernel, (T, QH * DH), [SMEM_SPEC] + [VMEM_SPEC] * (NX + 1)
+    )(place_zx, *attended, end)
     return mixer_output, attention_output
 
 

time: 118 us -> 115 us (0.975)
  waiting for transfers between devices: 30.8 us -> 18 us
  starting transfers between devices: 28.4 us -> 36.4 us
  Pallas kernels: 26.7 us -> 28.6 us
    ppermute x0 -> x3, starting transfers between devices: none -> 11.6 us  [per_device(): lax.ppermute(attended[s], 'cx', [(k, (k + s) % NX) for k in range(NX)])]
    all_to_all x1, waiting for transfers between devices: 7.39 us -> 0.01 us  [per_device(): entering = lax.all_to_all(prefix, ('cx', 'zh', 'zl'), 0, 0)]
    all_to_all x1 -> x0, waiting for transfers between devices: 6 us -> none  [per_device(): attended = lax.all_to_all(attended, 'cx', 0, 0)]
    all_to_all x1 -> x0, starting transfers between devices: 3.48 us -> none  [per_device(): attended = lax.all_to_all(attended, 'cx', 0, 0)]
    pallas_call x2, Pallas kernels: 10.9 us -> 12.2 us  [the longest x1 10.6 us: per_device(): pl.pallas_call(attend_other_kernel, out_shape=[jax.ShapeDtypeStruct((GDH,...]
  transfers between devices with their start and end apart: 6 -> 8, of which waited for: 4 -> 3; matrix products, arithmetic and copies ran while one was open for 1% -> 1% of each run, Pallas kernels for 18% -> 19%
where the time goes in v10:
time: 115 us; the launch traced here: 114 us
  starting transfers between devices  36.4 us (32%)
  Pallas kernels  28.6 us (25%)
  blocking collectives  23.4 us (20%)
  waiting for transfers between devices  18 us (16%)
  local copies, waits for them, and re-layouts  7.06 us (6%)
    all_gather x1, blocking collectives, per_device(): same = lax.all_gather(packed[:, GDH:, :], 'zh')  23.4 us
    ppermute x3, starting transfers between devices, per_device(): lax.ppermute(attended[s], 'cx', [(k, (k + s) % NX) for k in range(NX)])  11.6 us
    all_to_all x1, waiting for transfers between devices, per_device(): packed = lax.all_to_all(packed, 'cx', 0, 0)  11.5 us
    pallas_call x1, Pallas kernels, per_device(): pl.pallas_call(attend_other_kernel, out_shape=[jax.ShapeDtypeStruct((GDH,...  10.6 us
    pallas_call x1, Pallas kernels, per_device(): pl.pallas_call(attend_same_kernel, out_shape=[jax.ShapeDtypeStruct((NX, D...  7.49 us
    all_to_all x1, starting transfers between devices, per_device(): entering = lax.all_to_all(prefix, ('cx', 'zh', 'zl'), 0, 0)  7.45 us
    unnamed x20, local copies, waits for them, and re-layouts  6.15 us
    all_to_all x1, starting transfers between devices, per_device(): update = lax.all_to_all(update, ('cx', 'zh', 'zl'), 0, 0)  5.95 us
  transfers between devices with their start and end apart: 8, of which 3 were waited for; matrix products, arithmetic and copies ran while one was open for 1% of the time, Pallas kernels for 19%

profile of v10, /device:TPU:56, one launch (start us, length us, event | category | flops | bytes accessed | tf_op | source)
XLA Modules:
  0.0 114.2 jit_solution(14523399317133914404)
XLA Ops:
  0.6 0.0 copy-start.3
  0.6 1.1 copy-done.3
  1.7 0.0 copy-start.4
  1.7 0.7 copy-done.4
  2.4 0.0 copy-start.7
  2.5 0.9 copy-done.7
  3.3 0.0 copy-start.8
  3.3 0.9 copy-done.8
  4.2 0.0 copy-start
  4.2 0.0 copy-start.5
  4.2 0.0 copy-start.6
  4.2 1.2 %shard_map.87 = bf16[4,816,128]{2,1,0:T(8,128)(2,1)} custom-call(bf16[128,2560]{1,0:T(8,128)(2,1)S(1)} %copy-done.3, bf16[320,128]{1,0:T(8,128)(2,1)S(1)} %bitcast.15, bf16[320,128]{1,0:T(8,128)(2,1)S(1)} %bitcast.16, f32[40,128]{1,0:T(8,128)S(1)} %bitcast.12), custom_call_target="tpu_custom_call" | custom-call | tf_op jit(solution)/shard_map/pallas_call | solution.py:275
  5.4 4.3 %all-to-all-start = ((bf16[4,816,128]{2,1,0:T(8,128)(2,1)}), bf16[4,816,128]{2,1,0:T(8,128)(2,1)S(1)}, u32[]{:S(2)}, u32[]{:S(2)}) async-start(bf16[4,816,128]{2,1,0:T(8,128)(2,1)} %shard_map.87), calls=%async_computation | async-start | bytes 1671168 | tf_op jit(solution)/shard_map/all_to_all | solution.py:278
  9.7 0.0 copy-done
  9.7 0.0 copy-done.5
  9.7 0.0 copy-done.6
  9.7 1.3 %shard_map.86.in_ref = bf16[128,2560]{1,0:T(8,128)(2,1)S(1)} custom-call(bf16[128,2560]{1,0:T(8,128)(2,1)S(1)} %copy-done, bf16[128,128]{1,0:T(8,128)(2,1)S(1)} %copy-done.6, f32[40,128]{1,0:T(8,128)S(1)} %bitcast.13), custom_call_target="tpu_custom_call" | custom-call | tf_op jit(solution)/shard_map/pallas_call | solution.py:282
  11.0 11.5 %all-to-all-done.q_ref = bf16[4,816,128]{2,1,0:T(8,128)(2,1)S(1)} async-done(((bf16[4,816,128]{2,1,0:T(8,128)(2,1)}), bf16[4,816,128]{2,1,0:T(8,128)(2,1)S(1)}, u32[]{:S(2)}, u32[]{:S(2)}) %all-to-all-start) | async-done | bytes 835616 | tf_op jit(solution)/shard_map/all_to_all | solution.py:278
  22.5 23.4 %all-gather = bf16[16,176,128]{2,1,0:T(8,128)(2,1)S(1)} all-gather(bf16[4,176,128]{2,1,0:T(8,128)(2,1)S(1)} %slice.14), channel_id=2, replica_groups=mesh['dp'=16,'cx'=4,'zh'=4,'zl'=2] {'zh'}, dimensions={0}, use_global_device_ids=true | all-gather | bytes 901120 | tf_op jit(solution)/shard_map/all_gather | solution.py:279
  45.9 0.9 shard_map.88
  46.8 5.9 %all-to-all-start.1 = ((bf16[32,16,640]{2,1,0:T(8,128)(2,1)}), bf16[32,16,640]{2,1,0:T(8,128)(2,1)S(1)}, u32[]{:S(2)}, u32[]{:S(2)}) async-start(bf16[32,16,640]{2,1,0:T(8,128)(2,1)} %shard_map.88), calls=%async_computation.1 | async-start | bytes 1310720 | tf_op jit(solution)/shard_map/all_to_all | solution.py:286
  52.8 0.9 fusion
  53.7 3.7 %collective-permute-start = (bf16[2,4,176,128]{3,2,1,0:T(8,128)(2,1)}, bf16[2,4,176,128]{3,2,1,0:T(8,128)(2,1)S(1)}, u32[]{:S(2)}, u32[]{:S(2)}) collective-permute-start(bf16[2,4,176,128]{3,2,1,0:T(8,128)(2,1)} %bitcast.5), channel_id=1, source_target_pairs={{0,1},{1,2},{2,3},{3,4},{4,5},{5,6},{6,7},{7,0},{8,9},{9,10},{10,1... | collective-permute-start | bytes 1081352 | tf_op jit(solution)/shard_map/ppermute | solution.py:280
  57.4 3.4 %collective-permute-start.1 = (bf16[2,4,176,128]{3,2,1,0:T(8,128)(2,1)}, bf16[2,4,176,128]{3,2,1,0:T(8,128)(2,1)}, u32[]{:S(2)}, u32[]{:S(2)}) collective-permute-start(bf16[2,4,176,128]{3,2,1,0:T(8,128)(2,1)} %bitcast.6), channel_id=1, source_target_pairs={{0,7},{1,0},{2,1},{3,2},{4,3},{5,4},{6,5},{7,6},{8,15},{9,8},{10,9... | collective-permute-start | bytes 1081352 | tf_op jit(solution)/shard_map/ppermute | solution.py:281
  60.7 0.1 pad_add_fusion.place_ref
  60.8 7.5 %shard_map.89 = (f32[4,96,1024]{2,1,0:T(8,128)S(1)}, f32[4,1,1024]{2,1,0:T(1,128)S(1)}) custom-call(s32[2]{0:T(128)S(1)} %pad_add_fusion.place_ref, bf16[4,816,128]{2,1,0:T(8,128)(2,1)S(1)} %all-to-all-done.q_ref, bf16[4,4,176,128]{3,2,1,0:T(8,128)(2,1)S(1)} %bitcast.10), custom_call_target="tpu_custom_call" | custom-call | tf_op jit(solution)/shard_map/pallas_call | solution.py:292
  68.3 0.0 copy-start.1
  68.3 1.2 %copy-done.1 = f32[4,96,1024]{2,1,0:T(8,128)} copy-done((f32[4,96,1024]{2,1,0:T(8,128)}, f32[4,96,1024]{2,1,0:T(8,128)S(1)}, u32[]{:S(2)}) %copy-start.1) | copy-done | bytes 1572888
  69.5 5.3 %collective-permute-done.below_ref = bf16[2,4,176,128]{3,2,1,0:T(8,128)(2,1)S(1)} collective-permute-done((bf16[2,4,176,128]{3,2,1,0:T(8,128)(2,1)}, bf16[2,4,176,128]{3,2,1,0:T(8,128)(2,1)S(1)}, u32[]{:S(2)}, u32[]{:S(2)}) %collective-permute-start) | collective-permute-done | bytes 360480 | tf_op jit(solution)/shard_map/ppermute | solution.py:280
  74.8 0.0 collective-permute-done.1.above_ref
  74.8 0.0 all-to-all-done.1.in_ref
  74.8 2.8 %shard_map.90.after_ref = bf16[32,16,640]{2,1,0:T(8,128)(2,1)} custom-call(s32[1]{0:T(128)} %bitcast.1.place_ref, bf16[32,16,640]{2,1,0:T(8,128)(2,1)S(1)} %all-to-all-done.1.in_ref, bf16[4,4,176,128]{3,2,1,0:T(8,128)(2,1)S(1)} %bitcast.11, bf16[2,4,176,128]{3,2,1,0:T(8,128)(2,1)S(1)} %collective-permute-done.below_ref, ...), custom_call_target="tpu_custom_call" | custom-call | tf_op jit(solution)/shard_map/pallas_call | solution.py:303
  77.6 7.5 %all-to-all-start.2 = ((bf16[32,16,640]{2,1,0:T(8,128)(2,1)}), bf16[32,16,640]{2,1,0:T(8,128)(2,1)S(1)}, u32[]{:S(2)}, u32[]{:S(2)}) async-start(bf16[32,16,640]{2,1,0:T(8,128)(2,1)} %shard_map.90.after_ref), calls=%async_computation.2 | async-start | bytes 1310720 | tf_op jit(solution)/shard_map/all_to_all | solution.py:306
  85.0 0.0 copy-start.2
  85.1 1.4 %copy-done.2 = f32[4,96,1024]{2,1,0:T(8,128)S(1)} copy-done((f32[4,96,1024]{2,1,0:T(8,128)S(1)}, f32[4,96,1024]{2,1,0:T(8,128)}, u32[]{:S(2)}) %copy-start.2) | copy-done | bytes 1572888
  86.5 0.0 copy-start.9
  86.5 10.6 %shard_map.92 = (bf16[640,128]{1,0:T(8,128)(2,1)S(1)}, bf16[640,128]{1,0:T(8,128)(2,1)}, bf16[640,128]{1,0:T(8,128)(2,1)}, bf16[640,128]{1,0:T(8,128)(2,1)S(1)}) custom-call(s32[2]{0:T(128)S(1)} %pad_add_fusion.place_ref, bf16[4,816,128]{2,1,0:T(8,128)(2,1)S(1)} %all-to-all-done.q_ref, bf16[2,4,176,128]{3,2,1,0:T(8,128)(2,1)S(1)} %collective-permute-done.below_ref, ...), custom_call_target="tpu_custom_call" | custom-call | tf_op jit(solution)/shard_map/pallas_call | solution.py:307
  97.0 3.7 %collective-permute-start.2 = (bf16[640,128]{1,0:T(8,128)(2,1)}, bf16[640,128]{1,0:T(8,128)(2,1)S(1)}, u32[]{:S(2)}, u32[]{:S(2)}) collective-permute-start(bf16[640,128]{1,0:T(8,128)(2,1)} %get-tuple-element.14), channel_id=1, source_target_pairs={{0,8},{8,16},{16,24},{24,0},{1,9},{9,17},{17,25},{25,1},{2,10},{10... | collective-permute-start | bytes 491528 | tf_op jit(solution)/shard_map/ppermute | solution.py:316
  100.7 4.6 %collective-permute-start.3 = (bf16[640,128]{1,0:T(8,128)(2,1)}, bf16[640,128]{1,0:T(8,128)(2,1)S(1)}, u32[]{:S(2)}, u32[]{:S(2)}) collective-permute-start(bf16[640,128]{1,0:T(8,128)(2,1)} %get-tuple-element.15), channel_id=1, source_target_pairs={{0,16},{8,24},{16,0},{24,8},{1,17},{9,25},{17,1},{25,9},{2,18},{10... | collective-permute-start | bytes 491528 | tf_op jit(solution)/shard_map/ppermute | solution.py:316
  105.4 3.3 %collective-permute-start.4 = (bf16[640,128]{1,0:T(8,128)(2,1)S(1)}, bf16[640,128]{1,0:T(8,128)(2,1)S(1)}, u32[]{:S(2)}, u32[]{:S(2)}) collective-permute-start(bf16[640,128]{1,0:T(8,128)(2,1)S(1)} %get-tuple-element.16), channel_id=1, source_target_pairs={{0,24},{8,0},{16,8},{24,16},{1,25},{9,1},{17,9},{25,17},{2,26},{10... | collective-permute-start | bytes 491528 | tf_op jit(solution)/shard_map/ppermute | solution.py:316
  108.7 0.0 all-to-all-done.2.enter_ref
  108.7 0.0 copy-done.9
  108.7 2.7 %shard_map.91 = (bf16[128,2560]{1,0:T(8,128)(2,1)}, f32[8,128]{1,0:T(8,128)S(1)}) custom-call(bf16[128,2560]{1,0:T(8,128)(2,1)S(1)} %copy-done, bf16[128,128]{1,0:T(8,128)(2,1)S(1)} %copy-done.6, bf16[128,128]{1,0:T(8,128)(2,1)S(1)} %copy-done.9, f32[40,128]{1,0:T(8,128)S(1)} %bitcast.14, bf16[32,16,640]{2,1,0:T(8,128)(2,1)S(1)} %all-to-all-done.2.enter_ref), custom_call_target="tpu_custom_call" | custom-call | tf_op jit(solution)/shard_map/pallas_call | solution.py:319
  111.5 0.0 collective-permute-done.2.refs_1_
  111.5 0.0 collective-permute-done.3.refs_2_
  111.5 1.1 collective-permute-done.4.refs_3_
  112.6 1.6 %shard_map.93 = bf16[128,2560]{1,0:T(8,128)(2,1)} custom-call(s32[2]{0:T(128)S(1)} %pad_add_fusion.place_ref, bf16[640,128]{1,0:T(8,128)(2,1)S(1)} %get-tuple-element.13.refs_0_, bf16[640,128]{1,0:T(8,128)(2,1)S(1)} %collective-permute-done.2.refs_1_, bf16[640,128]{1,0:T(8,128)(2,1)S(1)} %collective-permute-done.3.refs_2_, ...), custom_call_target="tpu_custom_call" | custom-call | tf_op jit(solution)/shard_map/pallas_call | solution.py:329
  (1 shorter events, 0.0 us)
Async XLA Ops:
  0.6 1.1 copy-start.3
  1.7 0.7 copy-start.4
  2.4 0.9 copy-start.7
  3.3 0.9 copy-start.8
  4.2 5.5 %copy-start = (bf16[128,2560]{1,0:T(8,128)(2,1)S(1)}, bf16[128,2560]{1,0:T(8,128)(2,1)}, u32[]{:S(2)}) copy-start(bf16[128,2560]{1,0:T(8,128)(2,1)} %x_ref.3) | copy-start | bytes 1966084
  4.2 5.5 %copy-start.5 = (f32[128,40]{0,1:T(8,128)S(1)}, f32[128,40]{0,1:T(8,128)}, u32[]{:S(2)}) copy-start(f32[128,40]{0,1:T(8,128)} %param.10) | copy-start | bytes 61444
  4.2 5.5 %copy-start.6 = (bf16[128,128]{1,0:T(8,128)(2,1)S(1)}, bf16[128,128]{1,0:T(8,128)(2,1)}, u32[]{:S(2)}) copy-start(bf16[128,128]{1,0:T(8,128)(2,1)} %in_ref.3) | copy-start | bytes 98308
  5.4 17.1 %all-to-all-start = ((bf16[4,816,128]{2,1,0:T(8,128)(2,1)}), bf16[4,816,128]{2,1,0:T(8,128)(2,1)S(1)}, u32[]{:S(2)}, u32[]{:S(2)}) async-start(bf16[4,816,128]{2,1,0:T(8,128)(2,1)} %shard_map.87), calls=%async_computation | async-start | bytes 1671168 | tf_op jit(solution)/shard_map/all_to_all | solution.py:278
  46.8 28.0 %all-to-all-start.1 = ((bf16[32,16,640]{2,1,0:T(8,128)(2,1)}), bf16[32,16,640]{2,1,0:T(8,128)(2,1)S(1)}, u32[]{:S(2)}, u32[]{:S(2)}) async-start(bf16[32,16,640]{2,1,0:T(8,128)(2,1)} %shard_map.88), calls=%async_computation.1 | async-start | bytes 1310720 | tf_op jit(solution)/shard_map/all_to_all | solution.py:286
  53.7 21.1 %collective-permute-start = (bf16[2,4,176,128]{3,2,1,0:T(8,128)(2,1)}, bf16[2,4,176,128]{3,2,1,0:T(8,128)(2,1)S(1)}, u32[]{:S(2)}, u32[]{:S(2)}) collective-permute-start(bf16[2,4,176,128]{3,2,1,0:T(8,128)(2,1)} %bitcast.5), channel_id=1, source_target_pairs={{0,1},{1,2},{2,3},{3,4},{4,5},{5,6},{6,7},{7,0},{8,9},{9,10},{10,1... | collective-permute-start | bytes 1081352 | tf_op jit(solution)/shard_map/ppermute | solution.py:280
  57.4 17.4 %collective-permute-start.1 = (bf16[2,4,176,128]{3,2,1,0:T(8,128)(2,1)}, bf16[2,4,176,128]{3,2,1,0:T(8,128)(2,1)}, u32[]{:S(2)}, u32[]{:S(2)}) collective-permute-start(bf16[2,4,176,128]{3,2,1,0:T(8,128)(2,1)} %bitcast.6), channel_id=1, source_target_pairs={{0,7},{1,0},{2,1},{3,2},{4,3},{5,4},{6,5},{7,6},{8,15},{9,8},{10,9... | collective-permute-start | bytes 1081352 | tf_op jit(solution)/shard_map/ppermute | solution.py:281
  68.3 1.2 %copy-start.1 = (f32[4,96,1024]{2,1,0:T(8,128)}, f32[4,96,1024]{2,1,0:T(8,128)S(1)}, u32[]{:S(2)}) copy-start(f32[4,96,1024]{2,1,0:T(8,128)S(1)} %get-tuple-element.12.total_ref) | copy-start | bytes 4718596
  77.6 31.1 %all-to-all-start.2 = ((bf16[32,16,640]{2,1,0:T(8,128)(2,1)}), bf16[32,16,640]{2,1,0:T(8,128)(2,1)S(1)}, u32[]{:S(2)}, u32[]{:S(2)}) async-start(bf16[32,16,640]{2,1,0:T(8,128)(2,1)} %shard_map.90.after_ref), calls=%async_computation.2 | async-start | bytes 1310720 | tf_op jit(solution)/shard_map/all_to_all | solution.py:306
  85.0 1.4 %copy-start.2 = (f32[4,96,1024]{2,1,0:T(8,128)S(1)}, f32[4,96,1024]{2,1,0:T(8,128)}, u32[]{:S(2)}) copy-start(f32[4,96,1024]{2,1,0:T(8,128)} %copy-done.1) | copy-start | bytes 4718596
  86.5 22.3 %copy-start.9 = (bf16[128,128]{1,0:T(8,128)(2,1)S(1)}, bf16[128,128]{1,0:T(8,128)(2,1)}, u32[]{:S(2)}) copy-start(bf16[128,128]{1,0:T(8,128)(2,1)} %map_ref.1) | copy-start | bytes 98308
  97.0 14.4 %collective-permute-start.2 = (bf16[640,128]{1,0:T(8,128)(2,1)}, bf16[640,128]{1,0:T(8,128)(2,1)S(1)}, u32[]{:S(2)}, u32[]{:S(2)}) collective-permute-start(bf16[640,128]{1,0:T(8,128)(2,1)} %get-tuple-element.14), channel_id=1, source_target_pairs={{0,8},{8,16},{16,24},{24,0},{1,9},{9,17},{17,25},{25,1},{2,10},{10... | collective-permute-start | bytes 491528 | tf_op jit(solution)/shard_map/ppermute | solution.py:316
  100.7 10.7 %collective-permute-start.3 = (bf16[640,128]{1,0:T(8,128)(2,1)}, bf16[640,128]{1,0:T(8,128)(2,1)S(1)}, u32[]{:S(2)}, u32[]{:S(2)}) collective-permute-start(bf16[640,128]{1,0:T(8,128)(2,1)} %get-tuple-element.15), channel_id=1, source_target_pairs={{0,16},{8,24},{16,0},{24,8},{1,17},{9,25},{17,1},{25,9},{2,18},{10... | collective-permute-start | bytes 491528 | tf_op jit(solution)/shard_map/ppermute | solution.py:316
  105.4 7.2 %collective-permute-start.4 = (bf16[640,128]{1,0:T(8,128)(2,1)S(1)}, bf16[640,128]{1,0:T(8,128)(2,1)S(1)}, u32[]{:S(2)}, u32[]{:S(2)}) collective-permute-start(bf16[640,128]{1,0:T(8,128)(2,1)S(1)} %get-tuple-element.16), channel_id=1, source_target_pairs={{0,24},{8,0},{16,8},{24,16},{1,25},{9,1},{17,9},{25,17},{2,26},{10... | collective-permute-start | bytes 491528 | tf_op jit(solution)/shard_map/ppermute | solution.py:316

commit v11 on v10

--- a/solution.py
+++ b/solution.py
@@ -130,7 +130,17 @@
 KEYS = NH * T
 
 
-def pack_kernel(q_ref, k_ref, v_ref, decay_ref, out_ref):
+def pack_kernel(q_hbm, k_hbm, v_hbm, decay_hbm, out_ref, q_ref, k_ref, v_ref, decay_ref, sems):
+    copies = [
+        pltpu.make_async_copy(decay_hbm, decay_ref, sems.at[0]),
+        pltpu.make_async_copy(k_hbm, k_ref, sems.at[1]),
+        pltpu.make_async_copy(v_hbm, v_ref, sems.at[2]),
+        pltpu.make_async_copy(q_hbm, q_ref, sems.at[3]),
+    ]
+    for copy in copies:
+        copy.start()
+    for copy in copies:
+        copy.wait()
     total = lax.dot_general(
         jnp.ones((PIECE_ROWS, T), F32),
         decay_ref[...],
@@ -256,6 +266,14 @@
 VMEM_SPEC = pl.BlockSpec(memory_space=pltpu.VMEM)
 SMEM_SPEC = pl.BlockSpec(memory_space=pltpu.SMEM)
 ANY_SPEC = pl.BlockSpec(memory_space=pl.ANY)
+HBM_SPEC = pl.BlockSpec(memory_space=pltpu.HBM)
+PACK_BUFS = [
+    pltpu.VMEM((T, QH * DH), BF16),
+    pltpu.VMEM((KVH * DH, T), BF16),
+    pltpu.VMEM((KVH * DH, T), BF16),
+    pltpu.VMEM((MIXER_HEADS, T), F32),
+    pltpu.SemaphoreType.DMA((4,)),
+]
 
 
 def call(kernel, shape, specs, scratch=(), limit=12):
@@ -272,7 +290,7 @@
 def per_device(mixer_input, input_map, output_map, log_decay, query_rows, key_rows, value_rows):
     place_zx = jnp.stack([lax.axis_index(("zh", "zl")), lax.axis_index("cx")]).astype(jnp.int32)
     place = lax.axis_index(("cx", "zh", "zl")).astype(jnp.int32).reshape(1)
-    packed = call(pack_kernel, (KVH, GDH + 2 * DH + PIECE_ROWS, T), [VMEM_SPEC] * 4)(
+    packed = call(pack_kernel, (KVH, GDH + 2 * DH + PIECE_ROWS, T), [HBM_SPEC] * 4, PACK_BUFS, 62)(
         query_rows, key_rows.T, value_rows.T, log_decay.T
     )
     packed = lax.all_to_all(packed, "cx", 0, 0)

time: 115 us -> 113 us (0.983)
  local copies, waits for them, and re-layouts: 7.06 us -> 3.52 us
  Pallas kernels: 28.6 us -> 30 us
    unnamed x20 -> x12, local copies, waits for them, and re-layouts: 6.15 us -> 2.59 us
    pallas_call x1, Pallas kernels: 1.19 us -> 2.47 us  [per_device(): call(pack_kernel, (KVH, GDH + 2 * DH + PIECE_ROWS, T), [HBM_SPEC] * 4, PA...]
  transfers between devices with their start and end apart: 8 -> 8, of which waited for: 3 -> 3; matrix products, arithmetic and copies ran while one was open for 1% -> 1% of each run, Pallas kernels for 19% -> 20%
where the time goes in v11:
time: 113 us; the launch traced here: 112 us
  starting transfers between devices  36.4 us (32%)
  Pallas kernels  30 us (27%)
  blocking collectives  23.4 us (21%)
  waiting for transfers between devices  17.8 us (16%)
  local copies, waits for them, and re-layouts  3.52 us (3%)
    all_gather x1, blocking collectives, per_device(): same = lax.all_gather(packed[:, GDH:, :], 'zh')  23.4 us
    ppermute x3, starting transfers between devices, per_device(): lax.ppermute(attended[s], 'cx', [(k, (k + s) % NX) for k in range(NX)])  11.7 us
    all_to_all x1, waiting for transfers between devices, per_device(): packed = lax.all_to_all(packed, 'cx', 0, 0)  11.5 us
    pallas_call x1, Pallas kernels, per_device(): pl.pallas_call(attend_other_kernel, out_shape=[jax.ShapeDtypeStruct((GDH,...  10.6 us
    pallas_call x1, Pallas kernels, per_device(): pl.pallas_call(attend_same_kernel, out_shape=[jax.ShapeDtypeStruct((NX, D...  7.54 us
    all_to_all x1, starting transfers between devices, per_device(): entering = lax.all_to_all(prefix, ('cx', 'zh', 'zl'), 0, 0)  7.45 us
    all_to_all x1, starting transfers between devices, per_device(): update = lax.all_to_all(update, ('cx', 'zh', 'zl'), 0, 0)  5.95 us
    ppermute x1, waiting for transfers between devices, per_device(): lax.ppermute(same[:NH // 2], ('zh', 'zl'), [(k, (k + 1) % NZ) for k in ra...  5.23 us
  transfers between devices with their start and end apart: 8, of which 3 were waited for; matrix products, arithmetic and copies ran while one was open for 1% of the time, Pallas kernels for 20%

profile of v11, /device:TPU:56, one launch (start us, length us, event | category | flops | bytes accessed | tf_op | source)
XLA Modules:
  0.0 112.0 jit_solution(10461288675053452083)
XLA Ops:
  0.6 0.0 copy-start
  0.6 0.0 copy-start.3
  0.7 0.0 copy-start.4
  0.7 2.5 %shard_map.87 = bf16[4,816,128]{2,1,0:T(8,128)(2,1)} custom-call(bf16[128,2560]{1,0:T(8,128)(2,1)} %q_hbm.1, bf16[320,128]{1,0:T(8,128)(2,1)} %bitcast.15, bf16[320,128]{1,0:T(8,128)(2,1)} %bitcast.16, f32[40,128]{1,0:T(8,128)} %bitcast.12), custom_call_target="tpu_custom_call" | custom-call | tf_op jit(solution)/shard_map/pallas_call | solution.py:293
  3.1 4.3 %all-to-all-start = ((bf16[4,816,128]{2,1,0:T(8,128)(2,1)}), bf16[4,816,128]{2,1,0:T(8,128)(2,1)S(1)}, u32[]{:S(2)}, u32[]{:S(2)}) async-start(bf16[4,816,128]{2,1,0:T(8,128)(2,1)} %shard_map.87), calls=%async_computation | async-start | bytes 1671168 | tf_op jit(solution)/shard_map/all_to_all | solution.py:296
  7.4 0.0 copy-done
  7.4 0.0 copy-done.3
  7.5 0.0 copy-done.4
  7.5 1.3 %shard_map.86.in_ref = bf16[128,2560]{1,0:T(8,128)(2,1)S(1)} custom-call(bf16[128,2560]{1,0:T(8,128)(2,1)S(1)} %copy-done, bf16[128,128]{1,0:T(8,128)(2,1)S(1)} %copy-done.4, f32[40,128]{1,0:T(8,128)S(1)} %bitcast.13), custom_call_target="tpu_custom_call" | custom-call | tf_op jit(solution)/shard_map/pallas_call | solution.py:300
  8.7 11.5 %all-to-all-done.q_ref = bf16[4,816,128]{2,1,0:T(8,128)(2,1)S(1)} async-done(((bf16[4,816,128]{2,1,0:T(8,128)(2,1)}), bf16[4,816,128]{2,1,0:T(8,128)(2,1)S(1)}, u32[]{:S(2)}, u32[]{:S(2)}) %all-to-all-start) | async-done | bytes 835616 | tf_op jit(solution)/shard_map/all_to_all | solution.py:296
  20.3 23.4 %all-gather = bf16[16,176,128]{2,1,0:T(8,128)(2,1)S(1)} all-gather(bf16[4,176,128]{2,1,0:T(8,128)(2,1)S(1)} %slice.14), channel_id=2, replica_groups=mesh['dp'=16,'cx'=4,'zh'=4,'zl'=2] {'zh'}, dimensions={0}, use_global_device_ids=true | all-gather | bytes 901120 | tf_op jit(solution)/shard_map/all_gather | solution.py:297
  43.6 0.9 shard_map.88
  44.5 5.9 %all-to-all-start.1 = ((bf16[32,16,640]{2,1,0:T(8,128)(2,1)}), bf16[32,16,640]{2,1,0:T(8,128)(2,1)S(1)}, u32[]{:S(2)}, u32[]{:S(2)}) async-start(bf16[32,16,640]{2,1,0:T(8,128)(2,1)} %shard_map.88), calls=%async_computation.1 | async-start | bytes 1310720 | tf_op jit(solution)/shard_map/all_to_all | solution.py:304
  50.5 0.9 fusion
  51.4 3.7 %collective-permute-start = (bf16[2,4,176,128]{3,2,1,0:T(8,128)(2,1)}, bf16[2,4,176,128]{3,2,1,0:T(8,128)(2,1)S(1)}, u32[]{:S(2)}, u32[]{:S(2)}) collective-permute-start(bf16[2,4,176,128]{3,2,1,0:T(8,128)(2,1)} %bitcast.5), channel_id=1, source_target_pairs={{0,1},{1,2},{2,3},{3,4},{4,5},{5,6},{6,7},{7,0},{8,9},{9,10},{10,1... | collective-permute-start | bytes 1081352 | tf_op jit(solution)/shard_map/ppermute | solution.py:298
  55.1 3.4 %collective-permute-start.1 = (bf16[2,4,176,128]{3,2,1,0:T(8,128)(2,1)}, bf16[2,4,176,128]{3,2,1,0:T(8,128)(2,1)}, u32[]{:S(2)}, u32[]{:S(2)}) collective-permute-start(bf16[2,4,176,128]{3,2,1,0:T(8,128)(2,1)} %bitcast.6), channel_id=1, source_target_pairs={{0,7},{1,0},{2,1},{3,2},{4,3},{5,4},{6,5},{7,6},{8,15},{9,8},{10,9... | collective-permute-start | bytes 1081352 | tf_op jit(solution)/shard_map/ppermute | solution.py:299
  58.5 0.1 pad_add_fusion.place_ref
  58.6 7.5 %shard_map.89 = (f32[4,96,1024]{2,1,0:T(8,128)S(1)}, f32[4,1,1024]{2,1,0:T(1,128)S(1)}) custom-call(s32[2]{0:T(128)S(1)} %pad_add_fusion.place_ref, bf16[4,816,128]{2,1,0:T(8,128)(2,1)S(1)} %all-to-all-done.q_ref, bf16[4,4,176,128]{3,2,1,0:T(8,128)(2,1)S(1)} %bitcast.10), custom_call_target="tpu_custom_call" | custom-call | tf_op jit(solution)/shard_map/pallas_call | solution.py:310
  66.1 0.0 copy-start.1
  66.1 1.2 %copy-done.1 = f32[4,96,1024]{2,1,0:T(8,128)} copy-done((f32[4,96,1024]{2,1,0:T(8,128)}, f32[4,96,1024]{2,1,0:T(8,128)S(1)}, u32[]{:S(2)}) %copy-start.1) | copy-done | bytes 1572888
  67.3 5.2 %collective-permute-done.below_ref = bf16[2,4,176,128]{3,2,1,0:T(8,128)(2,1)S(1)} collective-permute-done((bf16[2,4,176,128]{3,2,1,0:T(8,128)(2,1)}, bf16[2,4,176,128]{3,2,1,0:T(8,128)(2,1)S(1)}, u32[]{:S(2)}, u32[]{:S(2)}) %collective-permute-start) | collective-permute-done | bytes 360480 | tf_op jit(solution)/shard_map/ppermute | solution.py:298
  72.5 0.0 collective-permute-done.1.above_ref
  72.5 0.0 all-to-all-done.1.in_ref
  72.5 2.8 %shard_map.90.after_ref = bf16[32,16,640]{2,1,0:T(8,128)(2,1)} custom-call(s32[1]{0:T(128)} %bitcast.1.place_ref, bf16[32,16,640]{2,1,0:T(8,128)(2,1)S(1)} %all-to-all-done.1.in_ref, bf16[4,4,176,128]{3,2,1,0:T(8,128)(2,1)S(1)} %bitcast.11, bf16[2,4,176,128]{3,2,1,0:T(8,128)(2,1)S(1)} %collective-permute-done.below_ref, ...), custom_call_target="tpu_custom_call" | custom-call | tf_op jit(solution)/shard_map/pallas_call | solution.py:321
  75.3 7.5 %all-to-all-start.2 = ((bf16[32,16,640]{2,1,0:T(8,128)(2,1)}), bf16[32,16,640]{2,1,0:T(8,128)(2,1)S(1)}, u32[]{:S(2)}, u32[]{:S(2)}) async-start(bf16[32,16,640]{2,1,0:T(8,128)(2,1)} %shard_map.90.after_ref), calls=%async_computation.2 | async-start | bytes 1310720 | tf_op jit(solution)/shard_map/all_to_all | solution.py:324
  82.8 0.0 copy-start.2
  82.8 1.4 %copy-done.2 = f32[4,96,1024]{2,1,0:T(8,128)S(1)} copy-done((f32[4,96,1024]{2,1,0:T(8,128)S(1)}, f32[4,96,1024]{2,1,0:T(8,128)}, u32[]{:S(2)}) %copy-start.2) | copy-done | bytes 1572888
  84.2 0.0 copy-start.5
  84.2 10.6 %shard_map.92 = (bf16[640,128]{1,0:T(8,128)(2,1)S(1)}, bf16[640,128]{1,0:T(8,128)(2,1)}, bf16[640,128]{1,0:T(8,128)(2,1)}, bf16[640,128]{1,0:T(8,128)(2,1)S(1)}) custom-call(s32[2]{0:T(128)S(1)} %pad_add_fusion.place_ref, bf16[4,816,128]{2,1,0:T(8,128)(2,1)S(1)} %all-to-all-done.q_ref, bf16[2,4,176,128]{3,2,1,0:T(8,128)(2,1)S(1)} %collective-permute-done.below_ref, ...), custom_call_target="tpu_custom_call" | custom-call | tf_op jit(solution)/shard_map/pallas_call | solution.py:325
  94.8 3.7 %collective-permute-start.2 = (bf16[640,128]{1,0:T(8,128)(2,1)}, bf16[640,128]{1,0:T(8,128)(2,1)S(1)}, u32[]{:S(2)}, u32[]{:S(2)}) collective-permute-start(bf16[640,128]{1,0:T(8,128)(2,1)} %get-tuple-element.14), channel_id=1, source_target_pairs={{0,8},{8,16},{16,24},{24,0},{1,9},{9,17},{17,25},{25,1},{2,10},{10... | collective-permute-start | bytes 491528 | tf_op jit(solution)/shard_map/ppermute | solution.py:334
  98.5 4.6 %collective-permute-start.3 = (bf16[640,128]{1,0:T(8,128)(2,1)}, bf16[640,128]{1,0:T(8,128)(2,1)S(1)}, u32[]{:S(2)}, u32[]{:S(2)}) collective-permute-start(bf16[640,128]{1,0:T(8,128)(2,1)} %get-tuple-element.15), channel_id=1, source_target_pairs={{0,16},{8,24},{16,0},{24,8},{1,17},{9,25},{17,1},{25,9},{2,18},{10... | collective-permute-start | bytes 491528 | tf_op jit(solution)/shard_map/ppermute | solution.py:334
  103.1 3.3 %collective-permute-start.4 = (bf16[640,128]{1,0:T(8,128)(2,1)S(1)}, bf16[640,128]{1,0:T(8,128)(2,1)S(1)}, u32[]{:S(2)}, u32[]{:S(2)}) collective-permute-start(bf16[640,128]{1,0:T(8,128)(2,1)S(1)} %get-tuple-element.16), channel_id=1, source_target_pairs={{0,24},{8,0},{16,8},{24,16},{1,25},{9,1},{17,9},{25,17},{2,26},{10... | collective-permute-start | bytes 491528 | tf_op jit(solution)/shard_map/ppermute | solution.py:334
  106.5 0.0 all-to-all-done.2.enter_ref
  106.5 0.0 copy-done.5
  106.5 2.7 %shard_map.91 = (bf16[128,2560]{1,0:T(8,128)(2,1)}, f32[8,128]{1,0:T(8,128)S(1)}) custom-call(bf16[128,2560]{1,0:T(8,128)(2,1)S(1)} %copy-done, bf16[128,128]{1,0:T(8,128)(2,1)S(1)} %copy-done.4, bf16[128,128]{1,0:T(8,128)(2,1)S(1)} %copy-done.5, f32[40,128]{1,0:T(8,128)S(1)} %bitcast.14, bf16[32,16,640]{2,1,0:T(8,128)(2,1)S(1)} %all-to-all-done.2.enter_ref), custom_call_target="tpu_custom_call" | custom-call | tf_op jit(solution)/shard_map/pallas_call | solution.py:337
  109.2 0.0 collective-permute-done.2.refs_1_
  109.3 0.0 collective-permute-done.3.refs_2_
  109.3 1.1 collective-permute-done.4.refs_3_
  110.3 1.6 %shard_map.93 = bf16[128,2560]{1,0:T(8,128)(2,1)} custom-call(s32[2]{0:T(128)S(1)} %pad_add_fusion.place_ref, bf16[640,128]{1,0:T(8,128)(2,1)S(1)} %get-tuple-element.13.refs_0_, bf16[640,128]{1,0:T(8,128)(2,1)S(1)} %collective-permute-done.2.refs_1_, bf16[640,128]{1,0:T(8,128)(2,1)S(1)} %collective-permute-done.3.refs_2_, ...), custom_call_target="tpu_custom_call" | custom-call | tf_op jit(solution)/shard_map/pallas_call | solution.py:347
  (1 shorter events, 0.0 us)
Async XLA Ops:
  0.6 6.8 %copy-start = (bf16[128,2560]{1,0:T(8,128)(2,1)S(1)}, bf16[128,2560]{1,0:T(8,128)(2,1)}, u32[]{:S(2)}) copy-start(bf16[128,2560]{1,0:T(8,128)(2,1)} %x_ref.3) | copy-start | bytes 1966084
  0.6 6.8 %copy-start.3 = (f32[128,40]{0,1:T(8,128)S(1)}, f32[128,40]{0,1:T(8,128)}, u32[]{:S(2)}) copy-start(f32[128,40]{0,1:T(8,128)} %param.10) | copy-start | bytes 61444
  0.7 6.8 %copy-start.4 = (bf16[128,128]{1,0:T(8,128)(2,1)S(1)}, bf16[128,128]{1,0:T(8,128)(2,1)}, u32[]{:S(2)}) copy-start(bf16[128,128]{1,0:T(8,128)(2,1)} %in_ref.3) | copy-start | bytes 98308
  3.1 17.1 %all-to-all-start = ((bf16[4,816,128]{2,1,0:T(8,128)(2,1)}), bf16[4,816,128]{2,1,0:T(8,128)(2,1)S(1)}, u32[]{:S(2)}, u32[]{:S(2)}) async-start(bf16[4,816,128]{2,1,0:T(8,128)(2,1)} %shard_map.87), calls=%async_computation | async-start | bytes 1671168 | tf_op jit(solution)/shard_map/all_to_all | solution.py:296
  44.5 28.0 %all-to-all-start.1 = ((bf16[32,16,640]{2,1,0:T(8,128)(2,1)}), bf16[32,16,640]{2,1,0:T(8,128)(2,1)S(1)}, u32[]{:S(2)}, u32[]{:S(2)}) async-start(bf16[32,16,640]{2,1,0:T(8,128)(2,1)} %shard_map.88), calls=%async_computation.1 | async-start | bytes 1310720 | tf_op jit(solution)/shard_map/all_to_all | solution.py:304
  51.4 21.1 %collective-permute-start = (bf16[2,4,176,128]{3,2,1,0:T(8,128)(2,1)}, bf16[2,4,176,128]{3,2,1,0:T(8,128)(2,1)S(1)}, u32[]{:S(2)}, u32[]{:S(2)}) collective-permute-start(bf16[2,4,176,128]{3,2,1,0:T(8,128)(2,1)} %bitcast.5), channel_id=1, source_target_pairs={{0,1},{1,2},{2,3},{3,4},{4,5},{5,6},{6,7},{7,0},{8,9},{9,10},{10,1... | collective-permute-start | bytes 1081352 | tf_op jit(solution)/shard_map/ppermute | solution.py:298
  55.1 17.4 %collective-permute-start.1 = (bf16[2,4,176,128]{3,2,1,0:T(8,128)(2,1)}, bf16[2,4,176,128]{3,2,1,0:T(8,128)(2,1)}, u32[]{:S(2)}, u32[]{:S(2)}) collective-permute-start(bf16[2,4,176,128]{3,2,1,0:T(8,128)(2,1)} %bitcast.6), channel_id=1, source_target_pairs={{0,7},{1,0},{2,1},{3,2},{4,3},{5,4},{6,5},{7,6},{8,15},{9,8},{10,9... | collective-permute-start | bytes 1081352 | tf_op jit(solution)/shard_map/ppermute | solution.py:299
  66.1 1.2 %copy-start.1 = (f32[4,96,1024]{2,1,0:T(8,128)}, f32[4,96,1024]{2,1,0:T(8,128)S(1)}, u32[]{:S(2)}) copy-start(f32[4,96,1024]{2,1,0:T(8,128)S(1)} %get-tuple-element.12.total_ref) | copy-start | bytes 4718596
  75.3 31.2 %all-to-all-start.2 = ((bf16[32,16,640]{2,1,0:T(8,128)(2,1)}), bf16[32,16,640]{2,1,0:T(8,128)(2,1)S(1)}, u32[]{:S(2)}, u32[]{:S(2)}) async-start(bf16[32,16,640]{2,1,0:T(8,128)(2,1)} %shard_map.90.after_ref), calls=%async_computation.2 | async-start | bytes 1310720 | tf_op jit(solution)/shard_map/all_to_all | solution.py:324
  82.8 1.4 %copy-start.2 = (f32[4,96,1024]{2,1,0:T(8,128)S(1)}, f32[4,96,1024]{2,1,0:T(8,128)}, u32[]{:S(2)}) copy-start(f32[4,96,1024]{2,1,0:T(8,128)} %copy-done.1) | copy-start | bytes 4718596
  84.2 22.3 %copy-start.5 = (bf16[128,128]{1,0:T(8,128)(2,1)S(1)}, bf16[128,128]{1,0:T(8,128)(2,1)}, u32[]{:S(2)}) copy-start(bf16[128,128]{1,0:T(8,128)(2,1)} %map_ref.1) | copy-start | bytes 98308
  94.8 14.4 %collective-permute-start.2 = (bf16[640,128]{1,0:T(8,128)(2,1)}, bf16[640,128]{1,0:T(8,128)(2,1)S(1)}, u32[]{:S(2)}, u32[]{:S(2)}) collective-permute-start(bf16[640,128]{1,0:T(8,128)(2,1)} %get-tuple-element.14), channel_id=1, source_target_pairs={{0,8},{8,16},{16,24},{24,0},{1,9},{9,17},{17,25},{25,1},{2,10},{10... | collective-permute-start | bytes 491528 | tf_op jit(solution)/shard_map/ppermute | solution.py:334
  98.5 10.7 %collective-permute-start.3 = (bf16[640,128]{1,0:T(8,128)(2,1)}, bf16[640,128]{1,0:T(8,128)(2,1)S(1)}, u32[]{:S(2)}, u32[]{:S(2)}) collective-permute-start(bf16[640,128]{1,0:T(8,128)(2,1)} %get-tuple-element.15), channel_id=1, source_target_pairs={{0,16},{8,24},{16,0},{24,8},{1,17},{9,25},{17,1},{25,9},{2,18},{10... | collective-permute-start | bytes 491528 | tf_op jit(solution)/shard_map/ppermute | solution.py:334
  103.1 7.2 %collective-permute-start.4 = (bf16[640,128]{1,0:T(8,128)(2,1)S(1)}, bf16[640,128]{1,0:T(8,128)(2,1)S(1)}, u32[]{:S(2)}, u32[]{:S(2)}) collective-permute-start(bf16[640,128]{1,0:T(8,128)(2,1)S(1)} %get-tuple-element.16), channel_id=1, source_target_pairs={{0,24},{8,0},{16,8},{24,16},{1,25},{9,1},{17,9},{25,17},{2,26},{10... | collective-permute-start | bytes 491528 | tf_op jit(solution)/shard_map/ppermute | solution.py:334

commit v12 on v11

--- a/solution.py
+++ b/solution.py
@@ -231,7 +231,17 @@
 def attend_other_kernel(
     place_ref, q_ref, below_ref, above_ref, total_ref, top_ref, after_ref, *refs
 ):
-    out_refs, bufs = refs[:NX], refs[NX:]
+    out_refs, bufs, total_buf, sems = refs[:NX], refs[NX:-2], refs[-2], refs[-1]
+    copies = [
+        pltpu.make_async_copy(total_ref.at[c], total_buf.at[c], sems.at[c]) for c in range(NX)
+    ]
+    for copy in copies:
+        copy.start()
+
+    def begin(c):
+        copies[c].wait()
+        return total_buf[c], top_ref[c]
+
 
     def end(c, total, top):
         done = (total[:DH, :] / total[DH : DH + 1, :]).astype(BF16)
@@ -250,7 +260,7 @@
         lambda c, i: below_ref[i, c] if i < half else above_ref[i - half, c],
         1 - place_ref[0] % 2,
         *bufs,
-        lambda c: (total_ref[c], top_ref[c]),
+        begin,
         end,
     )
 
@@ -325,10 +335,14 @@
     attended = pl.pallas_call(
         attend_other_kernel,
         out_shape=[jax.ShapeDtypeStruct((GDH, T), BF16)] * NX,
-        in_specs=[SMEM_SPEC] + [VMEM_SPEC] * 5 + [ANY_SPEC],
+        in_specs=[SMEM_SPEC] + [VMEM_SPEC] * 3 + [HBM_SPEC, VMEM_SPEC, ANY_SPEC],
         out_specs=[VMEM_SPEC] * NX,
-        scratch_shapes=bufs,
-        compiler_params=pltpu.CompilerParams(vmem_limit_bytes=24 << 20),
+        scratch_shapes=bufs
+        + [
+            pltpu.VMEM((NX, DH + 16, QUERIES), F32),
+            pltpu.SemaphoreType.DMA((NX,)),
+        ],
+        compiler_params=pltpu.CompilerParams(vmem_limit_bytes=56 << 20),
     )(place_zx, packed, below, above, total, top, prefix)
     attended = [attended[0]] + [
         lax.ppermute(attended[s], "cx", [(k, (k + s) % NX) for k in range(NX)])

time: 113 us -> 114 us (level)
  Pallas kernels: 30 us -> 31.7 us
    pallas_call x1, Pallas kernels: 10.6 us -> 12.2 us  [per_device(): pl.pallas_call(attend_other_kernel, out_shape=[jax.ShapeDtypeStruct((GDH,...]
    unnamed x12 -> x22, local copies, waits for them, and re-layouts: 2.59 us -> 2.12 us
  transfers between devices with their start and end apart: 8 -> 8, of which waited for: 3 -> 3; matrix products, arithmetic and copies ran while one was open for 1% -> 1% of each run, Pallas kernels for 20% -> 21%
where the time goes in v12:
time: 114 us; the launch traced here: 113 us
  starting transfers between devices  36.3 us (32%)
  Pallas kernels  31.7 us (28%)
  blocking collectives  23.4 us (21%)
  waiting for transfers between devices  18.1 us (16%)
  local copies, waits for them, and re-layouts  3.04 us (3%)
    all_gather x1, blocking collectives, per_device(): same = lax.all_gather(packed[:, GDH:, :], 'zh')  23.4 us
    pallas_call x1, Pallas kernels, per_device(): pl.pallas_call(attend_other_kernel, out_shape=[jax.ShapeDtypeStruct((GDH,...  12.2 us
    ppermute x3, starting transfers between devices, per_device(): lax.ppermute(attended[s], 'cx', [(k, (k + s) % NX) for k in range(NX)])  11.7 us
    all_to_all x1, waiting for transfers between devices, per_device(): packed = lax.all_to_all(packed, 'cx', 0, 0)  11.5 us
    pallas_call x1, Pallas kernels, per_device(): pl.pallas_call(attend_same_kernel, out_shape=[jax.ShapeDtypeStruct((NX, D...  7.54 us
    all_to_all x1, starting transfers between devices, per_device(): entering = lax.all_to_all(prefix, ('cx', 'zh', 'zl'), 0, 0)  7.35 us
    all_to_all x1, starting transfers between devices, per_device(): update = lax.all_to_all(update, ('cx', 'zh', 'zl'), 0, 0)  5.95 us
    ppermute x1, waiting for transfers between devices, per_device(): lax.ppermute(same[:NH // 2], ('zh', 'zl'), [(k, (k + 1) % NZ) for k in ra...  5.24 us
  transfers between devices with their start and end apart: 8, of which 3 were waited for; matrix products, arithmetic and copies ran while one was open for 1% of the time, Pallas kernels for 21%

profile of v12, /device:TPU:56, one launch (start us, length us, event | category | flops | bytes accessed | tf_op | source)
XLA Modules:
  0.0 113.4 jit_solution(2697369414264353119)
XLA Ops:
  0.6 0.0 copy-start.1
  0.6 0.0 copy-start.4
  0.7 0.0 copy-start.6
  0.7 2.5 %shard_map.87 = bf16[4,816,128]{2,1,0:T(8,128)(2,1)} custom-call(bf16[128,2560]{1,0:T(8,128)(2,1)} %q_hbm.1, bf16[320,128]{1,0:T(8,128)(2,1)} %bitcast.15, bf16[320,128]{1,0:T(8,128)(2,1)} %bitcast.16, f32[40,128]{1,0:T(8,128)} %bitcast.12), custom_call_target="tpu_custom_call" | custom-call | tf_op jit(solution)/shard_map/pallas_call | solution.py:303
  3.1 4.3 %all-to-all-start = ((bf16[4,816,128]{2,1,0:T(8,128)(2,1)}), bf16[4,816,128]{2,1,0:T(8,128)(2,1)S(1)}, u32[]{:S(2)}, u32[]{:S(2)}) async-start(bf16[4,816,128]{2,1,0:T(8,128)(2,1)} %shard_map.87), calls=%async_computation | async-start | bytes 1671168 | tf_op jit(solution)/shard_map/all_to_all | solution.py:306
  7.5 0.0 copy-done.1
  7.5 0.0 copy-done.4
  7.5 0.0 copy-done.6
  7.5 1.3 %shard_map.86.in_ref = bf16[128,2560]{1,0:T(8,128)(2,1)S(1)} custom-call(bf16[128,2560]{1,0:T(8,128)(2,1)S(1)} %copy-done.1, bf16[128,128]{1,0:T(8,128)(2,1)S(1)} %copy-done.6, f32[40,128]{1,0:T(8,128)S(1)} %bitcast.13), custom_call_target="tpu_custom_call" | custom-call | tf_op jit(solution)/shard_map/pallas_call | solution.py:310
  8.8 11.5 %all-to-all-done.q_ref = bf16[4,816,128]{2,1,0:T(8,128)(2,1)S(1)} async-done(((bf16[4,816,128]{2,1,0:T(8,128)(2,1)}), bf16[4,816,128]{2,1,0:T(8,128)(2,1)S(1)}, u32[]{:S(2)}, u32[]{:S(2)}) %all-to-all-start) | async-done | bytes 835616 | tf_op jit(solution)/shard_map/all_to_all | solution.py:306
  20.3 0.0 copy-start
  20.3 23.4 %all-gather = bf16[16,176,128]{2,1,0:T(8,128)(2,1)S(1)} all-gather(bf16[4,176,128]{2,1,0:T(8,128)(2,1)S(1)} %slice.14), channel_id=2, replica_groups=mesh['dp'=16,'cx'=4,'zh'=4,'zl'=2] {'zh'}, dimensions={0}, use_global_device_ids=true | all-gather | bytes 901120 | tf_op jit(solution)/shard_map/all_gather | solution.py:307
  43.7 0.9 shard_map.88
  44.5 5.9 %all-to-all-start.1 = ((bf16[32,16,640]{2,1,0:T(8,128)(2,1)}), bf16[32,16,640]{2,1,0:T(8,128)(2,1)S(1)}, u32[]{:S(2)}, u32[]{:S(2)}) async-start(bf16[32,16,640]{2,1,0:T(8,128)(2,1)} %shard_map.88), calls=%async_computation.1 | async-start | bytes 1310720 | tf_op jit(solution)/shard_map/all_to_all | solution.py:314
  50.5 0.9 fusion
  51.4 3.7 %collective-permute-start = (bf16[2,4,176,128]{3,2,1,0:T(8,128)(2,1)}, bf16[2,4,176,128]{3,2,1,0:T(8,128)(2,1)S(1)}, u32[]{:S(2)}, u32[]{:S(2)}) collective-permute-start(bf16[2,4,176,128]{3,2,1,0:T(8,128)(2,1)} %bitcast.5), channel_id=1, source_target_pairs={{0,1},{1,2},{2,3},{3,4},{4,5},{5,6},{6,7},{7,0},{8,9},{9,10},{10,1... | collective-permute-start | bytes 1081352 | tf_op jit(solution)/shard_map/ppermute | solution.py:308
  55.1 3.4 %collective-permute-start.1 = (bf16[2,4,176,128]{3,2,1,0:T(8,128)(2,1)}, bf16[2,4,176,128]{3,2,1,0:T(8,128)(2,1)}, u32[]{:S(2)}, u32[]{:S(2)}) collective-permute-start(bf16[2,4,176,128]{3,2,1,0:T(8,128)(2,1)} %bitcast.6), channel_id=1, source_target_pairs={{0,7},{1,0},{2,1},{3,2},{4,3},{5,4},{6,5},{7,6},{8,15},{9,8},{10,9... | collective-permute-start | bytes 1081352 | tf_op jit(solution)/shard_map/ppermute | solution.py:309
  58.5 0.1 pad_add_fusion.place_ref
  58.6 0.0 copy-done
  58.6 0.0 copy-start.9
  58.6 7.5 %shard_map.89 = (f32[4,96,1024]{2,1,0:T(8,128)S(1)}, f32[4,1,1024]{2,1,0:T(1,128)S(1)}) custom-call(s32[2]{0:T(128)S(1)} %pad_add_fusion.place_ref, bf16[4,816,128]{2,1,0:T(8,128)(2,1)S(1)} %all-to-all-done.q_ref, bf16[4,4,176,128]{3,2,1,0:T(8,128)(2,1)S(1)} %bitcast.10), custom_call_target="tpu_custom_call" | custom-call | tf_op jit(solution)/shard_map/pallas_call | solution.py:320
  66.1 0.0 copy-start.2
  66.1 1.2 %copy-done.2 = f32[4,96,1024]{2,1,0:T(8,128)} copy-done((f32[4,96,1024]{2,1,0:T(8,128)}, f32[4,96,1024]{2,1,0:T(8,128)S(1)}, u32[]{:S(2)}) %copy-start.2) | copy-done | bytes 1572888
  67.3 0.0 copy-start.7
  67.3 5.2 %collective-permute-done.below_ref = bf16[2,4,176,128]{3,2,1,0:T(8,128)(2,1)S(1)} collective-permute-done((bf16[2,4,176,128]{3,2,1,0:T(8,128)(2,1)}, bf16[2,4,176,128]{3,2,1,0:T(8,128)(2,1)S(1)}, u32[]{:S(2)}, u32[]{:S(2)}) %collective-permute-start) | collective-permute-done | bytes 360480 | tf_op jit(solution)/shard_map/ppermute | solution.py:308
  72.5 0.0 copy-start.3
  72.5 0.0 collective-permute-done.1.above_ref
  72.5 0.0 all-to-all-done.1.in_ref
  72.5 3.0 %shard_map.90.after_ref = bf16[32,16,640]{2,1,0:T(8,128)(2,1)} custom-call(s32[1]{0:T(128)} %bitcast.1.place_ref, bf16[32,16,640]{2,1,0:T(8,128)(2,1)S(1)} %all-to-all-done.1.in_ref, bf16[4,4,176,128]{3,2,1,0:T(8,128)(2,1)S(1)} %bitcast.11, bf16[2,4,176,128]{3,2,1,0:T(8,128)(2,1)S(1)} %collective-permute-done.below_ref, ...), custom_call_target="tpu_custom_call" | custom-call | tf_op jit(solution)/shard_map/pallas_call | solution.py:331
  75.5 0.0 copy-done.9
  75.5 0.0 copy-done.7
  75.5 0.0 copy-done.3
  75.5 7.3 %all-to-all-start.2 = ((bf16[32,16,640]{2,1,0:T(8,128)(2,1)}), bf16[32,16,640]{2,1,0:T(8,128)(2,1)S(1)}, u32[]{:S(2)}, u32[]{:S(2)}) async-start(bf16[32,16,640]{2,1,0:T(8,128)(2,1)} %shard_map.90.after_ref), calls=%async_computation.2 | async-start | bytes 1310720 | tf_op jit(solution)/shard_map/all_to_all | solution.py:334
  82.8 0.0 copy-start.8
  82.9 0.0 copy-start.10
  82.9 12.2 %shard_map.92 = (bf16[640,128]{1,0:T(8,128)(2,1)}, bf16[640,128]{1,0:T(8,128)(2,1)}, bf16[640,128]{1,0:T(8,128)(2,1)}, bf16[640,128]{1,0:T(8,128)(2,1)}) custom-call(s32[2]{0:T(128)} %copy-done.9, bf16[4,816,128]{2,1,0:T(8,128)(2,1)} %copy-done, bf16[2,4,176,128]{3,2,1,0:T(8,128)(2,1)} %copy-done.3, ...), custom_call_target="tpu_custom_call" | custom-call | tf_op jit(solution)/shard_map/pallas_call | solution.py:335
  95.1 3.7 %collective-permute-start.2 = (bf16[640,128]{1,0:T(8,128)(2,1)}, bf16[640,128]{1,0:T(8,128)(2,1)S(1)}, u32[]{:S(2)}, u32[]{:S(2)}) collective-permute-start(bf16[640,128]{1,0:T(8,128)(2,1)} %get-tuple-element.14), channel_id=1, source_target_pairs={{0,8},{8,16},{16,24},{24,0},{1,9},{9,17},{17,25},{25,1},{2,10},{10... | collective-permute-start | bytes 491528 | tf_op jit(solution)/shard_map/ppermute | solution.py:348
  98.8 4.6 %collective-permute-start.3 = (bf16[640,128]{1,0:T(8,128)(2,1)}, bf16[640,128]{1,0:T(8,128)(2,1)S(1)}, u32[]{:S(2)}, u32[]{:S(2)}) collective-permute-start(bf16[640,128]{1,0:T(8,128)(2,1)} %get-tuple-element.15), channel_id=1, source_target_pairs={{0,16},{8,24},{16,0},{24,8},{1,17},{9,25},{17,1},{25,9},{2,18},{10... | collective-permute-start | bytes 491528 | tf_op jit(solution)/shard_map/ppermute | solution.py:348
  103.4 3.3 %collective-permute-start.4 = (bf16[640,128]{1,0:T(8,128)(2,1)}, bf16[640,128]{1,0:T(8,128)(2,1)S(1)}, u32[]{:S(2)}, u32[]{:S(2)}) collective-permute-start(bf16[640,128]{1,0:T(8,128)(2,1)} %get-tuple-element.16), channel_id=1, source_target_pairs={{0,24},{8,0},{16,8},{24,16},{1,25},{9,1},{17,9},{25,17},{2,26},{10... | collective-permute-start | bytes 491528 | tf_op jit(solution)/shard_map/ppermute | solution.py:348
  106.8 0.0 all-to-all-done.2.enter_ref
  106.8 0.0 copy-done.8
  106.8 2.7 %shard_map.91 = (bf16[128,2560]{1,0:T(8,128)(2,1)}, f32[8,128]{1,0:T(8,128)S(1)}) custom-call(bf16[128,2560]{1,0:T(8,128)(2,1)S(1)} %copy-done.1, bf16[128,128]{1,0:T(8,128)(2,1)S(1)} %copy-done.6, bf16[128,128]{1,0:T(8,128)(2,1)S(1)} %copy-done.8, f32[40,128]{1,0:T(8,128)S(1)} %bitcast.14, bf16[32,16,640]{2,1,0:T(8,128)(2,1)S(1)} %all-to-all-done.2.enter_ref), custom_call_target="tpu_custom_call" | custom-call | tf_op jit(solution)/shard_map/pallas_call | solution.py:351
  109.5 0.0 collective-permute-done.2.refs_1_
  109.5 0.0 collective-permute-done.3.refs_2_
  109.5 1.3 %collective-permute-done.4.refs_3_ = bf16[640,128]{1,0:T(8,128)(2,1)S(1)} collective-permute-done((bf16[640,128]{1,0:T(8,128)(2,1)}, bf16[640,128]{1,0:T(8,128)(2,1)S(1)}, u32[]{:S(2)}, u32[]{:S(2)}) %collective-permute-start.4) | collective-permute-done | bytes 163872 | tf_op jit(solution)/shard_map/ppermute | solution.py:348
  110.9 0.0 copy-done.10
  110.9 0.0 copy-start.5
  110.9 0.9 copy-done.5
  111.8 1.6 %shard_map.93 = bf16[128,2560]{1,0:T(8,128)(2,1)} custom-call(s32[2]{0:T(128)S(1)} %copy-done.10, bf16[640,128]{1,0:T(8,128)(2,1)S(1)} %copy-done.5, bf16[640,128]{1,0:T(8,128)(2,1)S(1)} %collective-permute-done.2.refs_1_, bf16[640,128]{1,0:T(8,128)(2,1)S(1)} %collective-permute-done.3.refs_2_, bf16[640,128]{1,0:T(8,128)(2,1)S(1)} %collective-permute-done.4.refs_3_, ...), custom_call_target="tpu_custom_call" | custom-call | tf_op jit(solution)/shard_map/pallas_call | solution.py:361
  (1 shorter events, 0.0 us)
Async XLA Ops:
  0.6 6.8 %copy-start.1 = (bf16[128,2560]{1,0:T(8,128)(2,1)S(1)}, bf16[128,2560]{1,0:T(8,128)(2,1)}, u32[]{:S(2)}) copy-start(bf16[128,2560]{1,0:T(8,128)(2,1)} %x_ref.3) | copy-start | bytes 1966084
  0.6 6.8 %copy-start.4 = (f32[128,40]{0,1:T(8,128)S(1)}, f32[128,40]{0,1:T(8,128)}, u32[]{:S(2)}) copy-start(f32[128,40]{0,1:T(8,128)} %param.10) | copy-start | bytes 61444
  0.7 6.8 %copy-start.6 = (bf16[128,128]{1,0:T(8,128)(2,1)S(1)}, bf16[128,128]{1,0:T(8,128)(2,1)}, u32[]{:S(2)}) copy-start(bf16[128,128]{1,0:T(8,128)(2,1)} %in_ref.3) | copy-start | bytes 98308
  3.1 17.1 %all-to-all-start = ((bf16[4,816,128]{2,1,0:T(8,128)(2,1)}), bf16[4,816,128]{2,1,0:T(8,128)(2,1)S(1)}, u32[]{:S(2)}, u32[]{:S(2)}) async-start(bf16[4,816,128]{2,1,0:T(8,128)(2,1)} %shard_map.87), calls=%async_computation | async-start | bytes 1671168 | tf_op jit(solution)/shard_map/all_to_all | solution.py:306
  20.3 38.3 %copy-start = (bf16[4,816,128]{2,1,0:T(8,128)(2,1)}, bf16[4,816,128]{2,1,0:T(8,128)(2,1)S(1)}, u32[]{:S(2)}) copy-start(bf16[4,816,128]{2,1,0:T(8,128)(2,1)S(1)} %all-to-all-done.q_ref) | copy-start | bytes 2506756
  44.5 28.0 %all-to-all-start.1 = ((bf16[32,16,640]{2,1,0:T(8,128)(2,1)}), bf16[32,16,640]{2,1,0:T(8,128)(2,1)S(1)}, u32[]{:S(2)}, u32[]{:S(2)}) async-start(bf16[32,16,640]{2,1,0:T(8,128)(2,1)} %shard_map.88), calls=%async_computation.1 | async-start | bytes 1310720 | tf_op jit(solution)/shard_map/all_to_all | solution.py:314
  51.4 21.1 %collective-permute-start = (bf16[2,4,176,128]{3,2,1,0:T(8,128)(2,1)}, bf16[2,4,176,128]{3,2,1,0:T(8,128)(2,1)S(1)}, u32[]{:S(2)}, u32[]{:S(2)}) collective-permute-start(bf16[2,4,176,128]{3,2,1,0:T(8,128)(2,1)} %bitcast.5), channel_id=1, source_target_pairs={{0,1},{1,2},{2,3},{3,4},{4,5},{5,6},{6,7},{7,0},{8,9},{9,10},{10,1... | collective-permute-start | bytes 1081352 | tf_op jit(solution)/shard_map/ppermute | solution.py:308
  55.1 17.4 %collective-permute-start.1 = (bf16[2,4,176,128]{3,2,1,0:T(8,128)(2,1)}, bf16[2,4,176,128]{3,2,1,0:T(8,128)(2,1)}, u32[]{:S(2)}, u32[]{:S(2)}) collective-permute-start(bf16[2,4,176,128]{3,2,1,0:T(8,128)(2,1)} %bitcast.6), channel_id=1, source_target_pairs={{0,7},{1,0},{2,1},{3,2},{4,3},{5,4},{6,5},{7,6},{8,15},{9,8},{10,9... | collective-permute-start | bytes 1081352 | tf_op jit(solution)/shard_map/ppermute | solution.py:309
  58.6 16.9 %copy-start.9 = (s32[2]{0:T(128)}, s32[2]{0:T(128)S(1)}, u32[]{:S(2)}) copy-start(s32[2]{0:T(128)S(1)} %pad_add_fusion.place_ref) | copy-start | bytes 28
  66.1 1.2 %copy-start.2 = (f32[4,96,1024]{2,1,0:T(8,128)}, f32[4,96,1024]{2,1,0:T(8,128)S(1)}, u32[]{:S(2)}) copy-start(f32[4,96,1024]{2,1,0:T(8,128)S(1)} %get-tuple-element.12.total_ref) | copy-start | bytes 4718596
  67.3 8.2 %copy-start.7 = (f32[4,1,1024]{2,1,0:T(1,128)}, f32[4,1,1024]{2,1,0:T(1,128)S(1)}, u32[]{:S(2)}) copy-start(f32[4,1,1024]{2,1,0:T(1,128)S(1)} %get-tuple-element.10.after_ref.top_ref) | copy-start | bytes 49156
  72.5 3.0 %copy-start.3 = (bf16[2,4,176,128]{3,2,1,0:T(8,128)(2,1)}, bf16[2,4,176,128]{3,2,1,0:T(8,128)(2,1)S(1)}, u32[]{:S(2)}) copy-start(bf16[2,4,176,128]{3,2,1,0:T(8,128)(2,1)S(1)} %collective-permute-done.below_ref) | copy-start | bytes 1081348
  75.5 31.3 %all-to-all-start.2 = ((bf16[32,16,640]{2,1,0:T(8,128)(2,1)}), bf16[32,16,640]{2,1,0:T(8,128)(2,1)S(1)}, u32[]{:S(2)}, u32[]{:S(2)}) async-start(bf16[32,16,640]{2,1,0:T(8,128)(2,1)} %shard_map.90.after_ref), calls=%async_computation.2 | async-start | bytes 1310720 | tf_op jit(solution)/shard_map/all_to_all | solution.py:334
  82.8 24.0 %copy-start.8 = (bf16[128,128]{1,0:T(8,128)(2,1)S(1)}, bf16[128,128]{1,0:T(8,128)(2,1)}, u32[]{:S(2)}) copy-start(bf16[128,128]{1,0:T(8,128)(2,1)} %map_ref.1) | copy-start | bytes 98308
  82.9 28.0 %copy-start.10 = (s32[2]{0:T(128)S(1)}, s32[2]{0:T(128)}, u32[]{:S(2)}) copy-start(s32[2]{0:T(128)} %copy-done.9) | copy-start | bytes 28
  95.1 14.4 %collective-permute-start.2 = (bf16[640,128]{1,0:T(8,128)(2,1)}, bf16[640,128]{1,0:T(8,128)(2,1)S(1)}, u32[]{:S(2)}, u32[]{:S(2)}) collective-permute-start(bf16[640,128]{1,0:T(8,128)(2,1)} %get-tuple-element.14), channel_id=1, source_target_pairs={{0,8},{8,16},{16,24},{24,0},{1,9},{9,17},{17,25},{25,1},{2,10},{10... | collective-permute-start | bytes 491528 | tf_op jit(solution)/shard_map/ppermute | solution.py:348
  98.8 10.7 %collective-permute-start.3 = (bf16[640,128]{1,0:T(8,128)(2,1)}, bf16[640,128]{1,0:T(8,128)(2,1)S(1)}, u32[]{:S(2)}, u32[]{:S(2)}) collective-permute-start(bf16[640,128]{1,0:T(8,128)(2,1)} %get-tuple-element.15), channel_id=1, source_target_pairs={{0,16},{8,24},{16,0},{24,8},{1,17},{9,25},{17,1},{25,9},{2,18},{10... | collective-permute-start | bytes 491528 | tf_op jit(solution)/shard_map/ppermute | solution.py:348
  103.4 7.4 %collective-permute-start.4 = (bf16[640,128]{1,0:T(8,128)(2,1)}, bf16[640,128]{1,0:T(8,128)(2,1)S(1)}, u32[]{:S(2)}, u32[]{:S(2)}) collective-permute-start(bf16[640,128]{1,0:T(8,128)(2,1)} %get-tuple-element.16), channel_id=1, source_target_pairs={{0,24},{8,0},{16,8},{24,16},{1,25},{9,1},{17,9},{25,17},{2,26},{10... | collective-permute-start | bytes 491528 | tf_op jit(solution)/shard_map/ppermute | solution.py:348
  110.9 0.9 copy-start.5
